TPU v7x, 32 devices: a whole 2x2x4 slice. The times are simulated.
32 devices in a mesh: bx: 4 (over x, core), by: 8 (over z, y).
Axes of the slice: x: 2, y: 2, z: 4, core: 2. Of those that a mesh axis runs over, the one named last changes fastest.
Arguments:
- atom_pos: float32 [3, 16, 64, 128], P(None, 'bx', 'by'), may hold values from 0 to 1
- b_factor: float32 [16, 64, 128], P('bx', 'by'), may hold values from 100 to 400
- amplitude: float32 [16, 64, 128], P('bx', 'by'), may hold values from 0.5 to 2
- counts: int32 [16, 64], P('bx', 'by'), may hold values from 1 to 128, as said below
- density_map: bfloat16 [256, 1024, 128], P('bx', 'by'), may hold values from -1 to 1
Outputs:
- residual_map: bfloat16 [256, 1024, 128], P('bx', 'by')
- atom_gradient: float32 [4, 16, 64, 128], P(None, 'bx', 'by')
Inputs may be any that keep to these rules, and one draw needn't show every extreme that they name: Slots below counts[a, b] of subbrick (a, b) hold its atoms, the others are padding; in every draw some subbrick is full.
All inputs are finite; a program needn't handle non-finite values.
Results may differ from a plain program's by a relative error of at most 0.001.
Values sent between devices are 32-bit elements; how exact they have to be, the bound alone decides.
No kernel may reach another device: no remote copies, remote signals or barrier semaphores. Data moves between devices by JAX's collectives and lax.ppermute only.
A program may use at most 128 MiB of HBM per device.

v0:
```python
import math

import jax
import jax.numpy as jnp
from jax import lax
from jax.sharding import PartitionSpec as P

SUB = 16
RAD = 4
TILE = 24
DEPTH = 128


EIGHT_PI_SQ = 8.0 * math.pi**2
BLUR_VAR = 0.5


def from_behind(block, axis, distance):
    devices = range(lax.axis_size(axis))
    route = [(i - distance, i) for i in devices if i - distance in devices]
    return lax.ppermute(block, axis, route)


def with_halo(array, sides, width):
    for axis, dim in sides:
        peers, length = (lax.axis_size(axis), array.shape[dim])
        up = [(i, (i + 1) % peers) for i in range(peers - 1)]
        down = [(j, i) for i, j in up]
        last = lax.slice_in_dim(array, length - width, length, axis=dim)
        initial = lax.slice_in_dim(array, 0, width, axis=dim)
        before = lax.ppermute(last, axis, up)
        after = lax.ppermute(initial, axis, down)
        array = jnp.concatenate([before, array, after], axis=dim)
    return array


def profiles(coordinate, sharpness, span_len, offset):
    grid_pos = (jnp.arange(span_len) + offset).astype(jnp.float32)
    distance = grid_pos - coordinate[..., None]
    square = distance * distance
    reach_sq = float(RAD * RAD)
    falloff = jnp.where(square < reach_sq, 1.0 - square / reach_sq, 0.0)
    exponent = jnp.exp(-sharpness[..., None] * square)
    profile = exponent * falloff * falloff
    slope_d = (
        2.0 * distance * exponent * falloff * (sharpness[..., None] * falloff + 2.0 / reach_sq)
    )
    width_d = -square * profile
    return (profile, slope_d, width_d)


def all_profiles(coords, sharpness):
    along_x = profiles(coords[0], sharpness, TILE, -RAD)
    along_y = profiles(coords[1], sharpness, TILE, -RAD)
    along_z = profiles(coords[2], sharpness, DEPTH, 0)
    return (along_x, along_y, along_z)


def atom_terms(atom_pos, b_factor, amplitude, counts):
    live_slot = jnp.arange(amplitude.shape[-1])[None, None, :] < counts[..., None]
    weight = jnp.where(live_slot, amplitude, 0.0)
    sharpness = 0.5 / (b_factor / EIGHT_PI_SQ + BLUR_VAR)
    coords = jnp.stack([SUB * atom_pos[0], SUB * atom_pos[1], DEPTH * atom_pos[2]])
    return (weight, sharpness, coords)


def render(value_x, value_y, value_z, weight):
    plane_xy = value_x[..., :, None] * value_y[..., None, :]
    plane_xy = plane_xy.reshape(plane_xy.shape[:-2] + (TILE * TILE,))
    return jnp.einsum(
        "...cm,...ck->...mk", plane_xy, value_z * weight[..., None], precision=lax.Precision.HIGHEST
    )


def spread(tile_set, axis_dim):
    tile_count = tile_set.shape[axis_dim]
    head_part = lax.slice_in_dim(tile_set, 0, SUB, axis=axis_dim + 1)
    tail_part = lax.slice_in_dim(tile_set, SUB, TILE, axis=axis_dim + 1)
    tail_pad = [(0, 0)] * tile_set.ndim
    tail_pad[axis_dim + 1] = (0, SUB - 2 * RAD)
    tail_part = jnp.pad(tail_part, tail_pad)
    new_shape = tile_set.shape[:axis_dim] + (tile_count * SUB,) + tile_set.shape[axis_dim + 2 :]
    head_part = head_part.reshape(new_shape)
    tail_part = tail_part.reshape(new_shape)
    pad_after = [(0, 0)] * len(new_shape)
    pad_after[axis_dim] = (0, 2 * RAD)
    pad_before = [(0, 0)] * len(new_shape)
    pad_before[axis_dim] = (SUB, 0)
    shifted = lax.slice_in_dim(
        jnp.pad(tail_part, pad_before), 0, tile_count * SUB + 2 * RAD, axis=axis_dim
    )
    return jnp.pad(head_part, pad_after) + shifted


def collect(grid_field, axis_dim, tile_count):
    new_shape = grid_field.shape[:axis_dim] + (tile_count, SUB) + grid_field.shape[axis_dim + 1 :]
    head_part = lax.slice_in_dim(grid_field, 0, tile_count * SUB, axis=axis_dim).reshape(new_shape)
    pad_after = [(0, 0)] * grid_field.ndim
    pad_after[axis_dim] = (0, SUB - 2 * RAD)
    tail_part = lax.slice_in_dim(
        jnp.pad(grid_field, pad_after), SUB, tile_count * SUB + SUB, axis=axis_dim
    ).reshape(new_shape)
    tail_part = lax.slice_in_dim(tail_part, 0, 2 * RAD, axis=axis_dim + 1)
    return jnp.concatenate([head_part, tail_part], axis=axis_dim + 1)


def place_tiles(rendered):
    rows_n, cols_n = (rendered.shape[0], rendered.shape[1])
    tile_set = rendered.reshape(rows_n, cols_n, TILE, TILE, rendered.shape[-1])
    tile_set = jnp.transpose(tile_set, (0, 2, 1, 3, 4))
    return spread(spread(tile_set, 2), 0)


def tile_view(ext_field, rows_n, cols_n):
    part_x = collect(ext_field, 0, rows_n)
    part_xy = collect(part_x, 2, cols_n)
    part_xy = jnp.transpose(part_xy, (0, 2, 1, 3, 4))
    return part_xy.reshape(rows_n, cols_n, TILE * TILE, part_xy.shape[-1])


def over_y(block_pqc, profile_q):
    return jnp.sum(block_pqc * profile_q[..., None, :, :], axis=-2)


def over_x(row_pc, profile_p):
    return jnp.sum(row_pc * profile_p, axis=-2)


def gradients(tile_resid, weight, sharpness, along_x, along_y, along_z):
    stacked = jnp.stack(along_z, axis=-3)
    project = jnp.einsum(
        "...mk,...jck->...jmc", tile_resid, stacked, precision=lax.Precision.HIGHEST
    )
    project = project.reshape(project.shape[:-2] + (TILE, TILE, project.shape[-1]))
    value_x, slope_x, width_x = [jnp.swapaxes(profile, -1, -2) for profile in along_x]
    value_y, slope_y, width_y = [jnp.swapaxes(profile, -1, -2) for profile in along_y]
    base_proj = project[..., 0, :, :, :]
    lift_proj = project[..., 1, :, :, :]
    width_proj = project[..., 2, :, :, :]
    base_value = over_y(base_proj, value_y)
    base_slope = over_y(base_proj, slope_y)
    base_width = over_y(base_proj, width_y)
    lift_value = over_y(lift_proj, value_y)
    width_value = over_y(width_proj, value_y)
    grad_x = weight * over_x(base_value, slope_x)
    grad_y = weight * over_x(base_slope, value_x)
    grad_z = weight * over_x(lift_value, value_x)
    grad_sharp = weight * (
        over_x(base_value, width_x) + over_x(base_width, value_x) + over_x(width_value, value_x)
    )
    grad_b = grad_sharp * (-2.0 * sharpness * sharpness / EIGHT_PI_SQ)
    return jnp.stack([grad_x, grad_y, grad_z, grad_b], axis=0)


def fold_x(ext_field):
    from_above = from_behind(ext_field[:RAD], "bx", -1)
    from_below = from_behind(ext_field[-RAD:], "bx", 1)
    return jnp.concatenate(
        [
            ext_field[RAD : 2 * RAD] + from_below,
            ext_field[2 * RAD : -2 * RAD],
            ext_field[-2 * RAD : -RAD] + from_above,
        ],
        axis=0,
    )


def fold_y(ext_field):
    from_above = from_behind(ext_field[:, :RAD], "by", -1)
    from_below = from_behind(ext_field[:, -RAD:], "by", 1)
    return jnp.concatenate(
        [
            ext_field[:, RAD : 2 * RAD] + from_below,
            ext_field[:, 2 * RAD : -2 * RAD],
            ext_field[:, -2 * RAD : -RAD] + from_above,
        ],
        axis=1,
    )


def local(atom_pos, b_factor, amplitude, counts, density_map):
    weight, sharpness, coords = atom_terms(atom_pos, b_factor, amplitude, counts)
    rows_n, cols_n = counts.shape
    along_x, along_y, along_z = all_profiles(coords, sharpness)
    own_tiles = render(along_x[0], along_y[0], along_z[0], weight)
    ext_field = place_tiles(own_tiles)
    density = fold_y(fold_x(ext_field))
    residual = density - density_map.astype(jnp.float32)
    rimmed = with_halo(residual, (("bx", 0), ("by", 1)), RAD)
    tile_resid = tile_view(rimmed, rows_n, cols_n)
    atom_gradient = gradients(tile_resid, weight, sharpness, along_x, along_y, along_z)
    return (residual.astype(jnp.bfloat16), atom_gradient)


def solution(mesh):
    return jax.shard_map(
        local,
        mesh=mesh,
        in_specs=(
            P(None, "bx", "by", None),
            P("bx", "by", None),
            P("bx", "by", None),
            P("bx", "by"),
            P("bx", "by", None),
        ),
        out_specs=(P("bx", "by", None), P(None, "bx", "by", None)),
        check_vma=False,
    )
```

profile of v0, /device:TPU:0, one launch (start us, length us, event | category | flops | bytes accessed | tf_op | source)
XLA Modules:
  0.0 134.9 jit_solution(14153019637456852604)
XLA Ops:
  0.7 0.8 multiply_bitcast_fusion.3
  1.4 0.8 add_divide_fusion
  2.2 0.4 multiply_multiply_fusion.5
  2.6 1.2 broadcast_multiply_fusion
  3.8 10.4 %fusion.27 = f32[4,8,576,128]{3,2,1,0:T(8,128)S(1)} fusion(f32[4,8,128,576]{2,3,1,0:T(8,128)S(1)} %bitcast.66, f32[4,8,128]{2,1,0:T(8,128)S(1)} %get-tuple-element.45, f32[4,8,128]{2,1,0:T(8,128)S(1)} %get-tuple-element.28, f32[128]{0:T(128)S(1)} %iota_convert_fusion, f32[4,8,128]{2,1,0:T(8,128)S(1)} %get-tuple-element.44), kind=kOutput, calls=%fused_computation.50 | convolution fusion | flops 3629121536 | bytes 18924032 | tf_op jit(solution)/shard_map/...cm,...ck->...mk/dot_general | solution.py:70
  14.2 1.3 copy.17
  15.5 0.3 slice.129
  15.8 0.6 slice.128
  16.4 3.6 %pad.33 = f32[4,24,8,16,128]{4,3,2,1,0:T(8,128)} pad(f32[4,24,8,8,128]{4,3,2,1,0:T(8,128)S(1)} %slice.129, f32[]{:T(128)} %constant.7.clone.1), padding=0_0x0_0x0_0x0_8x0_0 | pad | bytes 9437188 | tf_op jit(solution)/shard_map/jit(_pad)/pad | solution.py:81
  20.0 3.7 %fusion.4 = f32[4,24,136,128]{3,2,1,0:T(8,128)S(1)} fusion(f32[4,24,128,128]{3,2,1,0:T(8,128)} %bitcast.73, f32[4,24,128,128]{3,2,1,0:T(8,128)S(1)} %bitcast.72), kind=kLoop, calls=%fused_computation.17 | loop fusion | flops 1671168 | bytes 19267584 | tf_op jit(solution)/shard_map/add | solution.py:92
  23.7 0.1 slice.131
  23.8 0.3 slice.130
  24.1 0.3 pad.36
  24.4 0.4 fusion.12
  24.9 2.4 %collective-permute-start = (f32[4,136,128]{2,1,0:T(8,128)S(1)}, f32[4,136,128]{2,1,0:T(8,128)S(1)}, u32[]{:S(2)}, u32[]{:S(2)}) collective-permute-start(f32[4,136,128]{2,1,0:T(8,128)S(1)} %slice.133), channel_id=1, source_target_pairs={{0,8},{8,16},{16,24},{1,9},{9,17},{17,25},{2,10},{10,18},{18,26},{... | collective-permute-start | bytes 835592 | tf_op jit(solution)/shard_map/ppermute | solution.py:21
  27.3 1.2 collective-permute-done
  28.5 1.3 collective-permute-start.1
  29.8 0.3 slice.134
  30.0 6.3 %collective-permute-done.1 = f32[4,136,128]{2,1,0:T(8,128)S(1)} collective-permute-done((f32[4,136,128]{2,1,0:T(8,128)S(1)}, f32[4,136,128]{2,1,0:T(8,128)S(1)}, u32[]{:S(2)}, u32[]{:S(2)}) %collective-permute-start.1) | collective-permute-done | bytes 278560 | tf_op jit(solution)/shard_map/ppermute | solution.py:21
  36.4 3.4 %collective-permute-start.2 = (f32[64,4,128]{2,1,0:T(4,128)S(1)}, f32[64,4,128]{2,1,0:T(4,128)S(1)}, u32[]{:S(2)}, u32[]{:S(2)}) collective-permute-start(f32[64,4,128]{2,1,0:T(4,128)S(1)} %pad_maximum_fusion.7), channel_id=1, source_target_pairs={{0,1},{1,2},{2,3},{3,4},{4,5},{5,6},{6,7},{8,9},{9,10},{10,11},{11... | collective-permute-start | bytes 393224 | tf_op jit(solution)/shard_map/ppermute | solution.py:21
  39.8 2.5 %collective-permute-done.2 = f32[64,4,128]{2,1,0:T(4,128)S(1)} collective-permute-done((f32[64,4,128]{2,1,0:T(4,128)S(1)}, f32[64,4,128]{2,1,0:T(4,128)S(1)}, u32[]{:S(2)}, u32[]{:S(2)}) %collective-permute-start.2) | collective-permute-done | bytes 131104 | tf_op jit(solution)/shard_map/ppermute | solution.py:21
  42.3 0.1 maximum_add_fusion.1
  42.4 1.3 collective-permute-start.3
  43.7 0.3 pad_maximum_fusion.2
  44.0 0.0 copy-start
  44.0 0.3 slice.137
  44.3 5.4 %collective-permute-done.3 = f32[64,4,128]{2,1,0:T(4,128)S(1)} collective-permute-done((f32[64,4,128]{2,1,0:T(4,128)S(1)}, f32[64,4,128]{2,1,0:T(4,128)S(1)}, u32[]{:S(2)}, u32[]{:S(2)}) %collective-permute-start.3) | collective-permute-done | bytes 131104 | tf_op jit(solution)/shard_map/ppermute | solution.py:21
  49.7 0.0 copy-done
  49.7 2.2 %fusion.86 = (bf16[64,128,128]{2,1,0:T(8,128)(2,1)}, f32[64,128,128]{2,1,0:T(8,128)S(1)}) fusion(bf16[64,128,128]{2,1,0:T(8,128)(2,1)S(1)} %copy-done, f32[64,4,128]{2,1,0:T(4,128)S(1)} %maximum_add_fusion, f32[64,120,128]{2,1,0:T(8,128)S(1)} %slice.137, f32[64,4,128]{2,1,0:T(4,128)S(1)} %get-tuple-element.24), kind=kLoop, calls=%fused_computation.143 | loop fusion | flops 5242880 | bytes 12582912 | tf_op jit(solution)/shard_map/convert_element_type | solution.py:192
  52.0 1.3 collective-permute-start.5
  53.3 6.5 %collective-permute-start.4 = (f32[4,128,128]{2,1,0:T(8,128)S(1)}, f32[4,128,128]{2,1,0:T(8,128)S(1)}, u32[]{:S(2)}, u32[]{:S(2)}) collective-permute-start(f32[4,128,128]{2,1,0:T(8,128)S(1)} %get-tuple-element.26), channel_id=1, source_target_pairs={{0,8},{8,16},{16,24},{1,9},{9,17},{17,25},{2,10},{10,18},{18,26},{... | collective-permute-start | bytes 786440 | tf_op jit(solution)/shard_map/ppermute | solution.py:31
  59.8 3.8 %multiply_multiply_fusion = (f32[4,8,1,128,128]{4,3,2,1,0:T(8,128)}, f32[4,8,1,128,128]{4,3,2,1,0:T(8,128)}, f32[4,8,1,128,128]{4,3,2,1,0:T(8,128)}) fusion(f32[4,8,128]{2,1,0:T(8,128)S(1)} %get-tuple-element.28, f32[128]{0:T(128)S(1)} %iota_convert_fusion, f32[4,8,128]{2,1,0:T(8,128)S(1)} %get-tuple-element.44, f32[4,8,128]{2,1,0:T(8,128)S(1)} %get-tuple-element.43), kind=kLoop, calls=%fused_computation.32 | loop fusion | flops 8912896 | bytes 6341120 | tf_op jit(solution)/shard_map/mul | solution.py:44
  63.6 0.0 collective-permute-done.5
  63.6 0.0 collective-permute-done.4
  63.6 0.1 pad_maximum_fusion.5
  63.7 1.3 collective-permute-start.7
  65.0 5.2 %collective-permute-start.6 = (f32[72,4,128]{2,1,0:T(4,128)S(1)}, f32[72,4,128]{2,1,0:T(4,128)S(1)}, u32[]{:S(2)}, u32[]{:S(2)}) collective-permute-start(f32[72,4,128]{2,1,0:T(4,128)S(1)} %get-tuple-element.22), channel_id=1, source_target_pairs={{0,1},{1,2},{2,3},{3,4},{4,5},{5,6},{6,7},{8,9},{9,10},{10,11},{11... | collective-permute-start | bytes 442376 | tf_op jit(solution)/shard_map/ppermute | solution.py:31
  70.2 1.4 %multiply_multiply_fusion.3 = (f32[4,8,24,128]{3,2,1,0:T(8,128)}, f32[4,8,24,128]{3,2,1,0:T(8,128)}, f32[4,8,24,128]{3,2,1,0:T(8,128)}) fusion(f32[4,8,128]{2,1,0:T(8,128)S(1)} %get-tuple-element.30, f32[24]{0:T(128)S(1)} %add_convert_fusion, f32[4,8,128]{2,1,0:T(8,128)S(1)} %get-tuple-element.44, f32[4,8,128]{2,1,0:T(8,128)S(1)} %get-tuple-element.43), kind=kLoop, calls=%fused_computation.67 | loop fusion | flops 1671168 | bytes 1228896 | tf_op jit(solution)/shard_map/mul | solution.py:44
  71.5 0.2 collective-permute-done.7
  71.8 4.7 %collective-permute-done.6 = f32[72,4,128]{2,1,0:T(4,128)S(1)} collective-permute-done((f32[72,4,128]{2,1,0:T(4,128)S(1)}, f32[72,4,128]{2,1,0:T(4,128)S(1)}, u32[]{:S(2)}, u32[]{:S(2)}) %collective-permute-start.6) | collective-permute-done | bytes 147488 | tf_op jit(solution)/shard_map/ppermute | solution.py:31
  76.4 2.3 %pad_maximum_fusion.1 = f32[72,136,128]{2,1,0:T(8,128)S(1)} fusion(f32[72,4,128]{2,1,0:T(4,128)S(1)} %collective-permute-done.7, f32[4,128,128]{2,1,0:T(8,128)S(1)} %collective-permute-done.5, f32[64,128,128]{2,1,0:T(8,128)S(1)} %get-tuple-element.17, f32[4,128,128]{2,1,0:T(8,128)S(1)} %collective-permute-done.4, f32[72,4,128]{2,1,0:T(4,128)S(1)} %collective-permute-done.6), kind=kLoop, calls=%fused_computation.28 | loop fusion | flops 5013504 | bytes 10027008 | tf_op jit(solution)/shard_map/concatenate | solution.py:33
  78.7 0.6 fusion.87
  79.3 0.1 slice.141
  79.5 0.5 pad_maximum_fusion
  79.9 0.8 fusion.5
  80.8 0.9 pad_slice_fusion.2
  81.7 0.3 slice.144
  82.0 1.0 maximum_bitcast_fusion
  83.0 1.2 copy.10
  84.2 0.0 copy-start.1
  84.2 0.0 copy-start.2
  84.2 0.0 copy-start.3
  84.2 27.7 %fusion.6 = f32[4,8,3,128,576]{3,4,2,1,0:T(8,128)} fusion(f32[4,8,576,128,1]{3,2,4,1,0:T(8,128)S(1)} %bitcast.70, f32[4,8,1,128,128]{4,3,2,1,0:T(8,128)} %get-tuple-element.36, f32[4,8,1,128,128]{4,3,2,1,0:T(8,128)} %get-tuple-element.35, f32[4,8,1,128,128]{4,3,2,1,0:T(8,128)} %get-tuple-element.34), kind=kOutput, calls=%fused_computation.19 | convolution fusion | flops 10874781696 | bytes 44040192 | tf_op jit(solution)/shard_map/...mk,...jck->...jmc/dot_general | solution.py:131
  111.9 0.0 copy-done.1
  111.9 0.0 copy-done.2
  111.9 0.0 copy-done.3
  111.9 0.0 copy-start.4
  112.0 21.6 %multiply_reduce_fusion.1 = (f32[4,8,24,128]{3,2,1,0:T(8,128)S(1)}, f32[4,8,24,128]{3,2,1,0:T(8,128)S(1)}, f32[4,8,24,128]{3,2,1,0:T(8,128)S(1)}, f32[4,8,24,128]{3,2,1,0:T(8,128)S(1)}, f32[4,8,24,128]{3,2,1,0:T(8,128)S(1)}) fusion(f32[4,8,3,24,24,128]{5,4,3,2,1,0:T(8,128)} %bitcast.63, f32[4,8,24,128]{3,2,1,0:T(8,128)S(1)} %copy-done.2, ...), kind=kLoop, calls=%fused_computation.10 | loop fusion | flops 23101440 | bytes 31457280 | tf_op jit(solution)/shard_map/reduce_sum | solution.py:122
  133.5 0.7 fusion.66
  134.3 0.0 copy-done.4
  134.3 0.6 pad_maximum_fusion.8
  (9 shorter events, 0.2 us)
Async XLA Ops:
  24.9 3.5 %collective-permute-start = (f32[4,136,128]{2,1,0:T(8,128)S(1)}, f32[4,136,128]{2,1,0:T(8,128)S(1)}, u32[]{:S(2)}, u32[]{:S(2)}) collective-permute-start(f32[4,136,128]{2,1,0:T(8,128)S(1)} %slice.133), channel_id=1, source_target_pairs={{0,8},{8,16},{16,24},{1,9},{9,17},{17,25},{2,10},{10,18},{18,26},{... | collective-permute-start | bytes 835592 | tf_op jit(solution)/shard_map/ppermute | solution.py:21
  28.5 7.9 %collective-permute-start.1 = (f32[4,136,128]{2,1,0:T(8,128)S(1)}, f32[4,136,128]{2,1,0:T(8,128)S(1)}, u32[]{:S(2)}, u32[]{:S(2)}) collective-permute-start(f32[4,136,128]{2,1,0:T(8,128)S(1)} %get-tuple-element.21), channel_id=1, source_target_pairs={{8,0},{16,8},{24,16},{9,1},{17,9},{25,17},{10,2},{18,10},{26,18},{... | collective-permute-start | bytes 835592 | tf_op jit(solution)/shard_map/ppermute | solution.py:21
  36.4 5.9 %collective-permute-start.2 = (f32[64,4,128]{2,1,0:T(4,128)S(1)}, f32[64,4,128]{2,1,0:T(4,128)S(1)}, u32[]{:S(2)}, u32[]{:S(2)}) collective-permute-start(f32[64,4,128]{2,1,0:T(4,128)S(1)} %pad_maximum_fusion.7), channel_id=1, source_target_pairs={{0,1},{1,2},{2,3},{3,4},{4,5},{5,6},{6,7},{8,9},{9,10},{10,11},{11... | collective-permute-start | bytes 393224 | tf_op jit(solution)/shard_map/ppermute | solution.py:21
  42.4 7.3 %collective-permute-start.3 = (f32[64,4,128]{2,1,0:T(4,128)S(1)}, f32[64,4,128]{2,1,0:T(4,128)S(1)}, u32[]{:S(2)}, u32[]{:S(2)}) collective-permute-start(f32[64,4,128]{2,1,0:T(4,128)S(1)} %get-tuple-element.25), channel_id=1, source_target_pairs={{1,0},{2,1},{3,2},{4,3},{5,4},{6,5},{7,6},{9,8},{10,9},{11,10},{12... | collective-permute-start | bytes 393224 | tf_op jit(solution)/shard_map/ppermute | solution.py:21
  44.0 5.7 %copy-start = (bf16[64,128,128]{2,1,0:T(8,128)(2,1)S(1)}, bf16[64,128,128]{2,1,0:T(8,128)(2,1)}, u32[]{:S(2)}) copy-start(bf16[64,128,128]{2,1,0:T(8,128)(2,1)} %param.9) | copy-start | bytes 6291460
  52.0 11.6 %collective-permute-start.5 = (f32[4,128,128]{2,1,0:T(8,128)S(1)}, f32[4,128,128]{2,1,0:T(8,128)S(1)}, u32[]{:S(2)}, u32[]{:S(2)}) collective-permute-start(f32[4,128,128]{2,1,0:T(8,128)S(1)} %get-tuple-element.27), channel_id=1, source_target_pairs={{8,0},{16,8},{24,16},{9,1},{17,9},{25,17},{10,2},{18,10},{26,18},{... | collective-permute-start | bytes 786440 | tf_op jit(solution)/shard_map/ppermute | solution.py:32
  53.3 10.3 %collective-permute-start.4 = (f32[4,128,128]{2,1,0:T(8,128)S(1)}, f32[4,128,128]{2,1,0:T(8,128)S(1)}, u32[]{:S(2)}, u32[]{:S(2)}) collective-permute-start(f32[4,128,128]{2,1,0:T(8,128)S(1)} %get-tuple-element.26), channel_id=1, source_target_pairs={{0,8},{8,16},{16,24},{1,9},{9,17},{17,25},{2,10},{10,18},{18,26},{... | collective-permute-start | bytes 786440 | tf_op jit(solution)/shard_map/ppermute | solution.py:31
  63.7 8.1 %collective-permute-start.7 = (f32[72,4,128]{2,1,0:T(4,128)S(1)}, f32[72,4,128]{2,1,0:T(4,128)S(1)}, u32[]{:S(2)}, u32[]{:S(2)}) collective-permute-start(f32[72,4,128]{2,1,0:T(4,128)S(1)} %get-tuple-element.23), channel_id=1, source_target_pairs={{1,0},{2,1},{3,2},{4,3},{5,4},{6,5},{7,6},{9,8},{10,9},{11,10},{12... | collective-permute-start | bytes 442376 | tf_op jit(solution)/shard_map/ppermute | solution.py:32
  65.0 11.4 %collective-permute-start.6 = (f32[72,4,128]{2,1,0:T(4,128)S(1)}, f32[72,4,128]{2,1,0:T(4,128)S(1)}, u32[]{:S(2)}, u32[]{:S(2)}) collective-permute-start(f32[72,4,128]{2,1,0:T(4,128)S(1)} %get-tuple-element.22), channel_id=1, source_target_pairs={{0,1},{1,2},{2,3},{3,4},{4,5},{5,6},{6,7},{8,9},{9,10},{10,11},{11... | collective-permute-start | bytes 442376 | tf_op jit(solution)/shard_map/ppermute | solution.py:31
  84.2 27.7 %copy-start.1 = (f32[4,8,24,128]{3,2,1,0:T(8,128)S(1)}, f32[4,8,24,128]{3,2,1,0:T(8,128)}, u32[]{:S(2)}) copy-start(f32[4,8,24,128]{3,2,1,0:T(8,128)} %get-tuple-element.31) | copy-start | bytes 1179652
  84.2 27.7 %copy-start.2 = (f32[4,8,24,128]{3,2,1,0:T(8,128)S(1)}, f32[4,8,24,128]{3,2,1,0:T(8,128)}, u32[]{:S(2)}) copy-start(f32[4,8,24,128]{3,2,1,0:T(8,128)} %get-tuple-element.32) | copy-start | bytes 1179652
  84.2 27.7 %copy-start.3 = (f32[4,8,24,128]{3,2,1,0:T(8,128)S(1)}, f32[4,8,24,128]{3,2,1,0:T(8,128)}, u32[]{:S(2)}) copy-start(f32[4,8,24,128]{3,2,1,0:T(8,128)} %get-tuple-element.33) | copy-start | bytes 1179652
  111.9 22.3 %copy-start.4 = (f32[4,8,128]{2,1,0:T(8,128)S(1)}, f32[4,8,128]{2,1,0:T(8,128)}, u32[]{:S(2)}) copy-start(f32[4,8,128]{2,1,0:T(8,128)} %param.6) | copy-start | bytes 49156
where the time goes:
time: 136 us; the launch traced here: 135 us
  other arithmetic  42.7 us (31%)
  matrix products  38.1 us (28%)
  starting transfers between devices  22.6 us (17%)
  waiting for transfers between devices  20.3 us (15%)
  local copies, waits for them, and re-layouts  10.2 us (7%)
    dot_general x1, matrix products, gradients(): jnp.einsum('...mk,...jck->...jmc', tile_resid, stacked, precision=lax.Pre...  27.7 us
    reduce_sum x1, other arithmetic, over_y(): return jnp.sum(block_pqc * profile_q[..., None, :, :], axis=-2)  21.6 us
    ppermute x4, waiting for transfers between devices, from_behind(): return lax.ppermute(block, axis, route)  15.4 us
    ppermute x2, starting transfers between devices, with_halo(): before = lax.ppermute(last, axis, up)  11.7 us
    dot_general x1, matrix products, render(): jnp.einsum('...cm,...ck->...mk', plane_xy, value_z * weight[..., None], p...  10.4 us
    ppermute x4, starting transfers between devices, from_behind(): return lax.ppermute(block, axis, route)  8.39 us
    mul x3, other arithmetic, profiles(): profile = exponent * falloff * falloff  5.53 us
    ppermute x2, waiting for transfers between devices, with_halo(): before = lax.ppermute(last, axis, up)  4.67 us
  transfers between devices with their start and end apart: 8, of which 6 were waited for; matrix products, arithmetic and copies ran while one was open for 4% of the time, Pallas kernels for 0%

commit v1 on v0

v1 whole, which is shorter than its diff:
```python
import functools
import math

import jax
import jax.numpy as jnp
from jax import lax
from jax.experimental import pallas as pl
from jax.experimental.pallas import tpu as pltpu
from jax.sharding import PartitionSpec as P

SUB = 16
RAD = 4
TILE = 24
CAP = 128
DEPTH = 128
FIELDS = 8

EIGHT_PI_SQ = 8.0 * math.pi**2
BLUR_VAR = 0.5
REACH_SQ = float(RAD * RAD)


def shift(block, axis, step):
    peers = lax.axis_size(axis)
    route = [(i, i + step) for i in range(peers) if 0 <= i + step < peers]
    return lax.ppermute(block, axis, route)


def split(value):
    high = value.astype(jnp.bfloat16)
    low = (value - high.astype(jnp.float32)).astype(jnp.bfloat16)
    return high, low


def base_profile(coordinate, sharpness, span, offset):
    grid = (lax.broadcasted_iota(jnp.int32, (span, CAP), 0) + offset).astype(jnp.float32)
    distance = grid - coordinate
    square = distance * distance
    falloff = jnp.maximum(1.0 - square * (1.0 / REACH_SQ), 0.0)
    damped = jnp.exp(-sharpness * square) * falloff
    return distance, square, falloff, damped


def value_only(coordinate, sharpness, span, offset):
    _, _, falloff, damped = base_profile(coordinate, sharpness, span, offset)
    return damped * falloff


def all_kinds(coordinate, sharpness, span, offset):
    distance, square, falloff, damped = base_profile(coordinate, sharpness, span, offset)
    value = damped * falloff
    slope = 2.0 * distance * (sharpness * value + (2.0 / REACH_SQ) * damped)
    width = -square * value
    return value, slope, width


def kernel(
    rows_n, cols_n,
    valid_ref, atoms_ref, xrim_ref, yrim_ref, map_hbm,
    out_hbm, grad_ref,
    field, pieces, map_v, out_v, prof_x, in_sem, out_sem,
):
    nx, ny = rows_n * SUB, cols_n * SUB
    ex, ey = nx + 2 * RAD, ny + 2 * RAD
    load = pltpu.make_async_copy(map_hbm, map_v, in_sem)
    load.start()

    def atom(ai, bi):
        data = atoms_ref[ai, bi]
        cx = data[0:1] * float(SUB)
        cy = data[1:2] * float(SUB)
        cz = data[2:3] * float(DEPTH)
        sharp = 0.5 / (data[3:4] / EIGHT_PI_SQ + BLUR_VAR)
        return cx, cy, cz, sharp, data[4:5]

    def clear(i, _):
        field[i] = jnp.zeros((ey, DEPTH), jnp.float32)
        return 0

    lax.fori_loop(0, ex, clear, 0)

    def render(ai, bi, p0, p_n, j0, j_n):
        cx, cy, cz, sharp, weight = atom(ai, bi)
        vx = value_only(cx, sharp, p_n, p0 - RAD) * weight
        vy = value_only(cy, sharp, 8 * j_n, 8 * j0 - RAD)
        z_hi, z_lo = split(value_only(cz, sharp, DEPTH, 0))
        weights = jnp.concatenate(
            [jnp.concatenate([z_hi, z_hi], 1), jnp.concatenate([z_lo, z_lo], 1)], 0
        )
        rows = []
        for p in range(p_n):
            for j in range(j_n):
                rows.append(vx[p : p + 1] * vy[8 * j : 8 * j + 8])
        plane_hi, plane_lo = split(jnp.concatenate(rows, 0))
        plane = jnp.concatenate([plane_hi, plane_lo], 1)
        both = lax.dot_general(
            plane, weights, (((1,), (1,)), ((), ())), preferred_element_type=jnp.float32
        )
        total = both[:, :DEPTH] + both[:, DEPTH:]
        x0 = SUB * (ai - 1) + p0
        y0 = SUB * (bi - 1) + 8 * j0
        if not isinstance(y0, int):
            y0 = pl.multiple_of(y0, 8)
        for p in range(p_n):
            field[x0 + p, pl.ds(y0, 8 * j_n), :] += total[8 * j_n * p : 8 * j_n * (p + 1)]

    def own(i, _):
        render(i // cols_n + 1, i % cols_n + 1, 0, TILE, 0, 3)
        return 0

    lax.fori_loop(0, rows_n * cols_n, own, 0)

    def x_side(i, _):
        render(0, i + 1, SUB, 8, 0, 3)
        render(rows_n + 1, i + 1, 0, 8, 0, 3)
        return 0

    lax.fori_loop(0, cols_n, x_side, 0)

    def y_side(i, _):
        render(i + 1, 0, 0, TILE, 2, 1)
        render(i + 1, cols_n + 1, 0, TILE, 0, 1)
        return 0

    lax.fori_loop(0, rows_n, y_side, 0)
    for ai, p0 in ((0, SUB), (rows_n + 1, 0)):
        for bi, j0 in ((0, 2), (cols_n + 1, 0)):
            render(ai, bi, p0, 8, j0, 1)

    load.wait()

    def brick(i, _):
        inside = field[i + RAD, RAD : RAD + ny, :] - map_v[i].astype(jnp.float32)
        field[i + RAD, RAD : RAD + ny, :] = inside
        out_v[i] = inside.astype(jnp.bfloat16)
        return 0

    lax.fori_loop(0, nx, brick, 0)
    store = pltpu.make_async_copy(out_v, out_hbm, out_sem)
    store.start()

    def y_rim(i, _):
        rim = yrim_ref[i]
        field[i, 0:RAD, :] = valid_ref[2] * (field[i, 0:RAD, :] - rim[0:RAD])
        field[i, RAD + ny : ey, :] = valid_ref[3] * (field[i, RAD + ny : ey, :] - rim[RAD : 2 * RAD])
        return 0

    lax.fori_loop(0, ex, y_rim, 0)
    for i in range(RAD):
        for side, row in ((0, i), (1, RAD + nx + i)):
            field[row, RAD : RAD + ny, :] -= xrim_ref[side, i]
            field[row] = valid_ref[side] * field[row]

    def pack(i, _):
        for j in range(ey // 8):
            pair = jnp.concatenate(
                [field[2 * i, 8 * j : 8 * j + 8, :], field[2 * i + 1, 8 * j : 8 * j + 8, :]], 0
            )
            hi, lo = split(pair)
            pieces[i, 16 * j : 16 * j + 16, :] = jnp.concatenate([hi, lo], 1)
        return 0

    lax.fori_loop(0, ex // 2, pack, 0)

    def gradient(i, _):
        a, b = i // cols_n, i % cols_n
        cx, cy, cz, sharp, weight = atom(a + 1, b + 1)
        for k, kind in enumerate(all_kinds(cx, sharp, TILE, -RAD)):
            prof_x[k] = kind
        vy, sy, wy = all_kinds(cy, sharp, TILE, -RAD)
        vz, sz, wz = all_kinds(cz, sharp, DEPTH, 0)
        vz_hi, vz_lo = split(vz)
        sz_hi, sz_lo = split(sz)
        wz_hi = wz.astype(jnp.bfloat16)
        tile = pieces[pl.ds(8 * a, TILE // 2), pl.ds(pl.multiple_of(32 * b, 32), 2 * TILE), :]
        tile = tile.reshape(TILE * TILE, 2 * DEPTH)

        def project(rhs):
            return jnp.dot(tile, rhs, preferred_element_type=jnp.float32)

        def twice(top):
            return jnp.concatenate([top, top], 0)

        proj_v = project(twice(jnp.concatenate([vz_hi, vz_lo], 1)))
        proj_s = project(twice(jnp.concatenate([sz_hi, sz_lo], 1)))
        proj_w = project(twice(wz_hi))
        acc = [[jnp.zeros((8, CAP), jnp.float32) for _ in range(3)] for _ in range(4)]
        for p in range(TILE):
            vx = prof_x[0, p : p + 1, :]
            sx = prof_x[1, p : p + 1, :]
            wx = prof_x[2, p : p + 1, :]
            for j in range(3):
                at = ((p // 2) * 3 + j) * 16 + (p % 2) * 8
                base = proj_v[at : at + 8, :CAP] + proj_v[at : at + 8, CAP:]
                lift = proj_s[at : at + 8, :CAP] + proj_s[at : at + 8, CAP:]
                wide = proj_w[at : at + 8]
                acc[0][j] += base * vx
                acc[1][j] += base * sx
                acc[2][j] += lift * vx
                acc[3][j] += base * wx + wide * vx
        g_x = g_y = g_z = g_s = 0.0
        for j in range(3):
            at = slice(8 * j, 8 * j + 8)
            g_x += acc[1][j] * vy[at]
            g_y += acc[0][j] * sy[at]
            g_z += acc[2][j] * vy[at]
            g_s += acc[3][j] * vy[at] + acc[0][j] * wy[at]
        scale = -2.0 * sharp * sharp / EIGHT_PI_SQ
        for k, g in enumerate((g_x, g_y, g_z, g_s)):
            g = weight * jnp.sum(g, axis=0, keepdims=True)
            if k == 3:
                g = g * scale
            grad_ref[k, a, pl.ds(b, 1), :] = g
        return 0

    lax.fori_loop(0, rows_n * cols_n, gradient, 0)
    store.wait()


def local(atom_pos, b_factor, amplitude, counts, density_map):
    rows_n, cols_n = counts.shape
    nx, ny = rows_n * SUB, cols_n * SUB
    ex, ey = nx + 2 * RAD, ny + 2 * RAD
    live = jnp.arange(CAP)[None, None, :] < counts[..., None]
    weight = jnp.where(live, amplitude, 0.0)
    zero = jnp.zeros_like(weight)
    atoms = jnp.stack([atom_pos[0], atom_pos[1], atom_pos[2], b_factor, weight, zero, zero, zero], 2)

    def message(rim, subs):
        return jnp.concatenate([rim.astype(jnp.float32).reshape(-1, DEPTH), subs.reshape(-1, CAP)], 0)

    cut = RAD * ny
    from_low = shift(message(density_map[-RAD:], atoms[-1]), "bx", 1)
    from_high = shift(message(density_map[:RAD], atoms[0]), "bx", -1)
    rim_low, rim_high = from_low[:cut].reshape(RAD, ny, DEPTH), from_high[:cut].reshape(RAD, ny, DEPTH)
    subs_low = from_low[cut:].reshape(1, cols_n, FIELDS, CAP)
    subs_high = from_high[cut:].reshape(1, cols_n, FIELDS, CAP)
    tall = jnp.concatenate([subs_low, atoms, subs_high], 0)

    def edge(array):
        return array.astype(jnp.float32)

    def column(at):
        return jnp.concatenate([rim_low[:, at], edge(density_map[:, at]), rim_high[:, at]], 0)

    cut = RAD * ex
    low = shift(message(column(slice(ny - RAD, ny)), tall[:, -1]), "by", 1)
    high = shift(message(column(slice(0, RAD)), tall[:, 0]), "by", -1)
    left, right = low[:cut].reshape(ex, RAD, DEPTH), high[:cut].reshape(ex, RAD, DEPTH)
    tall_low = low[cut:].reshape(rows_n + 2, 1, FIELDS, CAP)
    tall_high = high[cut:].reshape(rows_n + 2, 1, FIELDS, CAP)
    wide = jnp.concatenate([tall_low, tall, tall_high], 1)
    xrim = jnp.stack([rim_low, rim_high])
    yrim = jnp.concatenate([left, right], 1)
    ix, iy = lax.axis_index("bx"), lax.axis_index("by")
    valid = jnp.stack(
        [ix > 0, ix < lax.axis_size("bx") - 1, iy > 0, iy < lax.axis_size("by") - 1]
    ).astype(jnp.float32)

    vmem = pl.BlockSpec(memory_space=pltpu.VMEM)
    anywhere = pl.BlockSpec(memory_space=pl.ANY)
    residual, gradient = pl.pallas_call(
        functools.partial(kernel, rows_n, cols_n),
        out_shape=(
            jax.ShapeDtypeStruct((nx, ny, DEPTH), jnp.bfloat16),
            jax.ShapeDtypeStruct((4, rows_n, cols_n, CAP), jnp.float32),
        ),
        in_specs=[pl.BlockSpec(memory_space=pltpu.SMEM), vmem, vmem, vmem, anywhere],
        out_specs=(anywhere, vmem),
        scratch_shapes=[
            pltpu.VMEM((ex, ey, DEPTH), jnp.float32),
            pltpu.VMEM((ex // 2, 2 * ey, 2 * DEPTH), jnp.bfloat16),
            pltpu.VMEM((nx, ny, DEPTH), jnp.bfloat16),
            pltpu.VMEM((nx, ny, DEPTH), jnp.bfloat16),
            pltpu.VMEM((3, TILE, CAP), jnp.float32),
            pltpu.SemaphoreType.DMA,
            pltpu.SemaphoreType.DMA,
        ],
        compiler_params=pltpu.CompilerParams(vmem_limit_bytes=48 << 20),
    )(valid, wide, xrim, yrim, density_map)
    return residual, gradient


def solution(mesh):
    return jax.shard_map(
        local,
        mesh=mesh,
        in_specs=(
            P(None, "bx", "by", None),
            P("bx", "by", None),
            P("bx", "by", None),
            P("bx", "by"),
            P("bx", "by", None),
        ),
        out_specs=(P("bx", "by", None), P(None, "bx", "by", None)),
        check_vma=False,
    )
```

time: 136 us -> 59.4 us (0.44)
  the two profiles are of different devices: /device:TPU:0 before, /device:TPU:18 now
where the time goes in v1:
time: 59.4 us; the launch traced here: 58.9 us
  Pallas kernels  31.7 us (53%)
  waiting for transfers between devices  11.2 us (19%)
  starting transfers between devices  10.2 us (17%)
  local copies, waits for them, and re-layouts  2.9 us (5%)
  other arithmetic  1.96 us (3%)
  between operations  0.86 us (1%)
    pallas_call x1, Pallas kernels, local(): pl.pallas_call(functools.partial(kernel, rows_n, cols_n), out_shape=(jax....  31.7 us
    ppermute x4, waiting for transfers between devices, shift(): return lax.ppermute(block, axis, route)  11.2 us
    ppermute x4, starting transfers between devices, shift(): return lax.ppermute(block, axis, route)  10.2 us
  transfers between devices with their start and end apart: 4, of which 4 were waited for; matrix products, arithmetic and copies ran while one was open for 2% of the time, Pallas kernels for 0%

profile of v1, /device:TPU:18, one launch (start us, length us, event | category | flops | bytes accessed | tf_op | source)
XLA Modules:
  0.0 58.9 jit_solution(16097255237439802302)
XLA Ops:
  0.6 0.0 copy-start
  0.6 0.9 %fusion.5 = (f32[1,4,8,128]{3,2,1,0:T(8,128)S(1)}, f32[1,4,8,128]{3,2,1,0:T(8,128)S(1)}, f32[1,4,8,128]{3,2,1,0:T(8,128)S(1)}) fusion(f32[3,4,8,128]{3,2,1,0:T(8,128)} %param.5), kind=kLoop, calls=%fused_computation.29 | loop fusion | bytes 98304 | tf_op jit(solution)/shard_map/slice | solution.py:227
  1.5 0.8 %fusion.1 = f32[4,8,128]{2,1,0:T(8,128)S(1)} fusion(f32[4,8,128]{2,1,0:T(8,128)} %param.7, s32[4,8]{1,0:T(4,128)} %param.8), kind=kLoop, calls=%fused_computation.24 | loop fusion | flops 8192 | bytes 32896 | tf_op jit(solution)/shard_map/jit(_where)/select_n | solution.py:225
  2.4 0.9 %stack.38 = f32[4,8,8,128]{3,2,1,0:T(8,128)S(1)} concatenate(f32[4,8,1,128]{3,2,1,0:T(1,128)S(1)} %bitcast.49, f32[4,8,1,128]{3,2,1,0:T(1,128)S(1)} %bitcast.50, f32[4,8,1,128]{3,2,1,0:T(1,128)S(1)} %bitcast.48, f32[4,8,1,128]{3,2,1,0:T(1,128)} %bitcast.51, f32[4,8,1,128]{3,2,1,0:T(1,128)S(1)} %bitcast.47, f32[4,8,1,128]{3,2,1,0:T(1,128)S(1)} %stack_broadcast_in_dim.3, ...), dimensions={2} | concatenate | bytes 262144 | tf_op jit(solution)/shard_map/stack | solution.py:227
  3.3 1.0 %fusion.2 = (bf16[4,128,128]{2,1,0:T(8,128)(2,1)S(1)}, bf16[4,128,128]{2,1,0:T(8,128)(2,1)S(1)}) fusion(bf16[64,128,128]{2,1,0:T(8,128)(2,1)} %map_hbm.1), kind=kLoop, calls=%fused_computation.26 | loop fusion | bytes 524288 | tf_op jit(solution)/shard_map/slice | solution.py:233
  4.3 1.9 %collective-permute-start.1 = (f32[576,128]{1,0:T(8,128)S(1)}, f32[576,128]{1,0:T(8,128)S(1)}, u32[]{:S(2)}, u32[]{:S(2)}) collective-permute-start(f32[576,128]{1,0:T(8,128)S(1)} %pad_maximum_fusion.2), channel_id=1, source_target_pairs={{8,0},{16,8},{24,16},{9,1},{17,9},{25,17},{10,2},{18,10},{26,18},{... | collective-permute-start | bytes 884744 | tf_op jit(solution)/shard_map/ppermute | solution.py:26
  6.3 0.7 %pad_maximum_fusion.1 = f32[576,128]{1,0:T(8,128)} fusion(f32[64,128]{1,0:T(8,128)S(1)} %get-tuple-element.12, f32[512,128]{1,0:T(8,128)S(1)} %bitcast_convert_fusion.1), kind=kLoop, calls=%fused_computation.1 | loop fusion | flops 73728 | bytes 589824 | tf_op jit(solution)/shard_map/concatenate | solution.py:230
  7.0 2.4 %collective-permute-start = (f32[576,128]{1,0:T(8,128)}, f32[576,128]{1,0:T(8,128)S(1)}, u32[]{:S(2)}, u32[]{:S(2)}) collective-permute-start(f32[576,128]{1,0:T(8,128)} %pad_maximum_fusion.1), channel_id=1, source_target_pairs={{0,8},{8,16},{16,24},{1,9},{9,17},{17,25},{2,10},{10,18},{18,26},{... | collective-permute-start | bytes 884744 | tf_op jit(solution)/shard_map/ppermute | solution.py:26
  9.4 0.0 copy-done
  9.5 1.0 %collective-permute-done.1 = f32[576,128]{1,0:T(8,128)S(1)} collective-permute-done((f32[576,128]{1,0:T(8,128)S(1)}, f32[576,128]{1,0:T(8,128)S(1)}, u32[]{:S(2)}, u32[]{:S(2)}) %collective-permute-start.1) | collective-permute-done | bytes 294944 | tf_op jit(solution)/shard_map/ppermute | solution.py:26
  10.5 4.8 %collective-permute-done = f32[576,128]{1,0:T(8,128)S(1)} collective-permute-done((f32[576,128]{1,0:T(8,128)}, f32[576,128]{1,0:T(8,128)S(1)}, u32[]{:S(2)}, u32[]{:S(2)}) %collective-permute-start) | collective-permute-done | bytes 294944 | tf_op jit(solution)/shard_map/ppermute | solution.py:26
  15.3 0.1 pad_maximum_fusion.7
  15.5 3.3 %collective-permute-start.3 = (f32[336,128]{1,0:T(8,128)S(1)}, f32[336,128]{1,0:T(8,128)S(1)}, u32[]{:S(2)}, u32[]{:S(2)}) collective-permute-start(f32[336,128]{1,0:T(8,128)S(1)} %pad_maximum_fusion.6), channel_id=1, source_target_pairs={{1,0},{2,1},{3,2},{4,3},{5,4},{6,5},{7,6},{9,8},{10,9},{11,10},{12... | collective-permute-start | bytes 516104 | tf_op jit(solution)/shard_map/ppermute | solution.py:26
  18.8 2.5 %collective-permute-start.2 = (f32[336,128]{1,0:T(8,128)S(1)}, f32[336,128]{1,0:T(8,128)S(1)}, u32[]{:S(2)}, u32[]{:S(2)}) collective-permute-start(f32[336,128]{1,0:T(8,128)S(1)} %pad_maximum_fusion.5), channel_id=1, source_target_pairs={{0,1},{1,2},{2,3},{3,4},{4,5},{5,6},{6,7},{8,9},{9,10},{10,11},{11... | collective-permute-start | bytes 516104 | tf_op jit(solution)/shard_map/ppermute | solution.py:26
  21.3 0.1 add_convert_fusion.valid_ref
  21.5 2.1 %collective-permute-done.3 = f32[336,128]{1,0:T(8,128)S(1)} collective-permute-done((f32[336,128]{1,0:T(8,128)S(1)}, f32[336,128]{1,0:T(8,128)S(1)}, u32[]{:S(2)}, u32[]{:S(2)}) %collective-permute-start.3) | collective-permute-done | bytes 172064 | tf_op jit(solution)/shard_map/ppermute | solution.py:26
  23.5 3.4 %collective-permute-done.2 = f32[336,128]{1,0:T(8,128)S(1)} collective-permute-done((f32[336,128]{1,0:T(8,128)S(1)}, f32[336,128]{1,0:T(8,128)S(1)}, u32[]{:S(2)}, u32[]{:S(2)}) %collective-permute-start.2) | collective-permute-done | bytes 172064 | tf_op jit(solution)/shard_map/ppermute | solution.py:26
  27.0 0.1 pad_maximum_fusion.3.yrim_ref
  27.1 31.7 %shard_map.68 = (bf16[64,128,128]{2,1,0:T(8,128)(2,1)}, f32[4,4,8,128]{3,2,1,0:T(8,128)}) custom-call(f32[4]{0:T(128)S(1)} %add_convert_fusion.valid_ref, f32[6,10,8,128]{3,2,1,0:T(8,128)S(1)} %pad_maximum_fusion.4.atoms_ref, f32[2,4,128,128]{3,2,1,0:T(8,128)S(1)} %pad_maximum_fusion.xrim_ref, f32[72,8,128]{2,1,0:T(8,128)S(1)} %pad_maximum_fusion.3.yrim_ref, ...), custom_call_target="tpu_custom_call" | custom-call | tf_op jit(solution)/shard_map/pallas_call | solution.py:262
  (22 shorter events, 0.3 us)
Async XLA Ops:
  0.6 8.8 %copy-start = (bf16[64,128,128]{2,1,0:T(8,128)(2,1)S(1)}, bf16[64,128,128]{2,1,0:T(8,128)(2,1)}, u32[]{:S(2)}) copy-start(bf16[64,128,128]{2,1,0:T(8,128)(2,1)} %map_hbm.1) | copy-start | bytes 6291460
  4.3 6.1 %collective-permute-start.1 = (f32[576,128]{1,0:T(8,128)S(1)}, f32[576,128]{1,0:T(8,128)S(1)}, u32[]{:S(2)}, u32[]{:S(2)}) collective-permute-start(f32[576,128]{1,0:T(8,128)S(1)} %pad_maximum_fusion.2), channel_id=1, source_target_pairs={{8,0},{16,8},{24,16},{9,1},{17,9},{25,17},{10,2},{18,10},{26,18},{... | collective-permute-start | bytes 884744 | tf_op jit(solution)/shard_map/ppermute | solution.py:26
  7.0 8.2 %collective-permute-start = (f32[576,128]{1,0:T(8,128)}, f32[576,128]{1,0:T(8,128)S(1)}, u32[]{:S(2)}, u32[]{:S(2)}) collective-permute-start(f32[576,128]{1,0:T(8,128)} %pad_maximum_fusion.1), channel_id=1, source_target_pairs={{0,8},{8,16},{16,24},{1,9},{9,17},{17,25},{2,10},{10,18},{18,26},{... | collective-permute-start | bytes 884744 | tf_op jit(solution)/shard_map/ppermute | solution.py:26
  15.5 8.1 %collective-permute-start.3 = (f32[336,128]{1,0:T(8,128)S(1)}, f32[336,128]{1,0:T(8,128)S(1)}, u32[]{:S(2)}, u32[]{:S(2)}) collective-permute-start(f32[336,128]{1,0:T(8,128)S(1)} %pad_maximum_fusion.6), channel_id=1, source_target_pairs={{1,0},{2,1},{3,2},{4,3},{5,4},{6,5},{7,6},{9,8},{10,9},{11,10},{12... | collective-permute-start | bytes 516104 | tf_op jit(solution)/shard_map/ppermute | solution.py:26
  18.8 8.2 %collective-permute-start.2 = (f32[336,128]{1,0:T(8,128)S(1)}, f32[336,128]{1,0:T(8,128)S(1)}, u32[]{:S(2)}, u32[]{:S(2)}) collective-permute-start(f32[336,128]{1,0:T(8,128)S(1)} %pad_maximum_fusion.5), channel_id=1, source_target_pairs={{0,1},{1,2},{2,3},{3,4},{4,5},{5,6},{6,7},{8,9},{9,10},{10,11},{11... | collective-permute-start | bytes 516104 | tf_op jit(solution)/shard_map/ppermute | solution.py:26

commit v2 on v1

--- a/solution.py
+++ b/solution.py
@@ -22,7 +22,7 @@
 
 def shift(block, axis, step):
     peers = lax.axis_size(axis)
-    route = [(i, i + step) for i in range(peers) if 0 <= i + step < peers]
+    route = [(i, (i + step) % peers) for i in range(peers)]
     return lax.ppermute(block, axis, route)
 
 
@@ -108,21 +108,21 @@
         render(i // cols_n + 1, i % cols_n + 1, 0, TILE, 0, 3)
         return 0
 
-    lax.fori_loop(0, rows_n * cols_n, own, 0)
+    lax.fori_loop(0, rows_n * cols_n, own, 0, unroll=4)
 
     def x_side(i, _):
         render(0, i + 1, SUB, 8, 0, 3)
         render(rows_n + 1, i + 1, 0, 8, 0, 3)
         return 0
 
-    lax.fori_loop(0, cols_n, x_side, 0)
+    lax.fori_loop(0, cols_n, x_side, 0, unroll=4)
 
     def y_side(i, _):
         render(i + 1, 0, 0, TILE, 2, 1)
         render(i + 1, cols_n + 1, 0, TILE, 0, 1)
         return 0
 
-    lax.fori_loop(0, rows_n, y_side, 0)
+    lax.fori_loop(0, rows_n, y_side, 0, unroll=4)
     for ai, p0 in ((0, SUB), (rows_n + 1, 0)):
         for bi, j0 in ((0, 2), (cols_n + 1, 0)):
             render(ai, bi, p0, 8, j0, 1)
@@ -135,7 +135,7 @@
         out_v[i] = inside.astype(jnp.bfloat16)
         return 0
 
-    lax.fori_loop(0, nx, brick, 0)
+    lax.fori_loop(0, nx, brick, 0, unroll=4)
     store = pltpu.make_async_copy(out_v, out_hbm, out_sem)
     store.start()
 
@@ -160,7 +160,7 @@
             pieces[i, 16 * j : 16 * j + 16, :] = jnp.concatenate([hi, lo], 1)
         return 0
 
-    lax.fori_loop(0, ex // 2, pack, 0)
+    lax.fori_loop(0, ex // 2, pack, 0, unroll=2)
 
     def gradient(i, _):
         a, b = i // cols_n, i % cols_n
@@ -213,7 +213,7 @@
             grad_ref[k, a, pl.ds(b, 1), :] = g
         return 0
 
-    lax.fori_loop(0, rows_n * cols_n, gradient, 0)
+    lax.fori_loop(0, rows_n * cols_n, gradient, 0, unroll=8)
     store.wait()
 
 
@@ -221,6 +221,10 @@
     rows_n, cols_n = counts.shape
     nx, ny = rows_n * SUB, cols_n * SUB
     ex, ey = nx + 2 * RAD, ny + 2 * RAD
+    ix, iy = lax.axis_index("bx"), lax.axis_index("by")
+    valid = jnp.stack(
+        [ix > 0, ix < lax.axis_size("bx") - 1, iy > 0, iy < lax.axis_size("by") - 1]
+    ).astype(jnp.float32)
     live = jnp.arange(CAP)[None, None, :] < counts[..., None]
     weight = jnp.where(live, amplitude, 0.0)
     zero = jnp.zeros_like(weight)
@@ -235,7 +239,7 @@
     rim_low, rim_high = from_low[:cut].reshape(RAD, ny, DEPTH), from_high[:cut].reshape(RAD, ny, DEPTH)
     subs_low = from_low[cut:].reshape(1, cols_n, FIELDS, CAP)
     subs_high = from_high[cut:].reshape(1, cols_n, FIELDS, CAP)
-    tall = jnp.concatenate([subs_low, atoms, subs_high], 0)
+    tall = jnp.concatenate([subs_low * valid[0], atoms, subs_high * valid[1]], 0)
 
     def edge(array):
         return array.astype(jnp.float32)
@@ -249,14 +253,9 @@
     left, right = low[:cut].reshape(ex, RAD, DEPTH), high[:cut].reshape(ex, RAD, DEPTH)
     tall_low = low[cut:].reshape(rows_n + 2, 1, FIELDS, CAP)
     tall_high = high[cut:].reshape(rows_n + 2, 1, FIELDS, CAP)
-    wide = jnp.concatenate([tall_low, tall, tall_high], 1)
+    wide = jnp.concatenate([tall_low * valid[2], tall, tall_high * valid[3]], 1)
     xrim = jnp.stack([rim_low, rim_high])
     yrim = jnp.concatenate([left, right], 1)
-    ix, iy = lax.axis_index("bx"), lax.axis_index("by")
-    valid = jnp.stack(
-        [ix > 0, ix < lax.axis_size("bx") - 1, iy > 0, iy < lax.axis_size("by") - 1]
-    ).astype(jnp.float32)
-
     vmem = pl.BlockSpec(memory_space=pltpu.VMEM)
     anywhere = pl.BlockSpec(memory_space=pl.ANY)
     residual, gradient = pl.pallas_call(

time: 59.4 us -> 50.2 us (0.85)
  the two profiles are of different devices: /device:TPU:18 before, /device:TPU:0 now
where the time goes in v2:
time: 50.2 us; the launch traced here: 49.7 us
  Pallas kernels  18.9 us (38%)
  waiting for transfers between devices  15.6 us (31%)
  starting transfers between devices  7.16 us (14%)
  other arithmetic  3.75 us (7%)
  local copies, waits for them, and re-layouts  3.48 us (7%)
  between operations  0.83 us (2%)
    pallas_call x1, Pallas kernels, local(): pl.pallas_call(functools.partial(kernel, rows_n, cols_n), out_shape=(jax....  18.9 us
    ppermute x4, waiting for transfers between devices, shift(): return lax.ppermute(block, axis, route)  15.6 us
    ppermute x4, starting transfers between devices, shift(): return lax.ppermute(block, axis, route)  7.16 us
    mul x2, other arithmetic, local(): wide = jnp.concatenate([tall_low * valid[2], tall, tall_high * valid[3]], 1)  1.3 us
  transfers between devices with their start and end apart: 4, of which 4 were waited for; matrix products, arithmetic and copies ran while one was open for 2% of the time, Pallas kernels for 0%

profile of v2, /device:TPU:0, one launch (start us, length us, event | category | flops | bytes accessed | tf_op | source)
XLA Modules:
  0.0 49.7 jit_solution(5114857878600653900)
XLA Ops:
  0.6 0.0 copy-start
  0.6 0.9 %fusion.9 = (f32[1,4,8,128]{3,2,1,0:T(8,128)S(1)}, f32[1,4,8,128]{3,2,1,0:T(8,128)S(1)}, f32[1,4,8,128]{3,2,1,0:T(8,128)S(1)}) fusion(f32[3,4,8,128]{3,2,1,0:T(8,128)} %param.5), kind=kLoop, calls=%fused_computation.33 | loop fusion | bytes 98304 | tf_op jit(solution)/shard_map/slice | solution.py:231
  1.5 0.8 %fusion.5 = f32[4,8,128]{2,1,0:T(8,128)S(1)} fusion(f32[4,8,128]{2,1,0:T(8,128)} %param.7, s32[4,8]{1,0:T(4,128)} %param.8), kind=kLoop, calls=%fused_computation.28 | loop fusion | flops 8192 | bytes 32896 | tf_op jit(solution)/shard_map/jit(_where)/select_n | solution.py:229
  2.4 0.9 %stack.38 = f32[4,8,8,128]{3,2,1,0:T(8,128)S(1)} concatenate(f32[4,8,1,128]{3,2,1,0:T(1,128)S(1)} %bitcast.53, f32[4,8,1,128]{3,2,1,0:T(1,128)S(1)} %bitcast.54, f32[4,8,1,128]{3,2,1,0:T(1,128)S(1)} %bitcast.52, f32[4,8,1,128]{3,2,1,0:T(1,128)} %bitcast.55, f32[4,8,1,128]{3,2,1,0:T(1,128)S(1)} %bitcast.51, f32[4,8,1,128]{3,2,1,0:T(1,128)S(1)} %stack_broadcast_in_dim.3, ...), dimensions={2} | concatenate | bytes 262144 | tf_op jit(solution)/shard_map/stack | solution.py:231
  3.3 1.0 %fusion.6 = (bf16[4,128,128]{2,1,0:T(8,128)(2,1)S(1)}, bf16[4,128,128]{2,1,0:T(8,128)(2,1)S(1)}) fusion(bf16[64,128,128]{2,1,0:T(8,128)(2,1)} %map_hbm.1), kind=kLoop, calls=%fused_computation.30 | loop fusion | bytes 524288 | tf_op jit(solution)/shard_map/slice | solution.py:237
  4.3 2.4 %collective-permute-start.1 = (f32[576,128]{1,0:T(8,128)S(1)}, f32[576,128]{1,0:T(8,128)S(1)}, u32[]{:S(2)}, u32[]{:S(2)}) collective-permute-start(f32[576,128]{1,0:T(8,128)S(1)} %pad_maximum_fusion.2), channel_id=1, source_target_pairs={{0,24},{8,0},{16,8},{24,16},{1,25},{9,1},{17,9},{25,17},{2,26},{10... | collective-permute-start | bytes 884744 | tf_op jit(solution)/shard_map/ppermute | solution.py:26
  6.8 0.1 collective-permute-start
  6.9 0.1 add_convert_fusion.valid_ref
  7.0 0.0 copy-done
  7.0 0.6 %fusion.10 = (f32[1]{0:T(128)}, f32[1]{0:T(128)}, f32[1]{0:T(128)}, f32[1]{0:T(128)}) fusion(f32[4]{0:T(128)S(1)} %add_convert_fusion.valid_ref), kind=kLoop, calls=%fused_computation.34 | loop fusion | bytes 32 | tf_op jit(solution)/shard_map/slice | solution.py:256
  7.6 6.4 %collective-permute-done.1 = f32[576,128]{1,0:T(8,128)S(1)} collective-permute-done((f32[576,128]{1,0:T(8,128)S(1)}, f32[576,128]{1,0:T(8,128)S(1)}, u32[]{:S(2)}, u32[]{:S(2)}) %collective-permute-start.1) | collective-permute-done | bytes 294944 | tf_op jit(solution)/shard_map/ppermute | solution.py:26
  14.1 1.1 %collective-permute-done = f32[576,128]{1,0:T(8,128)S(1)} collective-permute-done((f32[576,128]{1,0:T(8,128)S(1)}, f32[576,128]{1,0:T(8,128)S(1)}, u32[]{:S(2)}, u32[]{:S(2)}) %collective-permute-start) | collective-permute-done | bytes 294944 | tf_op jit(solution)/shard_map/ppermute | solution.py:26
  15.2 0.6 %fusion = f32[1,8,8,128]{3,2,1,0:T(8,128)S(1)} fusion(f32[576,128]{1,0:T(8,128)S(1)} %collective-permute-done.1, f32[]{:T(128)} %bitcast.18), kind=kLoop, calls=%fused_computation.14 | loop fusion | flops 8192 | bytes 65540 | tf_op jit(solution)/shard_map/mul | solution.py:242
  15.8 0.6 %fusion.1 = f32[1,8,8,128]{3,2,1,0:T(8,128)S(1)} fusion(f32[576,128]{1,0:T(8,128)S(1)} %collective-permute-done, f32[]{:T(128)} %bitcast.16), kind=kLoop, calls=%fused_computation.16 | loop fusion | flops 8192 | bytes 65540 | tf_op jit(solution)/shard_map/mul | solution.py:242
  16.4 0.1 pad_maximum_fusion.7
  16.6 4.6 %collective-permute-start.3 = (f32[336,128]{1,0:T(8,128)S(1)}, f32[336,128]{1,0:T(8,128)S(1)}, u32[]{:S(2)}, u32[]{:S(2)}) collective-permute-start(f32[336,128]{1,0:T(8,128)S(1)} %pad_maximum_fusion.6), channel_id=1, source_target_pairs={{0,7},{1,0},{2,1},{3,2},{4,3},{5,4},{6,5},{7,6},{8,15},{9,8},{10,9... | collective-permute-start | bytes 516104 | tf_op jit(solution)/shard_map/ppermute | solution.py:26
  21.2 0.1 collective-permute-start.2
  21.3 2.8 %collective-permute-done.3 = f32[336,128]{1,0:T(8,128)S(1)} collective-permute-done((f32[336,128]{1,0:T(8,128)S(1)}, f32[336,128]{1,0:T(8,128)S(1)}, u32[]{:S(2)}, u32[]{:S(2)}) %collective-permute-start.3) | collective-permute-done | bytes 172064 | tf_op jit(solution)/shard_map/ppermute | solution.py:26
  24.2 5.2 %collective-permute-done.2 = f32[336,128]{1,0:T(8,128)S(1)} collective-permute-done((f32[336,128]{1,0:T(8,128)S(1)}, f32[336,128]{1,0:T(8,128)S(1)}, u32[]{:S(2)}, u32[]{:S(2)}) %collective-permute-start.2) | collective-permute-done | bytes 172064 | tf_op jit(solution)/shard_map/ppermute | solution.py:26
  29.4 0.1 pad_maximum_fusion.3.yrim_ref
  29.4 0.7 %fusion.2 = f32[6,1,8,128]{3,2,1,0:T(8,128)S(1)} fusion(f32[336,128]{1,0:T(8,128)S(1)} %collective-permute-done.3, f32[]{:T(128)} %bitcast.25), kind=kLoop, calls=%fused_computation.20 | loop fusion | flops 6144 | bytes 49156 | tf_op jit(solution)/shard_map/mul | solution.py:256
  30.1 0.7 %fusion.4 = f32[6,1,8,128]{3,2,1,0:T(8,128)S(1)} fusion(f32[336,128]{1,0:T(8,128)S(1)} %collective-permute-done.2, f32[]{:T(128)} %bitcast.21), kind=kLoop, calls=%fused_computation.25 | loop fusion | flops 6144 | bytes 49156 | tf_op jit(solution)/shard_map/mul | solution.py:256
  30.8 18.9 %shard_map.68 = (bf16[64,128,128]{2,1,0:T(8,128)(2,1)}, f32[4,4,8,128]{3,2,1,0:T(8,128)}) custom-call(f32[4]{0:T(128)S(1)} %add_convert_fusion.valid_ref, f32[6,10,8,128]{3,2,1,0:T(8,128)S(1)} %pad_maximum_fusion.4.atoms_ref, f32[2,4,128,128]{3,2,1,0:T(8,128)S(1)} %pad_maximum_fusion.xrim_ref, f32[72,8,128]{2,1,0:T(8,128)S(1)} %pad_maximum_fusion.3.yrim_ref, ...), custom_call_target="tpu_custom_call" | custom-call | tf_op jit(solution)/shard_map/pallas_call | solution.py:261
  (19 shorter events, 0.3 us)
Async XLA Ops:
  0.6 6.3 %copy-start = (bf16[64,128,128]{2,1,0:T(8,128)(2,1)S(1)}, bf16[64,128,128]{2,1,0:T(8,128)(2,1)}, u32[]{:S(2)}) copy-start(bf16[64,128,128]{2,1,0:T(8,128)(2,1)} %map_hbm.1) | copy-start | bytes 6291460
  4.3 9.7 %collective-permute-start.1 = (f32[576,128]{1,0:T(8,128)S(1)}, f32[576,128]{1,0:T(8,128)S(1)}, u32[]{:S(2)}, u32[]{:S(2)}) collective-permute-start(f32[576,128]{1,0:T(8,128)S(1)} %pad_maximum_fusion.2), channel_id=1, source_target_pairs={{0,24},{8,0},{16,8},{24,16},{1,25},{9,1},{17,9},{25,17},{2,26},{10... | collective-permute-start | bytes 884744 | tf_op jit(solution)/shard_map/ppermute | solution.py:26
  6.8 8.4 %collective-permute-start = (f32[576,128]{1,0:T(8,128)S(1)}, f32[576,128]{1,0:T(8,128)S(1)}, u32[]{:S(2)}, u32[]{:S(2)}) collective-permute-start(f32[576,128]{1,0:T(8,128)S(1)} %pad_maximum_fusion.1), channel_id=1, source_target_pairs={{0,8},{8,16},{16,24},{24,0},{1,9},{9,17},{17,25},{25,1},{2,10},{10... | collective-permute-start | bytes 884744 | tf_op jit(solution)/shard_map/ppermute | solution.py:26
  16.6 7.6 %collective-permute-start.3 = (f32[336,128]{1,0:T(8,128)S(1)}, f32[336,128]{1,0:T(8,128)S(1)}, u32[]{:S(2)}, u32[]{:S(2)}) collective-permute-start(f32[336,128]{1,0:T(8,128)S(1)} %pad_maximum_fusion.6), channel_id=1, source_target_pairs={{0,7},{1,0},{2,1},{3,2},{4,3},{5,4},{6,5},{7,6},{8,15},{9,8},{10,9... | collective-permute-start | bytes 516104 | tf_op jit(solution)/shard_map/ppermute | solution.py:26
  21.2 8.2 %collective-permute-start.2 = (f32[336,128]{1,0:T(8,128)S(1)}, f32[336,128]{1,0:T(8,128)S(1)}, u32[]{:S(2)}, u32[]{:S(2)}) collective-permute-start(f32[336,128]{1,0:T(8,128)S(1)} %pad_maximum_fusion.5), channel_id=1, source_target_pairs={{0,1},{1,2},{2,3},{3,4},{4,5},{5,6},{6,7},{7,0},{8,9},{9,10},{10,1... | collective-permute-start | bytes 516104 | tf_op jit(solution)/shard_map/ppermute | solution.py:26

commit v3 on v2

v3 whole, which is shorter than its diff:
```python
import functools
import math

import jax
import jax.numpy as jnp
from jax import lax
from jax.experimental import pallas as pl
from jax.experimental.pallas import tpu as pltpu
from jax.sharding import PartitionSpec as P

SUB = 16
RAD = 4
TILE = 24
CAP = 128
DEPTH = 128
FIELDS = 5
BAND = 24

EIGHT_PI_SQ = 8.0 * math.pi**2
BLUR_VAR = 0.5
REACH_SQ = float(RAD * RAD)
VMEM_LIMIT = 18 << 20


def shift(block, axis, step):
    peers = lax.axis_size(axis)
    route = [(i, (i + step) % peers) for i in range(peers)]
    return lax.ppermute(block, axis, route)


def swap(block, odd):
    nx, ny = lax.axis_size("bx"), lax.axis_size("by")
    route = []
    for x in range(nx):
        for y in range(ny):
            to_x, to_y = x, (y ^ 1 if not odd else ((y + 1) ^ 1) - 1)
            if not 0 <= to_y < ny:
                to_x, to_y = x ^ 1, y
            route.append((x * ny + y, to_x * ny + to_y))
    return lax.ppermute(block, ("bx", "by"), route)


def neighbours(low, high):
    even = lax.axis_index("by") % 2 == 0
    first = swap(jnp.where(even, high, low), False)
    second = swap(jnp.where(even, low, high), True)
    return jnp.where(even, second, first), jnp.where(even, first, second)


def split(value):
    high = value.astype(jnp.bfloat16)
    low = (value - high.astype(jnp.float32)).astype(jnp.bfloat16)
    return high, low


def base_profile(coordinate, sharpness, span, offset):
    grid = (lax.broadcasted_iota(jnp.int32, (span, CAP), 0) + offset).astype(jnp.float32)
    distance = grid - coordinate
    square = distance * distance
    falloff = jnp.maximum(1.0 - square * (1.0 / REACH_SQ), 0.0)
    damped = jnp.exp(-sharpness * square) * falloff
    return distance, square, falloff, damped


def value_only(coordinate, sharpness, span, offset):
    _, _, falloff, damped = base_profile(coordinate, sharpness, span, offset)
    return damped * falloff


def all_kinds(coordinate, sharpness, span, offset):
    distance, square, falloff, damped = base_profile(coordinate, sharpness, span, offset)
    value = damped * falloff
    slope = 2.0 * distance * (sharpness * value + (2.0 / REACH_SQ) * damped)
    width = -square * value
    return value, slope, width


def terms(x, y, z, b_factor):
    cx, cy, cz = x * float(SUB), y * float(SUB), z * float(DEPTH)
    return cx, cy, cz, 0.5 / (b_factor / EIGHT_PI_SQ + BLUR_VAR)


def fetch(pairs, sems):
    copies = [pltpu.make_async_copy(a, b, sems.at[i]) for i, (a, b) in enumerate(pairs)]
    for copy in copies:
        copy.start()
    return copies


def finish(copies):
    for copy in copies:
        copy.wait()


def masked(amplitude, count):
    slot = lax.broadcasted_iota(jnp.int32, (1, CAP), 1)
    return jnp.where(slot < count, amplitude, 0.0)


def own_atom(counts_ref, pos_ref, bfac_ref, amp_ref, a, b):
    row = pl.ds(b, 1)
    found = terms(*(pos_ref[k, a, row, :] for k in range(3)), bfac_ref[a, row, :])
    return found + (masked(amp_ref[a, row, :], counts_ref[a, b]),)


def sent_atom(message, start, stride, index, valid):
    row = [message[pl.ds(start + k * stride + index, 1), :] for k in range(FIELDS)]
    return terms(*row[:4]) + (row[4] * valid,)


def rendered(atom, p0, p_n, j0, j_n):
    cx, cy, cz, sharp, weight = atom
    vx = value_only(cx, sharp, p_n, p0 - RAD) * weight
    vy = value_only(cy, sharp, 8 * j_n, 8 * j0 - RAD)
    z_hi, z_lo = split(value_only(cz, sharp, DEPTH, 0))
    weights = jnp.concatenate(
        [jnp.concatenate([z_hi, z_hi], 1), jnp.concatenate([z_lo, z_lo], 1)], 0
    )
    rows = []
    for p in range(p_n):
        for j in range(j_n):
            rows.append(vx[p : p + 1] * vy[8 * j : 8 * j + 8])
    plane_hi, plane_lo = split(jnp.concatenate(rows, 0))
    plane = jnp.concatenate([plane_hi, plane_lo], 1)
    both = lax.dot_general(
        plane, weights, (((1,), (1,)), ((), ())), preferred_element_type=jnp.float32
    )
    total = both[:, :DEPTH] + both[:, DEPTH:]
    return [total[8 * j_n * p : 8 * j_n * (p + 1)] for p in range(p_n)]


def packed(first, second):
    hi, lo = split(jnp.concatenate([first, second], 0))
    return jnp.concatenate([hi, lo], 1)


def tile_gradient(atom, pieces, prof_x, grad_ref, a, b):
    cx, cy, cz, sharp, weight = atom
    for k, kind in enumerate(all_kinds(cx, sharp, TILE, -RAD)):
        prof_x[k] = kind
    vy, sy, wy = all_kinds(cy, sharp, TILE, -RAD)
    vz, sz, wz = all_kinds(cz, sharp, DEPTH, 0)
    vz_hi, vz_lo = split(vz)
    sz_hi, sz_lo = split(sz)
    wz_hi = wz.astype(jnp.bfloat16)
    tile = pieces[pl.ds(8 * a, TILE // 2), pl.ds(pl.multiple_of(32 * b, 32), 2 * TILE), :]
    tile = tile.reshape(TILE * TILE, 2 * DEPTH)

    def project(rhs):
        return jnp.dot(tile, jnp.concatenate([rhs, rhs], 0), preferred_element_type=jnp.float32)

    proj_v = project(jnp.concatenate([vz_hi, vz_lo], 1))
    proj_s = project(jnp.concatenate([sz_hi, sz_lo], 1))
    proj_w = project(wz_hi)
    acc = [[jnp.zeros((8, CAP), jnp.float32) for _ in range(3)] for _ in range(4)]
    for p in range(TILE):
        vx = prof_x[0, p : p + 1, :]
        sx = prof_x[1, p : p + 1, :]
        wx = prof_x[2, p : p + 1, :]
        for j in range(3):
            at = ((p // 2) * 3 + j) * 16 + (p % 2) * 8
            base = proj_v[at : at + 8, :CAP] + proj_v[at : at + 8, CAP:]
            lift = proj_s[at : at + 8, :CAP] + proj_s[at : at + 8, CAP:]
            wide = proj_w[at : at + 8]
            acc[0][j] += base * vx
            acc[1][j] += base * sx
            acc[2][j] += lift * vx
            acc[3][j] += base * wx + wide * vx
    g_x = g_y = g_z = g_s = 0.0
    for j in range(3):
        at = slice(8 * j, 8 * j + 8)
        g_x += acc[1][j] * vy[at]
        g_y += acc[0][j] * sy[at]
        g_z += acc[2][j] * vy[at]
        g_s += acc[3][j] * vy[at] + acc[0][j] * wy[at]
    scale = -2.0 * sharp * sharp / EIGHT_PI_SQ
    for k, g in enumerate((g_x, g_y, g_z, g_s)):
        g = weight * jnp.sum(g, axis=0, keepdims=True)
        if k == 3:
            g = g * scale
        grad_ref[k, a, pl.ds(b, 1), :] = g


def message_kernel(
    rows_n, cols_n,
    counts_hbm, pos_hbm, bfac_hbm, amp_hbm, map_hbm,
    xlow_ref, xhigh_ref, ylow_ref, yhigh_ref,
    counts_ref, pos_ref, bfac_ref, amp_ref, own_sems,
    xrim, yrim, sems,
):
    nx, ny = rows_n * SUB, cols_n * SUB
    held = (counts_ref, pos_ref, bfac_ref, amp_ref)
    fetched = fetch(zip((counts_hbm, pos_hbm, bfac_hbm, amp_hbm), held), own_sems)
    copies = []
    for k, at in enumerate((0, nx - RAD)):
        copies.append(pltpu.make_async_copy(map_hbm.at[pl.ds(at, RAD)], xrim.at[k], sems.at[k]))
    for k, at in enumerate((0, ny - SUB)):
        copies.append(
            pltpu.make_async_copy(map_hbm.at[:, pl.ds(at, SUB)], yrim.at[k], sems.at[2 + k])
        )
    for copy in copies:
        copy.start()

    def atoms(out, start, stride, index, a, b):
        fields = [pos_ref[k, a, b : b + 1, :] for k in range(3)] + [bfac_ref[a, b : b + 1, :]]
        fields.append(masked(amp_ref[a, b : b + 1, :], counts_ref[a, b]))
        for k, value in enumerate(fields):
            out[start + k * stride + index : start + k * stride + index + 1, :] = value

    finish(fetched)
    for b in range(cols_n):
        atoms(xlow_ref, RAD * ny, cols_n, b, 0, b)
        atoms(xhigh_ref, RAD * ny, cols_n, b, rows_n - 1, b)
    for out in (ylow_ref, yhigh_ref):
        out[nx * RAD :, :] = jnp.zeros((BAND, CAP), jnp.float32)
    for a in range(rows_n):
        atoms(ylow_ref, RAD * nx, rows_n, a, a, 0)
        atoms(yhigh_ref, RAD * nx, rows_n, a, a, cols_n - 1)
    for copy in copies:
        copy.wait()
    for k, out in enumerate((xlow_ref, xhigh_ref)):
        for i in range(RAD):
            out[ny * i : ny * (i + 1), :] = xrim[k, i].astype(jnp.float32)
    for i in range(nx):
        ylow_ref[RAD * i : RAD * (i + 1), :] = yrim[0, i].astype(jnp.float32)[:RAD]
        yhigh_ref[RAD * i : RAD * (i + 1), :] = yrim[1, i].astype(jnp.float32)[SUB - RAD :]


def inner_kernel(
    rows_n, cols_n,
    counts_hbm, pos_hbm, bfac_hbm, amp_hbm, map_hbm,
    out_hbm, pieces_hbm, xband_hbm, yband_hbm, grad_ref,
    counts_ref, pos_ref, bfac_ref, amp_ref, own_sems,
    field, pieces, map_v, out_v, prof_x, in_sem, out_sems,
):
    nx, ny = rows_n * SUB, cols_n * SUB
    ex, ey = nx + 2 * RAD, ny + 2 * RAD
    held = (counts_ref, pos_ref, bfac_ref, amp_ref)
    fetched = fetch(zip((counts_hbm, pos_hbm, bfac_hbm, amp_hbm), held), own_sems)
    load = pltpu.make_async_copy(map_hbm, map_v, in_sem)
    load.start()

    def clear(i, _):
        field[i] = jnp.zeros((ey, DEPTH), jnp.float32)
        return 0

    lax.fori_loop(0, ex, clear, 0)
    finish(fetched)
    atom_at = functools.partial(own_atom, counts_ref, pos_ref, bfac_ref, amp_ref)

    def own(i, _):
        a, b = i // cols_n, i % cols_n
        y0 = pl.multiple_of(SUB * b, SUB)
        for p, row in enumerate(rendered(atom_at(a, b), 0, TILE, 0, 3)):
            field[SUB * a + p, pl.ds(y0, TILE), :] += row
        return 0

    lax.fori_loop(0, rows_n * cols_n, own, 0, unroll=4)
    load.wait()

    def brick(i, _):
        inside = field[i + RAD, RAD : RAD + ny, :] - map_v[i].astype(jnp.float32)
        field[i + RAD, RAD : RAD + ny, :] = inside
        out_v[i] = inside.astype(jnp.bfloat16)
        return 0

    lax.fori_loop(0, nx, brick, 0, unroll=4)
    rest = pl.ds(2 * RAD, nx - 2 * RAD)
    pairs = [(out_v, out_hbm)]
    for k in range(2):
        pairs.append((field.at[pl.ds((ex - 2 * RAD) * k, 2 * RAD)], xband_hbm.at[k]))
        pairs.append((field.at[rest, pl.ds((ey - BAND) * k, BAND)], yband_hbm.at[k]))
    stores = fetch(pairs, out_sems)

    def pack(i, _):
        for j in range(ey // 8):
            rows = pl.ds(8 * j, 8)
            pieces[i, 16 * j : 16 * j + 16, :] = packed(field[2 * i, rows, :], field[2 * i + 1, rows, :])
        return 0

    lax.fori_loop(RAD, ex // 2 - RAD, pack, 0, unroll=2)
    kept = (pl.ds(RAD, ex // 2 - 2 * RAD), pl.ds(SUB, 2 * ey - 2 * SUB))
    last = pltpu.make_async_copy(pieces.at[kept], pieces_hbm, in_sem)
    last.start()

    def gradient(i, _):
        a, b = i // (cols_n - 2) + 1, i % (cols_n - 2) + 1
        tile_gradient(atom_at(a, b), pieces, prof_x, grad_ref, a, b)
        return 0

    lax.fori_loop(0, (rows_n - 2) * (cols_n - 2), gradient, 0, unroll=6)
    finish(stores)
    last.wait()


def sides_kernel(
    rows_n, cols_n,
    valid_ref, xlow_ref, xhigh_ref, ylow_ref, yhigh_ref, xband_hbm, yband_hbm,
    xband, yband,
    xfield, yfield, sems,
):
    nx, ny = rows_n * SUB, cols_n * SUB
    ex, ey = nx + 2 * RAD, ny + 2 * RAD
    fetched = fetch(((xband_hbm, xfield), (yband_hbm, yfield)), sems)
    xband[...] = jnp.zeros_like(xband)
    yband[...] = jnp.zeros_like(yband)

    def x_side(b, _):
        y0 = pl.multiple_of(SUB * b, SUB)
        for k, (message, p0) in enumerate(((xlow_ref, SUB), (xhigh_ref, 0))):
            atom = sent_atom(message, RAD * ny, cols_n, b, valid_ref[k])
            for p, row in enumerate(rendered(atom, p0, 2 * RAD, 0, 3)):
                xband[k, p, pl.ds(y0, TILE), :] += row
        return 0

    lax.fori_loop(0, cols_n, x_side, 0, unroll=4)
    for a in range(rows_n):
        for k, (message, j0, y0) in enumerate(((ylow_ref, 2, 0), (yhigh_ref, 0, ey - 8))):
            atom = sent_atom(message, RAD * nx, rows_n, a, valid_ref[2 + k])
            for p, row in enumerate(rendered(atom, 0, TILE, j0, 1)):
                x = SUB * a + p
                if x < 2 * RAD:
                    xband[0, x, y0 : y0 + 8, :] += row
                elif x >= ex - 2 * RAD:
                    xband[1, x - (ex - 2 * RAD), y0 : y0 + 8, :] += row
                else:
                    yband[k, x - 2 * RAD, (BAND - 8) * k : (BAND - 8) * k + 8, :] += row
    finish(fetched)
    xband[...] += xfield[...]
    yband[...] += yfield[...]


def outer_kernel(
    rows_n, cols_n,
    valid_ref, counts_hbm, pos_hbm, bfac_hbm, amp_hbm,
    xlow_ref, xhigh_ref, ylow_ref, yhigh_ref, clow_ref, chigh_ref,
    xband_in, yband_in, pieces_hbm, grad_in, out_in,
    out_hbm, grad_ref,
    counts_ref, pos_ref, bfac_ref, amp_ref, own_sems,
    xband, yband, pieces, xout, yout, prof_x, sems,
):
    nx, ny = rows_n * SUB, cols_n * SUB
    ex, ey = nx + 2 * RAD, ny + 2 * RAD
    kept = (pl.ds(RAD, ex // 2 - 2 * RAD), pl.ds(SUB, 2 * ey - 2 * SUB))
    held = (counts_ref, pos_ref, bfac_ref, amp_ref, pieces.at[kept])
    sources = (counts_hbm, pos_hbm, bfac_hbm, amp_hbm, pieces_hbm)
    fetched = fetch(zip(sources, held), own_sems)
    xband[...] = xband_in[...]
    yband[...] = yband_in[...]
    grad_ref[...] = grad_in[...]
    corner = RAD * RAD + FIELDS
    for ky, (message, j0, y0) in enumerate(((clow_ref, 2, 0), (chigh_ref, 0, ey - 8))):
        for kx, p0 in enumerate((SUB, 0)):
            ok = valid_ref[kx] * valid_ref[2 + ky]
            atom = sent_atom(message, corner * kx + RAD * RAD, 1, 0, ok)
            for p, row in enumerate(rendered(atom, p0, 2 * RAD, j0, 1)):
                xband[kx, p, y0 : y0 + 8, :] += row
    for kx, message in enumerate((xlow_ref, xhigh_ref)):
        for i in range(RAD):
            row = RAD * kx + i
            xband[kx, row, RAD : RAD + ny, :] -= message[ny * i : ny * (i + 1), :]
            for ky, sent in enumerate((clow_ref, chigh_ref)):
                y0 = (ey - RAD) * ky
                at = corner * kx + RAD * i
                xband[kx, row, y0 : y0 + RAD, :] -= sent[at : at + RAD, :]
            xband[kx, row] = valid_ref[kx] * xband[kx, row]
    for ky, message in enumerate((ylow_ref, yhigh_ref)):
        y0 = (ey - RAD) * ky
        for kx in range(2):
            for i in range(RAD):
                row = RAD * (1 - kx) + i
                at = RAD * ((nx - RAD) * kx + i)
                xband[kx, row, y0 : y0 + RAD, :] -= message[at : at + RAD, :]
            for i in range(2 * RAD):
                xband[kx, i, y0 : y0 + RAD, :] = valid_ref[2 + ky] * xband[kx, i, y0 : y0 + RAD, :]
        y0 = (BAND - RAD) * ky
        for i in range(nx - 2 * RAD):
            at = RAD * (RAD + i)
            inside = yband[ky, i, y0 : y0 + RAD, :] - message[at : at + RAD, :]
            yband[ky, i, y0 : y0 + RAD, :] = valid_ref[2 + ky] * inside

    stores = []
    for kx in range(2):
        for i in range(RAD):
            xout[kx, i] = xband[kx, RAD * (1 - kx) + i, RAD : RAD + ny, :].astype(jnp.bfloat16)
        stores.append(
            pltpu.make_async_copy(
                xout.at[kx], out_hbm.at[pl.ds((nx - RAD) * kx, RAD)], sems.at[kx]
            )
        )
    for ky in range(2):
        for i in range(nx - 2 * RAD):
            yout[ky, i] = yband[ky, i, RAD : RAD + SUB, :].astype(jnp.bfloat16)
        stores.append(
            pltpu.make_async_copy(
                yout.at[ky],
                out_hbm.at[pl.ds(RAD, nx - 2 * RAD), pl.ds((ny - SUB) * ky, SUB)],
                sems.at[2 + ky],
            )
        )
    for store in stores:
        store.start()
    for kx in range(2):
        for i in range(RAD):
            for j in range(ey // 8):
                rows = slice(8 * j, 8 * j + 8)
                pieces[(ex // 2 - RAD) * kx + i, 16 * j : 16 * j + 16, :] = packed(
                    xband[kx, 2 * i, rows, :], xband[kx, 2 * i + 1, rows, :]
                )
    for ky in range(2):
        rows = slice((BAND - 8) * ky, (BAND - 8) * ky + 8)
        at = 2 * (ey - 8) * ky
        for i in range(nx // 2 - RAD):
            pieces[RAD + i, at : at + 16, :] = packed(
                yband[ky, 2 * i, rows, :], yband[ky, 2 * i + 1, rows, :]
            )
    atom_at = functools.partial(own_atom, counts_ref, pos_ref, bfac_ref, amp_ref)
    finish(fetched)

    def x_edges(i, _):
        a, b = (i // cols_n) * (rows_n - 1), i % cols_n
        tile_gradient(atom_at(a, b), pieces, prof_x, grad_ref, a, b)
        return 0

    def y_edges(i, _):
        a, b = i // 2 + 1, (i % 2) * (cols_n - 1)
        tile_gradient(atom_at(a, b), pieces, prof_x, grad_ref, a, b)
        return 0

    lax.fori_loop(0, 2 * cols_n, x_edges, 0, unroll=8)
    lax.fori_loop(0, 2 * (rows_n - 2), y_edges, 0, unroll=4)
    for store in stores:
        store.wait()


def call(body, sizes, outs, in_specs, out_specs, scratch, cost, aliases=None):
    return pl.pallas_call(
        functools.partial(body, *sizes),
        out_shape=outs,
        in_specs=in_specs,
        out_specs=out_specs,
        scratch_shapes=scratch,
        input_output_aliases=aliases or {},
        cost_estimate=pl.CostEstimate(flops=cost, bytes_accessed=1 << 20, transcendentals=0),
        compiler_params=pltpu.CompilerParams(vmem_limit_bytes=VMEM_LIMIT),
    )


def local(atom_pos, b_factor, amplitude, counts, density_map):
    sizes = rows_n, cols_n = counts.shape
    nx, ny = rows_n * SUB, cols_n * SUB
    ex, ey = nx + 2 * RAD, ny + 2 * RAD
    ix, iy = lax.axis_index("bx"), lax.axis_index("by")
    valid = jnp.stack(
        [ix > 0, ix < lax.axis_size("bx") - 1, iy > 0, iy < lax.axis_size("by") - 1]
    ).astype(jnp.float32)
    f32, bf16 = jnp.float32, jnp.bfloat16
    shape = jax.ShapeDtypeStruct
    vmem = pl.BlockSpec(memory_space=pltpu.VMEM)
    smem = pl.BlockSpec(memory_space=pltpu.SMEM)
    hbm = pl.BlockSpec(memory_space=pltpu.HBM)
    own_scratch = [
        pltpu.SMEM(counts.shape, jnp.int32),
        pltpu.VMEM(atom_pos.shape, f32),
        pltpu.VMEM(b_factor.shape, f32),
        pltpu.VMEM(amplitude.shape, f32),
        pltpu.SemaphoreType.DMA((5,)),
    ]
    own = tuple(
        pltpu.with_memory_space_constraint(array, pltpu.HBM)
        for array in (counts, atom_pos, b_factor, amplitude)
    )
    density_map = pltpu.with_memory_space_constraint(density_map, pltpu.HBM)

    xsize, ysize = RAD * ny + FIELDS * cols_n, RAD * nx + BAND
    xlow, xhigh, ylow, yhigh = call(
        message_kernel,
        sizes,
        (shape((xsize, CAP), f32),) * 2 + (shape((ysize, CAP), f32),) * 2,
        [hbm] * 5,
        (vmem,) * 4,
        own_scratch
        + [
            pltpu.VMEM((2, RAD, ny, DEPTH), bf16),
            pltpu.VMEM((2, nx, SUB, DEPTH), bf16),
            pltpu.SemaphoreType.DMA((4,)),
        ],
        10**6,
    )(*own, density_map)
    from_ylow, from_yhigh = neighbours(ylow, yhigh)
    from_xlow, from_xhigh = shift(xhigh, "bx", 1), shift(xlow, "bx", -1)

    bands = shape((2, 2 * RAD, ey, DEPTH), f32), shape((2, nx - 2 * RAD, BAND, DEPTH), f32)
    residual, *kept, gradient = call(
        inner_kernel,
        sizes,
        (
            shape((nx, ny, DEPTH), bf16),
            pltpu.HBM((ex // 2 - 2 * RAD, 2 * ey - 2 * SUB, 2 * DEPTH), bf16),
            *(pltpu.HBM(band.shape, f32) for band in bands),
            shape((4, rows_n, cols_n, CAP), f32),
        ),
        [hbm] * 5,
        (hbm, hbm, hbm, hbm, vmem),
        own_scratch
        + [
            pltpu.VMEM((ex, ey, DEPTH), f32),
            pltpu.VMEM((ex // 2, 2 * ey, 2 * DEPTH), bf16),
            pltpu.VMEM((nx, ny, DEPTH), bf16),
            pltpu.VMEM((nx, ny, DEPTH), bf16),
            pltpu.VMEM((3, TILE, CAP), f32),
            pltpu.SemaphoreType.DMA,
            pltpu.SemaphoreType.DMA((5,)),
        ],
        10**10,
    )(*own, density_map)

    pieces, xband, yband = (
        pltpu.with_memory_space_constraint(array, pltpu.HBM) for array in kept
    )

    def corners(at, sub):
        parts = []
        for message in (from_xlow, from_xhigh):
            rim = message[: RAD * ny].reshape(RAD, ny, DEPTH)[:, at : at + RAD]
            subs = message[RAD * ny :].reshape(FIELDS, cols_n, CAP)[:, sub]
            parts += [rim.reshape(RAD * RAD, DEPTH), subs]
        return jnp.concatenate(parts, 0)

    from_clow, from_chigh = neighbours(corners(0, 0), corners(ny - RAD, cols_n - 1))

    messages = (from_xlow, from_xhigh, from_ylow, from_yhigh)
    xband, yband = call(
        sides_kernel,
        sizes,
        bands,
        [smem] + [vmem] * 4 + [hbm] * 2,
        (vmem, vmem),
        [pltpu.VMEM(band.shape, f32) for band in bands] + [pltpu.SemaphoreType.DMA((2,))],
        2 * 10**9,
    )(valid, *messages, xband, yband)

    residual, gradient = call(
        outer_kernel,
        sizes,
        (
            shape((nx, ny, DEPTH), bf16),
            shape((4, rows_n, cols_n, CAP), f32),
        ),
        [smem] + [hbm] * 4 + [vmem] * 8 + [hbm, vmem, hbm],
        (hbm, vmem),
        own_scratch
        + [
            pltpu.VMEM(xband.shape, f32),
            pltpu.VMEM(yband.shape, f32),
            pltpu.VMEM((ex // 2, 2 * ey, 2 * DEPTH), bf16),
            pltpu.VMEM((2, RAD, ny, DEPTH), bf16),
            pltpu.VMEM((2, nx - 2 * RAD, SUB, DEPTH), bf16),
            pltpu.VMEM((3, TILE, CAP), f32),
            pltpu.SemaphoreType.DMA((4,)),
        ],
        10**10,
        {15: 0},
    )(valid, *own, *messages, from_clow, from_chigh, xband, yband, pieces, gradient, residual)
    return residual, gradient


def solution(mesh):
    return jax.shard_map(
        local,
        mesh=mesh,
        in_specs=(
            P(None, "bx", "by", None),
            P("bx", "by", None),
            P("bx", "by", None),
            P("bx", "by"),
            P("bx", "by", None),
        ),
        out_specs=(P("bx", "by", None), P(None, "bx", "by", None)),
        check_vma=False,
    )
```

time: 50.2 us -> 34.3 us (0.68)
  waiting for transfers between devices: 15.6 us -> 0.02 us
  Pallas kernels: 18.9 us -> 23.6 us
  other arithmetic: 3.75 us -> 0.16 us
  local copies, waits for them, and re-layouts: 3.48 us -> 0.08 us
  starting transfers between devices: 7.16 us -> 9.39 us
    ppermute x4 -> x2, waiting for transfers between devices: 15.6 us -> 0.01 us  [shift(): return lax.ppermute(block, axis, route)]
    ppermute x0 -> x4, starting transfers between devices: none -> 7.65 us  [swap(): return lax.ppermute(block, ('bx', 'by'), route)]
    ppermute x4 -> x2, starting transfers between devices: 7.16 us -> 1.75 us  [shift(): return lax.ppermute(block, axis, route)]
    pallas_call x1 -> x4, Pallas kernels: 18.9 us -> 23.6 us  [the longest x1 10.3 us: local(): call(inner_kernel, sizes, (shape((nx, ny, DEPTH), bf16), pltpu.HBM((ex //...]
    mul x4 -> x0, other arithmetic: 2.5 us -> none  [the longest x2 1.3 us: local(): wide = jnp.concatenate([tall_low * valid[2], tall, tall_high * valid[3]], 1)]
    slice x9 -> x6, local copies, waits for them, and re-layouts: 2.56 us -> 0.06 us  [the longest x4 0.05 us: corners(): rim = message[:RAD * ny].reshape(RAD, ny, DEPTH)[:, at:at + RAD]]
    another operation x4 -> x0, local copies, waits for them, and re-layouts: 0.91 us -> none  [the longest x3 0.91 us: local(): jnp.stack([atom_pos[0], atom_pos[1], atom_pos[2], b_factor, weight, zero,...]
    select_n x1 -> x4, other arithmetic: 0.79 us -> 0.08 us  [the longest x2 0.05 us: neighbours(): first = swap(jnp.where(even, high, low), False)]
  transfers between devices with their start and end apart: 4 -> 6, of which waited for: 4 -> 0; matrix products, arithmetic and copies ran while one was open for 2% -> 0% of each run, Pallas kernels for 0% -> 39%
where the time goes in v3:
time: 34.3 us; the launch traced here: 34.1 us
  Pallas kernels  23.6 us (69%)
  starting transfers between devices  9.39 us (27%)
  between operations  0.83 us (2%)
    pallas_call x1, Pallas kernels, local(): call(inner_kernel, sizes, (shape((nx, ny, DEPTH), bf16), pltpu.HBM((ex //...  10.3 us
    pallas_call x1, Pallas kernels, local(): call(outer_kernel, sizes, (shape((nx, ny, DEPTH), bf16), shape((4, rows_n...  9.09 us
    ppermute x4, starting transfers between devices, swap(): return lax.ppermute(block, ('bx', 'by'), route)  7.65 us
    pallas_call x1, Pallas kernels, local(): call(sides_kernel, sizes, bands, [smem] + [vmem] * 4 + [hbm] * 2, (vmem,...  2.87 us
    ppermute x2, starting transfers between devices, shift(): return lax.ppermute(block, axis, route)  1.75 us
    pallas_call x1, Pallas kernels, local(): call(message_kernel, sizes, (shape((xsize, CAP), f32),) * 2 + (shape((ysi...  1.38 us
  transfers between devices with their start and end apart: 6, of which 0 were waited for; matrix products, arithmetic and copies ran while one was open for 0% of the time, Pallas kernels for 39%

profile of v3, /device:TPU:0, one launch (start us, length us, event | category | flops | bytes accessed | tf_op | source)
XLA Modules:
  0.0 34.1 jit_solution(9257536790376494929)
XLA Ops:
  0.6 1.4 %shard_map.68 = (f32[552,128]{1,0:T(8,128)S(1)}, f32[552,128]{1,0:T(8,128)S(1)}, f32[280,128]{1,0:T(8,128)S(1)}, f32[280,128]{1,0:T(8,128)S(1)}) custom-call(s32[4,8]{1,0:T(4,128)} %counts_hbm.5, f32[3,4,8,128]{3,2,1,0:T(8,128)} %pos_hbm.5, f32[4,8,128]{2,1,0:T(8,128)} %bfac_hbm.5, f32[4,8,128]{2,1,0:T(8,128)} %amp_hbm.5, bf16[64,128,128]{2,1,0:T(8,128)(2,1)} %map_hbm.3), custom_call_target="tpu_custom_call" | custom-call | flops 1000000 | bytes 1048576 | tf_op jit(solution)/shard_map/pallas_call | solution.py:476
  2.1 0.5 %collective-permute-start.2 = (f32[280,128]{1,0:T(8,128)S(1)}, f32[280,128]{1,0:T(8,128)S(1)}, u32[]{:S(2)}, u32[]{:S(2)}) collective-permute-start(f32[280,128]{1,0:T(8,128)S(1)} %get-tuple-element.27), channel_id=1, source_target_pairs={{0,8},{1,2},{2,1},{3,4},{4,3},{5,6},{6,5},{7,15},{8,0},{9,10},{10,... | collective-permute-start | bytes 430088 | tf_op jit(solution)/shard_map/ppermute | solution.py:40
  2.6 4.0 %collective-permute-start.3 = (f32[280,128]{1,0:T(8,128)S(1)}, f32[280,128]{1,0:T(8,128)S(1)}, u32[]{:S(2)}, u32[]{:S(2)}) collective-permute-start(f32[280,128]{1,0:T(8,128)S(1)} %get-tuple-element.26), channel_id=1, source_target_pairs={{0,1},{1,0},{2,3},{3,2},{4,5},{5,4},{6,7},{7,6},{8,9},{9,8},{10,11... | collective-permute-start | bytes 430088 | tf_op jit(solution)/shard_map/ppermute | solution.py:40
  6.6 0.0 collective-permute-start
  6.6 1.7 %collective-permute-start.1 = (f32[552,128]{1,0:T(8,128)S(1)}, f32[552,128]{1,0:T(8,128)S(1)}, u32[]{:S(2)}, u32[]{:S(2)}) collective-permute-start(f32[552,128]{1,0:T(8,128)S(1)} %get-tuple-element.14), channel_id=1, source_target_pairs={{0,24},{8,0},{16,8},{24,16},{1,25},{9,1},{17,9},{25,17},{2,26},{10... | collective-permute-start | bytes 847880 | tf_op jit(solution)/shard_map/ppermute | solution.py:28
  8.4 10.3 %shard_map.69 = (bf16[64,128,128]{2,1,0:T(8,128)(2,1)}, bf16[28,240,256]{2,1,0:T(8,128)(2,1)}, f32[2,8,136,128]{3,2,1,0:T(8,128)}, f32[2,56,24,128]{3,2,1,0:T(8,128)}, f32[4,4,8,128]{3,2,1,0:T(8,128)S(1)}) custom-call(s32[4,8]{1,0:T(4,128)} %counts_hbm.5, f32[3,4,8,128]{3,2,1,0:T(8,128)} %pos_hbm.5, f32[4,8,128]{2,1,0:T(8,128)} %bfac_hbm.5, ...), custom_call_target="tpu_custom_call" | custom-call | flops 10000000000 | bytes 1048576 | tf_op jit(solution)/shard_map/pallas_call | solution.py:494
  18.7 0.1 add_convert_fusion.valid_ref
  18.7 0.0 collective-permute-done.2
  18.7 0.0 collective-permute-done.3
  18.8 0.0 collective-permute-done.1.xhigh_ref
  18.8 0.0 collective-permute-done.xlow_ref
  19.0 0.1 collective-permute-start.4
  19.1 3.0 %collective-permute-start.5 = (f32[42,128]{1,0:T(8,128)S(1)}, f32[42,128]{1,0:T(8,128)S(1)}, u32[]{:S(2)}, u32[]{:S(2)}) collective-permute-start(f32[42,128]{1,0:T(8,128)S(1)} %get-tuple-element.34), channel_id=1, source_target_pairs={{0,1},{1,0},{2,3},{3,2},{4,5},{5,4},{6,7},{7,6},{8,9},{9,8},{10,11... | collective-permute-start | bytes 64520 | tf_op jit(solution)/shard_map/ppermute | solution.py:40
  22.1 2.9 %shard_map.70 = (f32[2,8,136,128]{3,2,1,0:T(8,128)S(1)}, f32[2,56,24,128]{3,2,1,0:T(8,128)S(1)}) custom-call(f32[4]{0:T(128)S(1)} %add_convert_fusion.valid_ref, f32[552,128]{1,0:T(8,128)S(1)} %collective-permute-done.xlow_ref, f32[552,128]{1,0:T(8,128)S(1)} %collective-permute-done.1.xhigh_ref, f32[280,128]{1,0:T(8,128)S(1)} %get-tuple-element.25.ylow_ref, ...), custom_call_target="tpu_custom_call" | custom-call | flops 2000000000 | bytes 1048576 | tf_op jit(solution)/shard_map/pallas_call | solution.py:533
  25.0 0.0 collective-permute-done.4
  25.0 0.0 collective-permute-done.5
  25.0 9.1 %shard_map.71 = (bf16[64,128,128]{2,1,0:T(8,128)(2,1)}, f32[4,4,8,128]{3,2,1,0:T(8,128)}) custom-call(f32[4]{0:T(128)S(1)} %add_convert_fusion.valid_ref, s32[4,8]{1,0:T(4,128)} %counts_hbm.5, f32[3,4,8,128]{3,2,1,0:T(8,128)} %pos_hbm.5, f32[4,8,128]{2,1,0:T(8,128)} %bfac_hbm.5, f32[4,8,128]{2,1,0:T(8,128)} %amp_hbm.5, ...), custom_call_target="tpu_custom_call", output_to_operand_aliasing={{0}: (15, {})} | custom-call | flops 10000000000 | bytes 1048576 | tf_op jit(solution)/shard_map/pallas_call | solution.py:543
  (14 shorter events, 0.2 us)
Async XLA Ops:
  2.1 16.7 %collective-permute-start.2 = (f32[280,128]{1,0:T(8,128)S(1)}, f32[280,128]{1,0:T(8,128)S(1)}, u32[]{:S(2)}, u32[]{:S(2)}) collective-permute-start(f32[280,128]{1,0:T(8,128)S(1)} %get-tuple-element.27), channel_id=1, source_target_pairs={{0,8},{1,2},{2,1},{3,4},{4,3},{5,6},{6,5},{7,15},{8,0},{9,10},{10,... | collective-permute-start | bytes 430088 | tf_op jit(solution)/shard_map/ppermute | solution.py:40
  2.6 16.2 %collective-permute-start.3 = (f32[280,128]{1,0:T(8,128)S(1)}, f32[280,128]{1,0:T(8,128)S(1)}, u32[]{:S(2)}, u32[]{:S(2)}) collective-permute-start(f32[280,128]{1,0:T(8,128)S(1)} %get-tuple-element.26), channel_id=1, source_target_pairs={{0,1},{1,0},{2,3},{3,2},{4,5},{5,4},{6,7},{7,6},{8,9},{9,8},{10,11... | collective-permute-start | bytes 430088 | tf_op jit(solution)/shard_map/ppermute | solution.py:40
  6.6 12.2 %collective-permute-start = (f32[552,128]{1,0:T(8,128)S(1)}, f32[552,128]{1,0:T(8,128)S(1)}, u32[]{:S(2)}, u32[]{:S(2)}) collective-permute-start(f32[552,128]{1,0:T(8,128)S(1)} %get-tuple-element.13), channel_id=1, source_target_pairs={{0,8},{8,16},{16,24},{24,0},{1,9},{9,17},{17,25},{25,1},{2,10},{10... | collective-permute-start | bytes 847880 | tf_op jit(solution)/shard_map/ppermute | solution.py:28
  6.6 12.2 %collective-permute-start.1 = (f32[552,128]{1,0:T(8,128)S(1)}, f32[552,128]{1,0:T(8,128)S(1)}, u32[]{:S(2)}, u32[]{:S(2)}) collective-permute-start(f32[552,128]{1,0:T(8,128)S(1)} %get-tuple-element.14), channel_id=1, source_target_pairs={{0,24},{8,0},{16,8},{24,16},{1,25},{9,1},{17,9},{25,17},{2,26},{10... | collective-permute-start | bytes 847880 | tf_op jit(solution)/shard_map/ppermute | solution.py:28
  19.0 6.0 %collective-permute-start.4 = (f32[42,128]{1,0:T(8,128)S(1)}, f32[42,128]{1,0:T(8,128)S(1)}, u32[]{:S(2)}, u32[]{:S(2)}) collective-permute-start(f32[42,128]{1,0:T(8,128)S(1)} %get-tuple-element.35), channel_id=1, source_target_pairs={{0,8},{1,2},{2,1},{3,4},{4,3},{5,6},{6,5},{7,15},{8,0},{9,10},{10,... | collective-permute-start | bytes 64520 | tf_op jit(solution)/shard_map/ppermute | solution.py:40
  19.1 5.9 %collective-permute-start.5 = (f32[42,128]{1,0:T(8,128)S(1)}, f32[42,128]{1,0:T(8,128)S(1)}, u32[]{:S(2)}, u32[]{:S(2)}) collective-permute-start(f32[42,128]{1,0:T(8,128)S(1)} %get-tuple-element.34), channel_id=1, source_target_pairs={{0,1},{1,0},{2,3},{3,2},{4,5},{5,4},{6,7},{7,6},{8,9},{9,8},{10,11... | collective-permute-start | bytes 64520 | tf_op jit(solution)/shard_map/ppermute | solution.py:40

commit v4 on v3

--- a/solution.py
+++ b/solution.py
@@ -40,11 +40,33 @@
     return lax.ppermute(block, ("bx", "by"), route)
 
 
-def neighbours(low, high):
-    even = lax.axis_index("by") % 2 == 0
-    first = swap(jnp.where(even, high, low), False)
-    second = swap(jnp.where(even, low, high), True)
-    return jnp.where(even, second, first), jnp.where(even, first, second)
+def is_even():
+    return lax.axis_index("by") % 2 == 0
+
+
+def valid_sides():
+    found = []
+    for axis in ("bx", "by"):
+        at = lax.axis_index(axis)
+        found += [at > 0, at < lax.axis_size(axis) - 1]
+    return [jnp.where(side, 1.0, 0.0) for side in found]
+
+
+class Picked:
+    def __init__(self, flag, when_true, when_false, start=0):
+        self.flag, self.refs, self.start = flag, (when_true, when_false), start
+
+    def rows(self, at, count):
+        where = pl.ds(self.start + at, count)
+        return jnp.where(self.flag, self.refs[0][where, :], self.refs[1][where, :])
+
+
+class Plain:
+    def __init__(self, ref):
+        self.ref = ref
+
+    def rows(self, at, count):
+        return self.ref[pl.ds(at, count), :]
 
 
 def split(value):
@@ -97,14 +119,12 @@
     return jnp.where(slot < count, amplitude, 0.0)
 
 
-def own_atom(counts_ref, pos_ref, bfac_ref, amp_ref, a, b):
-    row = pl.ds(b, 1)
-    found = terms(*(pos_ref[k, a, row, :] for k in range(3)), bfac_ref[a, row, :])
-    return found + (masked(amp_ref[a, row, :], counts_ref[a, b]),)
+def own_atom(terms_ref, index):
+    return tuple(terms_ref[index, k : k + 1, :] for k in range(FIELDS))
 
 
 def sent_atom(message, start, stride, index, valid):
-    row = [message[pl.ds(start + k * stride + index, 1), :] for k in range(FIELDS)]
+    row = [message.rows(start + k * stride + index, 1) for k in range(FIELDS)]
     return terms(*row[:4]) + (row[4] * valid,)
 
 
@@ -184,7 +204,7 @@
 def message_kernel(
     rows_n, cols_n,
     counts_hbm, pos_hbm, bfac_hbm, amp_hbm, map_hbm,
-    xlow_ref, xhigh_ref, ylow_ref, yhigh_ref,
+    xlow_ref, xhigh_ref, first_ref, second_ref, terms_ref,
     counts_ref, pos_ref, bfac_ref, amp_ref, own_sems,
     xrim, yrim, sems,
 ):
@@ -201,42 +221,60 @@
     for copy in copies:
         copy.start()
 
+    def fields(a, b):
+        found = [pos_ref[k, a, b : b + 1, :] for k in range(3)] + [bfac_ref[a, b : b + 1, :]]
+        return found + [masked(amp_ref[a, b : b + 1, :], counts_ref[a, b])]
+
     def atoms(out, start, stride, index, a, b):
-        fields = [pos_ref[k, a, b : b + 1, :] for k in range(3)] + [bfac_ref[a, b : b + 1, :]]
-        fields.append(masked(amp_ref[a, b : b + 1, :], counts_ref[a, b]))
-        for k, value in enumerate(fields):
+        for k, value in enumerate(fields(a, b)):
             out[start + k * stride + index : start + k * stride + index + 1, :] = value
 
     finish(fetched)
+    for a in range(rows_n):
+        found = terms(pos_ref[0, a], pos_ref[1, a], pos_ref[2, a], bfac_ref[a])
+        for b in range(cols_n):
+            row = slice(b, b + 1)
+            weight = masked(amp_ref[a, row, :], counts_ref[a, b])
+            terms_ref[a * cols_n + b, 0:FIELDS, :] = jnp.concatenate(
+                [value[row] for value in found] + [weight], 0
+            )
     for b in range(cols_n):
         atoms(xlow_ref, RAD * ny, cols_n, b, 0, b)
         atoms(xhigh_ref, RAD * ny, cols_n, b, rows_n - 1, b)
-    for out in (ylow_ref, yhigh_ref):
+    even = is_even()
+
+    def put(where, low, high):
+        first_ref[where, :] = jnp.where(even, high, low)
+        second_ref[where, :] = jnp.where(even, low, high)
+
+    for out in (first_ref, second_ref):
         out[nx * RAD :, :] = jnp.zeros((BAND, CAP), jnp.float32)
     for a in range(rows_n):
-        atoms(ylow_ref, RAD * nx, rows_n, a, a, 0)
-        atoms(yhigh_ref, RAD * nx, rows_n, a, a, cols_n - 1)
+        low, high = fields(a, 0), fields(a, cols_n - 1)
+        for k in range(FIELDS):
+            at = RAD * nx + k * rows_n + a
+            put(slice(at, at + 1), low[k], high[k])
     for copy in copies:
         copy.wait()
     for k, out in enumerate((xlow_ref, xhigh_ref)):
         for i in range(RAD):
             out[ny * i : ny * (i + 1), :] = xrim[k, i].astype(jnp.float32)
     for i in range(nx):
-        ylow_ref[RAD * i : RAD * (i + 1), :] = yrim[0, i].astype(jnp.float32)[:RAD]
-        yhigh_ref[RAD * i : RAD * (i + 1), :] = yrim[1, i].astype(jnp.float32)[SUB - RAD :]
+        put(
+            slice(RAD * i, RAD * (i + 1)),
+            yrim[0, i].astype(jnp.float32)[:RAD],
+            yrim[1, i].astype(jnp.float32)[SUB - RAD :],
+        )
 
 
 def inner_kernel(
     rows_n, cols_n,
-    counts_hbm, pos_hbm, bfac_hbm, amp_hbm, map_hbm,
-    out_hbm, pieces_hbm, xband_hbm, yband_hbm, grad_ref,
-    counts_ref, pos_ref, bfac_ref, amp_ref, own_sems,
-    field, pieces, map_v, out_v, prof_x, in_sem, out_sems,
+    terms_ref, map_hbm,
+    out_hbm, pieces, xband, yband, grad_ref,
+    field, map_v, out_v, prof_x, in_sem, out_sems,
 ):
     nx, ny = rows_n * SUB, cols_n * SUB
     ex, ey = nx + 2 * RAD, ny + 2 * RAD
-    held = (counts_ref, pos_ref, bfac_ref, amp_ref)
-    fetched = fetch(zip((counts_hbm, pos_hbm, bfac_hbm, amp_hbm), held), own_sems)
     load = pltpu.make_async_copy(map_hbm, map_v, in_sem)
     load.start()
 
@@ -245,13 +283,11 @@
         return 0
 
     lax.fori_loop(0, ex, clear, 0)
-    finish(fetched)
-    atom_at = functools.partial(own_atom, counts_ref, pos_ref, bfac_ref, amp_ref)
 
     def own(i, _):
         a, b = i // cols_n, i % cols_n
         y0 = pl.multiple_of(SUB * b, SUB)
-        for p, row in enumerate(rendered(atom_at(a, b), 0, TILE, 0, 3)):
+        for p, row in enumerate(rendered(own_atom(terms_ref, i), 0, TILE, 0, 3)):
             field[SUB * a + p, pl.ds(y0, TILE), :] += row
         return 0
 
@@ -268,8 +304,8 @@
     rest = pl.ds(2 * RAD, nx - 2 * RAD)
     pairs = [(out_v, out_hbm)]
     for k in range(2):
-        pairs.append((field.at[pl.ds((ex - 2 * RAD) * k, 2 * RAD)], xband_hbm.at[k]))
-        pairs.append((field.at[rest, pl.ds((ey - BAND) * k, BAND)], yband_hbm.at[k]))
+        pairs.append((field.at[pl.ds((ex - 2 * RAD) * k, 2 * RAD)], xband.at[k]))
+        pairs.append((field.at[rest, pl.ds((ey - BAND) * k, BAND)], yband.at[k]))
     stores = fetch(pairs, out_sems)
 
     def pack(i, _):
@@ -279,44 +315,52 @@
         return 0
 
     lax.fori_loop(RAD, ex // 2 - RAD, pack, 0, unroll=2)
-    kept = (pl.ds(RAD, ex // 2 - 2 * RAD), pl.ds(SUB, 2 * ey - 2 * SUB))
-    last = pltpu.make_async_copy(pieces.at[kept], pieces_hbm, in_sem)
-    last.start()
-
     def gradient(i, _):
         a, b = i // (cols_n - 2) + 1, i % (cols_n - 2) + 1
-        tile_gradient(atom_at(a, b), pieces, prof_x, grad_ref, a, b)
+        tile_gradient(own_atom(terms_ref, a * cols_n + b), pieces, prof_x, grad_ref, a, b)
         return 0
 
     lax.fori_loop(0, (rows_n - 2) * (cols_n - 2), gradient, 0, unroll=6)
     finish(stores)
-    last.wait()
+
+
+def corner_kernel(rows_n, cols_n, xlow_ref, xhigh_ref, out_ref):
+    ny = cols_n * SUB
+    at = 0
+    for y0, sub in ((0, 0), (ny - RAD, cols_n - 1)):
+        for message in (xlow_ref, xhigh_ref):
+            for i in range(RAD):
+                out_ref[at : at + RAD, :] = message[ny * i + y0 : ny * i + y0 + RAD, :]
+                at += RAD
+            for k in range(FIELDS):
+                row = RAD * ny + k * cols_n + sub
+                out_ref[at : at + 1, :] = message[row : row + 1, :]
+                at += 1
+    out_ref[at:, :] = jnp.zeros((out_ref.shape[0] - at, CAP), jnp.float32)
 
 
 def sides_kernel(
     rows_n, cols_n,
-    valid_ref, xlow_ref, xhigh_ref, ylow_ref, yhigh_ref, xband_hbm, yband_hbm,
+    xlow_ref, xhigh_ref, first_ref, second_ref, xband_in, yband_in,
     xband, yband,
-    xfield, yfield, sems,
 ):
     nx, ny = rows_n * SUB, cols_n * SUB
     ex, ey = nx + 2 * RAD, ny + 2 * RAD
-    fetched = fetch(((xband_hbm, xfield), (yband_hbm, yfield)), sems)
-    xband[...] = jnp.zeros_like(xband)
-    yband[...] = jnp.zeros_like(yband)
+    even, valid = is_even(), valid_sides()
+    ylow, yhigh = Picked(even, second_ref, first_ref), Picked(even, first_ref, second_ref)
 
     def x_side(b, _):
         y0 = pl.multiple_of(SUB * b, SUB)
-        for k, (message, p0) in enumerate(((xlow_ref, SUB), (xhigh_ref, 0))):
-            atom = sent_atom(message, RAD * ny, cols_n, b, valid_ref[k])
+        for k, (message, p0) in enumerate(((Plain(xlow_ref), SUB), (Plain(xhigh_ref), 0))):
+            atom = sent_atom(message, RAD * ny, cols_n, b, valid[k])
             for p, row in enumerate(rendered(atom, p0, 2 * RAD, 0, 3)):
                 xband[k, p, pl.ds(y0, TILE), :] += row
         return 0
 
     lax.fori_loop(0, cols_n, x_side, 0, unroll=4)
     for a in range(rows_n):
-        for k, (message, j0, y0) in enumerate(((ylow_ref, 2, 0), (yhigh_ref, 0, ey - 8))):
-            atom = sent_atom(message, RAD * nx, rows_n, a, valid_ref[2 + k])
+        for k, (message, j0, y0) in enumerate(((ylow, 2, 0), (yhigh, 0, ey - 8))):
+            atom = sent_atom(message, RAD * nx, rows_n, a, valid[2 + k])
             for p, row in enumerate(rendered(atom, 0, TILE, j0, 1)):
                 x = SUB * a + p
                 if x < 2 * RAD:
@@ -325,33 +369,26 @@
                     xband[1, x - (ex - 2 * RAD), y0 : y0 + 8, :] += row
                 else:
                     yband[k, x - 2 * RAD, (BAND - 8) * k : (BAND - 8) * k + 8, :] += row
-    finish(fetched)
-    xband[...] += xfield[...]
-    yband[...] += yfield[...]
 
 
 def outer_kernel(
     rows_n, cols_n,
-    valid_ref, counts_hbm, pos_hbm, bfac_hbm, amp_hbm,
-    xlow_ref, xhigh_ref, ylow_ref, yhigh_ref, clow_ref, chigh_ref,
-    xband_in, yband_in, pieces_hbm, grad_in, out_in,
-    out_hbm, grad_ref,
-    counts_ref, pos_ref, bfac_ref, amp_ref, own_sems,
-    xband, yband, pieces, xout, yout, prof_x, sems,
+    terms_ref, xlow_ref, xhigh_ref, first_ref, second_ref, cfirst_ref, csecond_ref,
+    xband_in, yband_in, pieces_in, grad_in, out_in,
+    out_hbm, grad_ref, xband, yband, pieces,
+    xout, yout, prof_x, sems,
 ):
     nx, ny = rows_n * SUB, cols_n * SUB
     ex, ey = nx + 2 * RAD, ny + 2 * RAD
-    kept = (pl.ds(RAD, ex // 2 - 2 * RAD), pl.ds(SUB, 2 * ey - 2 * SUB))
-    held = (counts_ref, pos_ref, bfac_ref, amp_ref, pieces.at[kept])
-    sources = (counts_hbm, pos_hbm, bfac_hbm, amp_hbm, pieces_hbm)
-    fetched = fetch(zip(sources, held), own_sems)
-    xband[...] = xband_in[...]
-    yband[...] = yband_in[...]
     grad_ref[...] = grad_in[...]
     corner = RAD * RAD + FIELDS
-    for ky, (message, j0, y0) in enumerate(((clow_ref, 2, 0), (chigh_ref, 0, ey - 8))):
+    even, valid = is_even(), valid_sides()
+    ylow, yhigh = Picked(even, second_ref, first_ref), Picked(even, first_ref, second_ref)
+    clow = Picked(even, csecond_ref, cfirst_ref, 2 * corner)
+    chigh = Picked(even, cfirst_ref, csecond_ref)
+    for ky, (message, j0, y0) in enumerate(((clow, 2, 0), (chigh, 0, ey - 8))):
         for kx, p0 in enumerate((SUB, 0)):
-            ok = valid_ref[kx] * valid_ref[2 + ky]
+            ok = valid[kx] * valid[2 + ky]
             atom = sent_atom(message, corner * kx + RAD * RAD, 1, 0, ok)
             for p, row in enumerate(rendered(atom, p0, 2 * RAD, j0, 1)):
                 xband[kx, p, y0 : y0 + 8, :] += row
@@ -359,25 +396,25 @@
         for i in range(RAD):
             row = RAD * kx + i
             xband[kx, row, RAD : RAD + ny, :] -= message[ny * i : ny * (i + 1), :]
-            for ky, sent in enumerate((clow_ref, chigh_ref)):
+            for ky, sent in enumerate((clow, chigh)):
                 y0 = (ey - RAD) * ky
                 at = corner * kx + RAD * i
-                xband[kx, row, y0 : y0 + RAD, :] -= sent[at : at + RAD, :]
-            xband[kx, row] = valid_ref[kx] * xband[kx, row]
-    for ky, message in enumerate((ylow_ref, yhigh_ref)):
+                xband[kx, row, y0 : y0 + RAD, :] -= sent.rows(at, RAD)
+            xband[kx, row] = valid[kx] * xband[kx, row]
+    for ky, message in enumerate((ylow, yhigh)):
         y0 = (ey - RAD) * ky
         for kx in range(2):
             for i in range(RAD):
                 row = RAD * (1 - kx) + i
                 at = RAD * ((nx - RAD) * kx + i)
-                xband[kx, row, y0 : y0 + RAD, :] -= message[at : at + RAD, :]
+                xband[kx, row, y0 : y0 + RAD, :] -= message.rows(at, RAD)
             for i in range(2 * RAD):
-                xband[kx, i, y0 : y0 + RAD, :] = valid_ref[2 + ky] * xband[kx, i, y0 : y0 + RAD, :]
+                xband[kx, i, y0 : y0 + RAD, :] = valid[2 + ky] * xband[kx, i, y0 : y0 + RAD, :]
         y0 = (BAND - RAD) * ky
         for i in range(nx - 2 * RAD):
             at = RAD * (RAD + i)
-            inside = yband[ky, i, y0 : y0 + RAD, :] - message[at : at + RAD, :]
-            yband[ky, i, y0 : y0 + RAD, :] = valid_ref[2 + ky] * inside
+            inside = yband[ky, i, y0 : y0 + RAD, :] - message.rows(at, RAD)
+            yband[ky, i, y0 : y0 + RAD, :] = valid[2 + ky] * inside
 
     stores = []
     for kx in range(2):
@@ -414,17 +451,15 @@
             pieces[RAD + i, at : at + 16, :] = packed(
                 yband[ky, 2 * i, rows, :], yband[ky, 2 * i + 1, rows, :]
             )
-    atom_at = functools.partial(own_atom, counts_ref, pos_ref, bfac_ref, amp_ref)
-    finish(fetched)
 
     def x_edges(i, _):
         a, b = (i // cols_n) * (rows_n - 1), i % cols_n
-        tile_gradient(atom_at(a, b), pieces, prof_x, grad_ref, a, b)
+        tile_gradient(own_atom(terms_ref, a * cols_n + b), pieces, prof_x, grad_ref, a, b)
         return 0
 
     def y_edges(i, _):
         a, b = i // 2 + 1, (i % 2) * (cols_n - 1)
-        tile_gradient(atom_at(a, b), pieces, prof_x, grad_ref, a, b)
+        tile_gradient(own_atom(terms_ref, a * cols_n + b), pieces, prof_x, grad_ref, a, b)
         return 0
 
     lax.fori_loop(0, 2 * cols_n, x_edges, 0, unroll=8)
@@ -450,15 +485,11 @@
     sizes = rows_n, cols_n = counts.shape
     nx, ny = rows_n * SUB, cols_n * SUB
     ex, ey = nx + 2 * RAD, ny + 2 * RAD
-    ix, iy = lax.axis_index("bx"), lax.axis_index("by")
-    valid = jnp.stack(
-        [ix > 0, ix < lax.axis_size("bx") - 1, iy > 0, iy < lax.axis_size("by") - 1]
-    ).astype(jnp.float32)
     f32, bf16 = jnp.float32, jnp.bfloat16
     shape = jax.ShapeDtypeStruct
     vmem = pl.BlockSpec(memory_space=pltpu.VMEM)
-    smem = pl.BlockSpec(memory_space=pltpu.SMEM)
     hbm = pl.BlockSpec(memory_space=pltpu.HBM)
+    pin = functools.partial(pltpu.with_memory_space_constraint, memory_space=pltpu.VMEM)
     own_scratch = [
         pltpu.SMEM(counts.shape, jnp.int32),
         pltpu.VMEM(atom_pos.shape, f32),
@@ -473,12 +504,14 @@
     density_map = pltpu.with_memory_space_constraint(density_map, pltpu.HBM)
 
     xsize, ysize = RAD * ny + FIELDS * cols_n, RAD * nx + BAND
-    xlow, xhigh, ylow, yhigh = call(
+    xlow, xhigh, first, second, found = call(
         message_kernel,
         sizes,
-        (shape((xsize, CAP), f32),) * 2 + (shape((ysize, CAP), f32),) * 2,
+        (shape((xsize, CAP), f32),) * 2
+        + (shape((ysize, CAP), f32),) * 2
+        + (pltpu.VMEM((rows_n * cols_n, 8, CAP), f32),),
         [hbm] * 5,
-        (vmem,) * 4,
+        (vmem,) * 5,
         own_scratch
         + [
             pltpu.VMEM((2, RAD, ny, DEPTH), bf16),
@@ -487,25 +520,27 @@
         ],
         10**6,
     )(*own, density_map)
-    from_ylow, from_yhigh = neighbours(ylow, yhigh)
+    from_first, from_second = swap(first, False), swap(second, True)
     from_xlow, from_xhigh = shift(xhigh, "bx", 1), shift(xlow, "bx", -1)
 
-    bands = shape((2, 2 * RAD, ey, DEPTH), f32), shape((2, nx - 2 * RAD, BAND, DEPTH), f32)
+    bands = (
+        pltpu.VMEM((2, 2 * RAD, ey, DEPTH), f32),
+        pltpu.VMEM((2, nx - 2 * RAD, BAND, DEPTH), f32),
+    )
+    pieces = pltpu.VMEM((ex // 2, 2 * ey, 2 * DEPTH), bf16)
     residual, *kept, gradient = call(
         inner_kernel,
         sizes,
         (
             shape((nx, ny, DEPTH), bf16),
-            pltpu.HBM((ex // 2 - 2 * RAD, 2 * ey - 2 * SUB, 2 * DEPTH), bf16),
-            *(pltpu.HBM(band.shape, f32) for band in bands),
+            pieces,
+            *bands,
             shape((4, rows_n, cols_n, CAP), f32),
         ),
-        [hbm] * 5,
-        (hbm, hbm, hbm, hbm, vmem),
-        own_scratch
-        + [
+        [vmem, hbm],
+        (hbm, vmem, vmem, vmem, vmem),
+        [
             pltpu.VMEM((ex, ey, DEPTH), f32),
-            pltpu.VMEM((ex // 2, 2 * ey, 2 * DEPTH), bf16),
             pltpu.VMEM((nx, ny, DEPTH), bf16),
             pltpu.VMEM((nx, ny, DEPTH), bf16),
             pltpu.VMEM((3, TILE, CAP), f32),
@@ -513,55 +548,55 @@
             pltpu.SemaphoreType.DMA((5,)),
         ],
         10**10,
-    )(*own, density_map)
-
-    pieces, xband, yband = (
-        pltpu.with_memory_space_constraint(array, pltpu.HBM) for array in kept
-    )
-
-    def corners(at, sub):
-        parts = []
-        for message in (from_xlow, from_xhigh):
-            rim = message[: RAD * ny].reshape(RAD, ny, DEPTH)[:, at : at + RAD]
-            subs = message[RAD * ny :].reshape(FIELDS, cols_n, CAP)[:, sub]
-            parts += [rim.reshape(RAD * RAD, DEPTH), subs]
-        return jnp.concatenate(parts, 0)
-
-    from_clow, from_chigh = neighbours(corners(0, 0), corners(ny - RAD, cols_n - 1))
-
-    messages = (from_xlow, from_xhigh, from_ylow, from_yhigh)
+    )(pin(found), density_map)
+    kept_pieces, xband, yband = kept
+
+    corners = call(
+        corner_kernel,
+        sizes,
+        shape((4 * (RAD * RAD + FIELDS) + 4, CAP), f32),
+        [vmem, vmem],
+        vmem,
+        [],
+        10**5,
+    )(from_xlow, from_xhigh)
+    from_corners = swap(corners, False), swap(corners, True)
+
+    messages = (from_xlow, from_xhigh, from_first, from_second)
     xband, yband = call(
         sides_kernel,
         sizes,
         bands,
-        [smem] + [vmem] * 4 + [hbm] * 2,
+        [vmem] * 6,
         (vmem, vmem),
-        [pltpu.VMEM(band.shape, f32) for band in bands] + [pltpu.SemaphoreType.DMA((2,))],
+        [],
         2 * 10**9,
-    )(valid, *messages, xband, yband)
-
-    residual, gradient = call(
+        {4: 0, 5: 1},
+    )(*messages, pin(xband), pin(yband))
+
+    residual, gradient, *_ = call(
         outer_kernel,
         sizes,
         (
             shape((nx, ny, DEPTH), bf16),
             shape((4, rows_n, cols_n, CAP), f32),
+            *bands,
+            pieces,
         ),
-        [smem] + [hbm] * 4 + [vmem] * 8 + [hbm, vmem, hbm],
-        (hbm, vmem),
-        own_scratch
-        + [
-            pltpu.VMEM(xband.shape, f32),
-            pltpu.VMEM(yband.shape, f32),
-            pltpu.VMEM((ex // 2, 2 * ey, 2 * DEPTH), bf16),
+        [vmem] * 11 + [hbm],
+        (hbm, vmem, vmem, vmem, vmem),
+        [
             pltpu.VMEM((2, RAD, ny, DEPTH), bf16),
             pltpu.VMEM((2, nx - 2 * RAD, SUB, DEPTH), bf16),
             pltpu.VMEM((3, TILE, CAP), f32),
             pltpu.SemaphoreType.DMA((4,)),
         ],
         10**10,
-        {15: 0},
-    )(valid, *own, *messages, from_clow, from_chigh, xband, yband, pieces, gradient, residual)
+        {11: 0, 7: 2, 8: 3, 9: 4},
+    )(
+        pin(found), *messages, *from_corners,
+        pin(xband), pin(yband), pin(kept_pieces), gradient, residual,
+    )
     return residual, gradient
 
 

time: 34.3 us -> 29.7 us (0.87); the launches traced: 34.1 us -> 29.1 us
  Pallas kernels: 23.6 us -> 20.4 us
  starting transfers between devices: 9.39 us -> 7.95 us
    pallas_call x1, Pallas kernels: 9.09 us -> 6.98 us  [local(): call(outer_kernel, sizes, (shape((nx, ny, DEPTH), bf16), shape((4, rows_n...]
    ppermute x4, starting transfers between devices: 7.65 us -> 6.21 us  [swap(): return lax.ppermute(block, ('bx', 'by'), route)]
    pallas_call x2 -> x3, Pallas kernels: 13.1 us -> 12 us  [the longest x1 10.1 us: local(): call(inner_kernel, sizes, (shape((nx, ny, DEPTH), bf16), pieces, *bands,...]
  transfers between devices with their start and end apart: 6 -> 6, of which waited for: 0 -> 1; matrix products, arithmetic and copies ran while one was open for 0% -> 0% of each run, Pallas kernels for 39% -> 41%
where the time goes in v4:
time: 29.7 us; the launch traced here: 29.1 us
  Pallas kernels  20.4 us (69%)
  starting transfers between devices  7.95 us (27%)
  between operations  0.7 us (2%)
    pallas_call x1, Pallas kernels, local(): call(inner_kernel, sizes, (shape((nx, ny, DEPTH), bf16), pieces, *bands,...  10.1 us
    pallas_call x1, Pallas kernels, local(): call(outer_kernel, sizes, (shape((nx, ny, DEPTH), bf16), shape((4, rows_n...  6.98 us
    ppermute x4, starting transfers between devices, swap(): return lax.ppermute(block, ('bx', 'by'), route)  6.21 us
    pallas_call x1, Pallas kernels, local(): call(sides_kernel, sizes, bands, [vmem] * 6, (vmem, vmem), [], 2 * 10 **...  1.93 us
    ppermute x2, starting transfers between devices, shift(): return lax.ppermute(block, axis, route)  1.75 us
    pallas_call x1, Pallas kernels, local(): call(message_kernel, sizes, (shape((xsize, CAP), f32),) * 2 + (shape((ysi...  1.39 us
  transfers between devices with their start and end apart: 6, of which 1 were waited for; matrix products, arithmetic and copies ran while one was open for 0% of the time, Pallas kernels for 41%

profile of v4, /device:TPU:0, one launch (start us, length us, event | category | flops | bytes accessed | tf_op | source)
XLA Modules:
  0.0 29.1 jit_solution(15495671156409722487)
XLA Ops:
  0.6 1.4 %shard_map.68 = (f32[552,128]{1,0:T(8,128)S(1)}, f32[552,128]{1,0:T(8,128)S(1)}, f32[280,128]{1,0:T(8,128)S(1)}, f32[280,128]{1,0:T(8,128)S(1)}, f32[32,8,128]{2,1,0:T(8,128)S(1)}) custom-call(s32[4,8]{1,0:T(4,128)} %counts_hbm.1, f32[3,4,8,128]{3,2,1,0:T(8,128)} %pos_hbm.1, f32[4,8,128]{2,1,0:T(8,128)} %bfac_hbm.1, f32[4,8,128]{2,1,0:T(8,128)} %amp_hbm.1, ...), custom_call_target="tpu_custom_call" | custom-call | flops 1000000 | bytes 1048576 | tf_op jit(solution)/shard_map/pallas_call | solution.py:507
  2.0 3.0 %collective-permute-start.2 = (f32[280,128]{1,0:T(8,128)S(1)}, f32[280,128]{1,0:T(8,128)S(1)}, u32[]{:S(2)}, u32[]{:S(2)}) collective-permute-start(f32[280,128]{1,0:T(8,128)S(1)} %get-tuple-element.19), channel_id=1, source_target_pairs={{0,1},{1,0},{2,3},{3,2},{4,5},{5,4},{6,7},{7,6},{8,9},{9,8},{10,11... | collective-permute-start | bytes 430088 | tf_op jit(solution)/shard_map/ppermute | solution.py:40
  5.1 0.0 collective-permute-start.3
  5.1 0.5 %collective-permute-start = (f32[552,128]{1,0:T(8,128)S(1)}, f32[552,128]{1,0:T(8,128)S(1)}, u32[]{:S(2)}, u32[]{:S(2)}) collective-permute-start(f32[552,128]{1,0:T(8,128)S(1)} %get-tuple-element.17), channel_id=1, source_target_pairs={{0,8},{8,16},{16,24},{24,0},{1,9},{9,17},{17,25},{25,1},{2,10},{10... | collective-permute-start | bytes 847880 | tf_op jit(solution)/shard_map/ppermute | solution.py:28
  5.6 1.2 %collective-permute-start.1 = (f32[552,128]{1,0:T(8,128)S(1)}, f32[552,128]{1,0:T(8,128)S(1)}, u32[]{:S(2)}, u32[]{:S(2)}) collective-permute-start(f32[552,128]{1,0:T(8,128)S(1)} %get-tuple-element.18), channel_id=1, source_target_pairs={{0,24},{8,0},{16,8},{24,16},{1,25},{9,1},{17,9},{25,17},{2,26},{10... | collective-permute-start | bytes 847880 | tf_op jit(solution)/shard_map/ppermute | solution.py:28
  6.8 10.1 %shard_map.70 = (bf16[64,128,128]{2,1,0:T(8,128)(2,1)}, bf16[36,272,256]{2,1,0:T(8,128)(2,1)S(1)}, f32[2,8,136,128]{3,2,1,0:T(8,128)S(1)}, f32[2,56,24,128]{3,2,1,0:T(8,128)S(1)}, f32[4,4,8,128]{3,2,1,0:T(8,128)S(1)}) custom-call(f32[32,8,128]{2,1,0:T(8,128)S(1)} %get-tuple-element.16.terms_ref, bf16[64,128,128]{2,1,0:T(8,128)(2,1)} %map_hbm.3), custom_call_target="tpu_custom_call" | custom-call | flops 10000000000 | bytes 1048576 | tf_op jit(solution)/shard_map/pallas_call | solution.py:531
  16.9 0.0 collective-permute-done.xlow_ref
  16.9 0.0 collective-permute-done.1.xhigh_ref
  16.9 0.1 collective-permute-start.5
  17.0 3.1 %collective-permute-start.4 = (f32[88,128]{1,0:T(8,128)S(1)}, f32[88,128]{1,0:T(8,128)S(1)}, u32[]{:S(2)}, u32[]{:S(2)}) collective-permute-start(f32[88,128]{1,0:T(8,128)S(1)} %shard_map.69), channel_id=1, source_target_pairs={{0,1},{1,0},{2,3},{3,2},{4,5},{5,4},{6,7},{7,6},{8,9},{9,8},{10,11... | collective-permute-start | bytes 135176 | tf_op jit(solution)/shard_map/ppermute | solution.py:40
  20.1 0.0 collective-permute-done.2.first_ref
  20.1 0.0 collective-permute-done.3.second_ref
  20.1 1.9 %shard_map.71 = (f32[2,8,136,128]{3,2,1,0:T(8,128)S(1)}, f32[2,56,24,128]{3,2,1,0:T(8,128)S(1)}) custom-call(f32[552,128]{1,0:T(8,128)S(1)} %collective-permute-done.xlow_ref, f32[552,128]{1,0:T(8,128)S(1)} %collective-permute-done.1.xhigh_ref, f32[280,128]{1,0:T(8,128)S(1)} %collective-permute-done.2.first_ref, ...), custom_call_target="tpu_custom_call", output_to_operand_aliasing={{0}: (4, {}), {1}: (5, {})} | custom-call | flops 2000000000 | bytes 1048576 | tf_op jit(solution)/shard_map/pallas_call | solution.py:566
  22.0 0.0 collective-permute-done.5.csecond_ref
  22.1 0.1 collective-permute-done.4.cfirst_ref
  22.1 7.0 %shard_map.72 = (bf16[64,128,128]{2,1,0:T(8,128)(2,1)}, f32[4,4,8,128]{3,2,1,0:T(8,128)}, f32[2,8,136,128]{3,2,1,0:T(8,128)S(1)}, f32[2,56,24,128]{3,2,1,0:T(8,128)S(1)}, bf16[36,272,256]{2,1,0:T(8,128)(2,1)S(1)}) custom-call(f32[32,8,128]{2,1,0:T(8,128)S(1)} %get-tuple-element.16.terms_ref,, ...), custom_call_target="tpu_custom_call", output_to_operand_aliasing={{0}: (11, {}), {2}: (7, {}), {3}: (8, {}), {4}: (9, {})} | custom-call | flops 10000000000 | bytes 1048576 | tf_op jit(solution)/shard_map/pallas_call | solution.py:577
  (1 shorter events, 0.0 us)
Async XLA Ops:
  2.0 18.1 %collective-permute-start.2 = (f32[280,128]{1,0:T(8,128)S(1)}, f32[280,128]{1,0:T(8,128)S(1)}, u32[]{:S(2)}, u32[]{:S(2)}) collective-permute-start(f32[280,128]{1,0:T(8,128)S(1)} %get-tuple-element.19), channel_id=1, source_target_pairs={{0,1},{1,0},{2,3},{3,2},{4,5},{5,4},{6,7},{7,6},{8,9},{9,8},{10,11... | collective-permute-start | bytes 430088 | tf_op jit(solution)/shard_map/ppermute | solution.py:40
  5.1 15.0 %collective-permute-start.3 = (f32[280,128]{1,0:T(8,128)S(1)}, f32[280,128]{1,0:T(8,128)S(1)}, u32[]{:S(2)}, u32[]{:S(2)}) collective-permute-start(f32[280,128]{1,0:T(8,128)S(1)} %get-tuple-element.20), channel_id=1, source_target_pairs={{0,8},{1,2},{2,1},{3,4},{4,3},{5,6},{6,5},{7,15},{8,0},{9,10},{10,... | collective-permute-start | bytes 430088 | tf_op jit(solution)/shard_map/ppermute | solution.py:40
  5.1 11.8 %collective-permute-start = (f32[552,128]{1,0:T(8,128)S(1)}, f32[552,128]{1,0:T(8,128)S(1)}, u32[]{:S(2)}, u32[]{:S(2)}) collective-permute-start(f32[552,128]{1,0:T(8,128)S(1)} %get-tuple-element.17), channel_id=1, source_target_pairs={{0,8},{8,16},{16,24},{24,0},{1,9},{9,17},{17,25},{25,1},{2,10},{10... | collective-permute-start | bytes 847880 | tf_op jit(solution)/shard_map/ppermute | solution.py:28
  5.6 11.3 %collective-permute-start.1 = (f32[552,128]{1,0:T(8,128)S(1)}, f32[552,128]{1,0:T(8,128)S(1)}, u32[]{:S(2)}, u32[]{:S(2)}) collective-permute-start(f32[552,128]{1,0:T(8,128)S(1)} %get-tuple-element.18), channel_id=1, source_target_pairs={{0,24},{8,0},{16,8},{24,16},{1,25},{9,1},{17,9},{25,17},{2,26},{10... | collective-permute-start | bytes 847880 | tf_op jit(solution)/shard_map/ppermute | solution.py:28
  16.9 5.1 %collective-permute-start.5 = (f32[88,128]{1,0:T(8,128)S(1)}, f32[88,128]{1,0:T(8,128)S(1)}, u32[]{:S(2)}, u32[]{:S(2)}) collective-permute-start(f32[88,128]{1,0:T(8,128)S(1)} %shard_map.69), channel_id=1, source_target_pairs={{0,8},{1,2},{2,1},{3,4},{4,3},{5,6},{6,5},{7,15},{8,0},{9,10},{10,... | collective-permute-start | bytes 135176 | tf_op jit(solution)/shard_map/ppermute | solution.py:40
  17.0 5.1 %collective-permute-start.4 = (f32[88,128]{1,0:T(8,128)S(1)}, f32[88,128]{1,0:T(8,128)S(1)}, u32[]{:S(2)}, u32[]{:S(2)}) collective-permute-start(f32[88,128]{1,0:T(8,128)S(1)} %shard_map.69), channel_id=1, source_target_pairs={{0,1},{1,0},{2,3},{3,2},{4,5},{5,4},{6,7},{7,6},{8,9},{9,8},{10,11... | collective-permute-start | bytes 135176 | tf_op jit(solution)/shard_map/ppermute | solution.py:40

commit v5 on v4

--- a/solution.py
+++ b/solution.py
@@ -53,11 +53,11 @@
 
 
 class Picked:
-    def __init__(self, flag, when_true, when_false, start=0):
-        self.flag, self.refs, self.start = flag, (when_true, when_false), start
+    def __init__(self, flag, when_true, when_false):
+        self.flag, self.refs = flag, (when_true, when_false)
 
     def rows(self, at, count):
-        where = pl.ds(self.start + at, count)
+        where = pl.ds(at, count)
         return jnp.where(self.flag, self.refs[0][where, :], self.refs[1][where, :])
 
 
@@ -278,20 +278,24 @@
     load = pltpu.make_async_copy(map_hbm, map_v, in_sem)
     load.start()
 
-    def clear(i, _):
+    for i in range(2 * RAD):
         field[i] = jnp.zeros((ey, DEPTH), jnp.float32)
-        return 0
-
-    lax.fori_loop(0, ex, clear, 0)
+    for i in range(2 * RAD, ex):
+        field[i, 0 : 2 * RAD, :] = jnp.zeros((2 * RAD, DEPTH), jnp.float32)
 
     def own(i, _):
         a, b = i // cols_n, i % cols_n
         y0 = pl.multiple_of(SUB * b, SUB)
+        y1 = pl.multiple_of(SUB * b + 2 * RAD, 2 * RAD)
         for p, row in enumerate(rendered(own_atom(terms_ref, i), 0, TILE, 0, 3)):
-            field[SUB * a + p, pl.ds(y0, TILE), :] += row
+            if p < 2 * RAD:
+                field[SUB * a + p, pl.ds(y0, TILE), :] += row
+            else:
+                field[SUB * a + p, pl.ds(y0, 2 * RAD), :] += row[: 2 * RAD]
+                field[SUB * a + p, pl.ds(y1, SUB), :] = row[2 * RAD :]
         return 0
 
-    lax.fori_loop(0, rows_n * cols_n, own, 0, unroll=4)
+    lax.fori_loop(0, rows_n * cols_n, own, 0, unroll=8)
     load.wait()
 
     def brick(i, _):
@@ -300,7 +304,7 @@
         out_v[i] = inside.astype(jnp.bfloat16)
         return 0
 
-    lax.fori_loop(0, nx, brick, 0, unroll=4)
+    lax.fori_loop(0, nx, brick, 0, unroll=8)
     rest = pl.ds(2 * RAD, nx - 2 * RAD)
     pairs = [(out_v, out_hbm)]
     for k in range(2):
@@ -314,29 +318,30 @@
             pieces[i, 16 * j : 16 * j + 16, :] = packed(field[2 * i, rows, :], field[2 * i + 1, rows, :])
         return 0
 
-    lax.fori_loop(RAD, ex // 2 - RAD, pack, 0, unroll=2)
+    lax.fori_loop(RAD, ex // 2 - RAD, pack, 0, unroll=4)
     def gradient(i, _):
         a, b = i // (cols_n - 2) + 1, i % (cols_n - 2) + 1
         tile_gradient(own_atom(terms_ref, a * cols_n + b), pieces, prof_x, grad_ref, a, b)
         return 0
 
-    lax.fori_loop(0, (rows_n - 2) * (cols_n - 2), gradient, 0, unroll=6)
+    lax.fori_loop(0, (rows_n - 2) * (cols_n - 2), gradient, 0, unroll=12)
     finish(stores)
 
 
-def corner_kernel(rows_n, cols_n, xlow_ref, xhigh_ref, out_ref):
-    ny = cols_n * SUB
-    at = 0
-    for y0, sub in ((0, 0), (ny - RAD, cols_n - 1)):
-        for message in (xlow_ref, xhigh_ref):
-            for i in range(RAD):
-                out_ref[at : at + RAD, :] = message[ny * i + y0 : ny * i + y0 + RAD, :]
-                at += RAD
+def corner_kernel(rows_n, cols_n, first_ref, second_ref, up_ref, down_ref):
+    nx = rows_n * SUB
+    even = is_even()
+    ylow, yhigh = Picked(even, second_ref, first_ref), Picked(even, first_ref, second_ref)
+    block = RAD * RAD
+    for out, x0, a in ((up_ref, nx - RAD, rows_n - 1), (down_ref, 0, 0)):
+        for ky, message in enumerate((ylow, yhigh)):
+            at = (block + FIELDS) * ky
+            out[at : at + block, :] = message.rows(RAD * x0, block)
             for k in range(FIELDS):
-                row = RAD * ny + k * cols_n + sub
-                out_ref[at : at + 1, :] = message[row : row + 1, :]
-                at += 1
-    out_ref[at:, :] = jnp.zeros((out_ref.shape[0] - at, CAP), jnp.float32)
+                row = at + block + k
+                out[row : row + 1, :] = message.rows(RAD * nx + k * rows_n + a, 1)
+        at = 2 * (block + FIELDS)
+        out[at:, :] = jnp.zeros((out.shape[0] - at, CAP), jnp.float32)
 
 
 def sides_kernel(
@@ -373,7 +378,7 @@
 
 def outer_kernel(
     rows_n, cols_n,
-    terms_ref, xlow_ref, xhigh_ref, first_ref, second_ref, cfirst_ref, csecond_ref,
+    terms_ref, xlow_ref, xhigh_ref, first_ref, second_ref, clow_ref, chigh_ref,
     xband_in, yband_in, pieces_in, grad_in, out_in,
     out_hbm, grad_ref, xband, yband, pieces,
     xout, yout, prof_x, sems,
@@ -384,22 +389,20 @@
     corner = RAD * RAD + FIELDS
     even, valid = is_even(), valid_sides()
     ylow, yhigh = Picked(even, second_ref, first_ref), Picked(even, first_ref, second_ref)
-    clow = Picked(even, csecond_ref, cfirst_ref, 2 * corner)
-    chigh = Picked(even, cfirst_ref, csecond_ref)
-    for ky, (message, j0, y0) in enumerate(((clow, 2, 0), (chigh, 0, ey - 8))):
+    sent = Plain(clow_ref), Plain(chigh_ref)
+    for ky, (j0, y0) in enumerate(((2, 0), (0, ey - 8))):
         for kx, p0 in enumerate((SUB, 0)):
             ok = valid[kx] * valid[2 + ky]
-            atom = sent_atom(message, corner * kx + RAD * RAD, 1, 0, ok)
+            atom = sent_atom(sent[kx], corner * ky + RAD * RAD, 1, 0, ok)
             for p, row in enumerate(rendered(atom, p0, 2 * RAD, j0, 1)):
                 xband[kx, p, y0 : y0 + 8, :] += row
     for kx, message in enumerate((xlow_ref, xhigh_ref)):
         for i in range(RAD):
             row = RAD * kx + i
             xband[kx, row, RAD : RAD + ny, :] -= message[ny * i : ny * (i + 1), :]
-            for ky, sent in enumerate((clow, chigh)):
+            for ky in range(2):
                 y0 = (ey - RAD) * ky
-                at = corner * kx + RAD * i
-                xband[kx, row, y0 : y0 + RAD, :] -= sent.rows(at, RAD)
+                xband[kx, row, y0 : y0 + RAD, :] -= sent[kx].rows(corner * ky + RAD * i, RAD)
             xband[kx, row] = valid[kx] * xband[kx, row]
     for ky, message in enumerate((ylow, yhigh)):
         y0 = (ey - RAD) * ky
@@ -452,18 +455,15 @@
                 yband[ky, 2 * i, rows, :], yband[ky, 2 * i + 1, rows, :]
             )
 
-    def x_edges(i, _):
-        a, b = (i // cols_n) * (rows_n - 1), i % cols_n
+    def edges(i, _):
+        k = jnp.maximum(i - 2 * cols_n, 0)
+        side = i < 2 * cols_n
+        a = jnp.where(side, (i // cols_n) * (rows_n - 1), k // 2 + 1)
+        b = jnp.where(side, i % cols_n, (k % 2) * (cols_n - 1))
         tile_gradient(own_atom(terms_ref, a * cols_n + b), pieces, prof_x, grad_ref, a, b)
         return 0
 
-    def y_edges(i, _):
-        a, b = i // 2 + 1, (i % 2) * (cols_n - 1)
-        tile_gradient(own_atom(terms_ref, a * cols_n + b), pieces, prof_x, grad_ref, a, b)
-        return 0
-
-    lax.fori_loop(0, 2 * cols_n, x_edges, 0, unroll=8)
-    lax.fori_loop(0, 2 * (rows_n - 2), y_edges, 0, unroll=4)
+    lax.fori_loop(0, 2 * cols_n + 2 * (rows_n - 2), edges, 0, unroll=10)
     for store in stores:
         store.wait()
 
@@ -551,16 +551,11 @@
     )(pin(found), density_map)
     kept_pieces, xband, yband = kept
 
-    corners = call(
-        corner_kernel,
-        sizes,
-        shape((4 * (RAD * RAD + FIELDS) + 4, CAP), f32),
-        [vmem, vmem],
-        vmem,
-        [],
-        10**5,
-    )(from_xlow, from_xhigh)
-    from_corners = swap(corners, False), swap(corners, True)
+    edge = shape((2 * (RAD * RAD + FIELDS) + 6, CAP), f32)
+    up, down = call(
+        corner_kernel, sizes, (edge, edge), [vmem, vmem], (vmem, vmem), [], 10**5
+    )(from_first, from_second)
+    from_corners = shift(up, "bx", 1), shift(down, "bx", -1)
 
     messages = (from_xlow, from_xhigh, from_first, from_second)
     xband, yband = call(

time: 29.7 us -> 27.2 us (0.916)
  the two profiles are of different devices: /device:TPU:0 before, /device:TPU:21 now
where the time goes in v5:
time: 27.2 us; the launch traced here: 27.1 us
  Pallas kernels  18.4 us (68%)
  starting transfers between devices  6.68 us (25%)
  waiting for transfers between devices  1.3 us (5%)
  between operations  0.69 us (3%)
    pallas_call x1, Pallas kernels, local(): call(inner_kernel, sizes, (shape((nx, ny, DEPTH), bf16), pieces, *bands,...  8.58 us
    pallas_call x1, Pallas kernels, local(): call(outer_kernel, sizes, (shape((nx, ny, DEPTH), bf16), shape((4, rows_n...  6.48 us
    ppermute x4, starting transfers between devices, shift(): return lax.ppermute(block, axis, route)  4.13 us
    ppermute x2, starting transfers between devices, swap(): return lax.ppermute(block, ('bx', 'by'), route)  2.54 us
    pallas_call x1, Pallas kernels, local(): call(sides_kernel, sizes, bands, [vmem] * 6, (vmem, vmem), [], 2 * 10 **...  1.94 us
    pallas_call x1, Pallas kernels, local(): call(message_kernel, sizes, (shape((xsize, CAP), f32),) * 2 + (shape((ysi...  1.39 us
    ppermute x4, waiting for transfers between devices, shift(): return lax.ppermute(block, axis, route)  1.29 us
  transfers between devices with their start and end apart: 6, of which 1 were waited for; matrix products, arithmetic and copies ran while one was open for 0% of the time, Pallas kernels for 39%

profile of v5, /device:TPU:21, one launch (start us, length us, event | category | flops | bytes accessed | tf_op | source)
XLA Modules:
  0.0 27.1 jit_solution(9790296874468856592)
XLA Ops:
  0.6 1.4 %shard_map.68 = (f32[552,128]{1,0:T(8,128)S(1)}, f32[552,128]{1,0:T(8,128)S(1)}, f32[280,128]{1,0:T(8,128)S(1)}, f32[280,128]{1,0:T(8,128)S(1)}, f32[32,8,128]{2,1,0:T(8,128)S(1)}) custom-call(s32[4,8]{1,0:T(4,128)} %counts_hbm.1, f32[3,4,8,128]{3,2,1,0:T(8,128)} %pos_hbm.1, f32[4,8,128]{2,1,0:T(8,128)} %bfac_hbm.1, f32[4,8,128]{2,1,0:T(8,128)} %amp_hbm.1, ...), custom_call_target="tpu_custom_call" | custom-call | flops 1000000 | bytes 1048576 | tf_op jit(solution)/shard_map/pallas_call | solution.py:507
  2.0 0.3 %collective-permute-start.2 = (f32[280,128]{1,0:T(8,128)S(1)}, f32[280,128]{1,0:T(8,128)S(1)}, u32[]{:S(2)}, u32[]{:S(2)}) collective-permute-start(f32[280,128]{1,0:T(8,128)S(1)} %get-tuple-element.21), channel_id=1, source_target_pairs={{0,1},{1,0},{2,3},{3,2},{4,5},{5,4},{6,7},{7,6},{8,9},{9,8},{10,11... | collective-permute-start | bytes 430088 | tf_op jit(solution)/shard_map/ppermute | solution.py:40
  2.3 2.3 %collective-permute-start.3 = (f32[280,128]{1,0:T(8,128)S(1)}, f32[280,128]{1,0:T(8,128)S(1)}, u32[]{:S(2)}, u32[]{:S(2)}) collective-permute-start(f32[280,128]{1,0:T(8,128)S(1)} %get-tuple-element.22), channel_id=1, source_target_pairs={{0,8},{1,2},{2,1},{3,4},{4,3},{5,6},{6,5},{7,15},{8,0},{9,10},{10,... | collective-permute-start | bytes 430088 | tf_op jit(solution)/shard_map/ppermute | solution.py:40
  4.6 2.3 %collective-permute-start = (f32[552,128]{1,0:T(8,128)S(1)}, f32[552,128]{1,0:T(8,128)S(1)}, u32[]{:S(2)}, u32[]{:S(2)}) collective-permute-start(f32[552,128]{1,0:T(8,128)S(1)} %get-tuple-element.19), channel_id=1, source_target_pairs={{0,8},{8,16},{16,24},{24,0},{1,9},{9,17},{17,25},{25,1},{2,10},{10... | collective-permute-start | bytes 847880 | tf_op jit(solution)/shard_map/ppermute | solution.py:28
  6.9 0.0 collective-permute-start.1
  6.9 8.6 %shard_map.70 = (bf16[64,128,128]{2,1,0:T(8,128)(2,1)}, bf16[36,272,256]{2,1,0:T(8,128)(2,1)S(1)}, f32[2,8,136,128]{3,2,1,0:T(8,128)S(1)}, f32[2,56,24,128]{3,2,1,0:T(8,128)S(1)}, f32[4,4,8,128]{3,2,1,0:T(8,128)S(1)}) custom-call(f32[32,8,128]{2,1,0:T(8,128)S(1)} %get-tuple-element.18.terms_ref, bf16[64,128,128]{2,1,0:T(8,128)(2,1)} %map_hbm.3), custom_call_target="tpu_custom_call" | custom-call | flops 10000000000 | bytes 1048576 | tf_op jit(solution)/shard_map/pallas_call | solution.py:531
  15.5 0.0 collective-permute-done.2.first_ref
  15.5 0.0 collective-permute-done.3.second_ref
  15.5 1.8 %collective-permute-start.4 = (f32[48,128]{1,0:T(8,128)S(1)}, f32[48,128]{1,0:T(8,128)S(1)}, u32[]{:S(2)}, u32[]{:S(2)}) collective-permute-start(f32[48,128]{1,0:T(8,128)S(1)} %get-tuple-element.23), channel_id=1, source_target_pairs={{0,8},{8,16},{16,24},{24,0},{1,9},{9,17},{17,25},{25,1},{2,10},{10... | collective-permute-start | bytes 73736 | tf_op jit(solution)/shard_map/ppermute | solution.py:28
  17.3 0.0 collective-permute-start.5
  17.3 0.0 collective-permute-done.xlow_ref
  17.3 0.0 collective-permute-done.1.xhigh_ref
  17.4 1.9 %shard_map.71 = (f32[2,8,136,128]{3,2,1,0:T(8,128)S(1)}, f32[2,56,24,128]{3,2,1,0:T(8,128)S(1)}) custom-call(f32[552,128]{1,0:T(8,128)S(1)} %collective-permute-done.xlow_ref, f32[552,128]{1,0:T(8,128)S(1)} %collective-permute-done.1.xhigh_ref, f32[280,128]{1,0:T(8,128)S(1)} %collective-permute-done.2.first_ref, ...), custom_call_target="tpu_custom_call", output_to_operand_aliasing={{0}: (4, {}), {1}: (5, {})} | custom-call | flops 2000000000 | bytes 1048576 | tf_op jit(solution)/shard_map/pallas_call | solution.py:561
  19.3 0.0 collective-permute-done.4.clow_ref
  19.3 1.3 %collective-permute-done.5.chigh_ref = f32[48,128]{1,0:T(8,128)S(1)} collective-permute-done((f32[48,128]{1,0:T(8,128)S(1)}, f32[48,128]{1,0:T(8,128)S(1)}, u32[]{:S(2)}, u32[]{:S(2)}) %collective-permute-start.5) | collective-permute-done | bytes 24608 | tf_op jit(solution)/shard_map/ppermute | solution.py:28
  20.6 6.5 %shard_map.72 = (bf16[64,128,128]{2,1,0:T(8,128)(2,1)}, f32[4,4,8,128]{3,2,1,0:T(8,128)}, f32[2,8,136,128]{3,2,1,0:T(8,128)S(1)}, f32[2,56,24,128]{3,2,1,0:T(8,128)S(1)}, bf16[36,272,256]{2,1,0:T(8,128)(2,1)S(1)}) custom-call(f32[32,8,128]{2,1,0:T(8,128)S(1)} %get-tuple-element.18.terms_ref,, ...), custom_call_target="tpu_custom_call", output_to_operand_aliasing={{0}: (11, {}), {2}: (7, {}), {3}: (8, {}), {4}: (9, {})} | custom-call | flops 10000000000 | bytes 1048576 | tf_op jit(solution)/shard_map/pallas_call | solution.py:572
  (1 shorter events, 0.0 us)
Async XLA Ops:
  2.0 13.5 %collective-permute-start.2 = (f32[280,128]{1,0:T(8,128)S(1)}, f32[280,128]{1,0:T(8,128)S(1)}, u32[]{:S(2)}, u32[]{:S(2)}) collective-permute-start(f32[280,128]{1,0:T(8,128)S(1)} %get-tuple-element.21), channel_id=1, source_target_pairs={{0,1},{1,0},{2,3},{3,2},{4,5},{5,4},{6,7},{7,6},{8,9},{9,8},{10,11... | collective-permute-start | bytes 430088 | tf_op jit(solution)/shard_map/ppermute | solution.py:40
  2.3 13.2 %collective-permute-start.3 = (f32[280,128]{1,0:T(8,128)S(1)}, f32[280,128]{1,0:T(8,128)S(1)}, u32[]{:S(2)}, u32[]{:S(2)}) collective-permute-start(f32[280,128]{1,0:T(8,128)S(1)} %get-tuple-element.22), channel_id=1, source_target_pairs={{0,8},{1,2},{2,1},{3,4},{4,3},{5,6},{6,5},{7,15},{8,0},{9,10},{10,... | collective-permute-start | bytes 430088 | tf_op jit(solution)/shard_map/ppermute | solution.py:40
  4.6 12.8 %collective-permute-start = (f32[552,128]{1,0:T(8,128)S(1)}, f32[552,128]{1,0:T(8,128)S(1)}, u32[]{:S(2)}, u32[]{:S(2)}) collective-permute-start(f32[552,128]{1,0:T(8,128)S(1)} %get-tuple-element.19), channel_id=1, source_target_pairs={{0,8},{8,16},{16,24},{24,0},{1,9},{9,17},{17,25},{25,1},{2,10},{10... | collective-permute-start | bytes 847880 | tf_op jit(solution)/shard_map/ppermute | solution.py:28
  6.9 10.4 %collective-permute-start.1 = (f32[552,128]{1,0:T(8,128)S(1)}, f32[552,128]{1,0:T(8,128)S(1)}, u32[]{:S(2)}, u32[]{:S(2)}) collective-permute-start(f32[552,128]{1,0:T(8,128)S(1)} %get-tuple-element.20), channel_id=1, source_target_pairs={{0,24},{8,0},{16,8},{24,16},{1,25},{9,1},{17,9},{25,17},{2,26},{10... | collective-permute-start | bytes 847880 | tf_op jit(solution)/shard_map/ppermute | solution.py:28
  15.5 3.8 %collective-permute-start.4 = (f32[48,128]{1,0:T(8,128)S(1)}, f32[48,128]{1,0:T(8,128)S(1)}, u32[]{:S(2)}, u32[]{:S(2)}) collective-permute-start(f32[48,128]{1,0:T(8,128)S(1)} %get-tuple-element.23), channel_id=1, source_target_pairs={{0,8},{8,16},{16,24},{24,0},{1,9},{9,17},{17,25},{25,1},{2,10},{10... | collective-permute-start | bytes 73736 | tf_op jit(solution)/shard_map/ppermute | solution.py:28
  17.3 3.3 %collective-permute-start.5 = (f32[48,128]{1,0:T(8,128)S(1)}, f32[48,128]{1,0:T(8,128)S(1)}, u32[]{:S(2)}, u32[]{:S(2)}) collective-permute-start(f32[48,128]{1,0:T(8,128)S(1)} %get-tuple-element.24), channel_id=1, source_target_pairs={{0,24},{8,0},{16,8},{24,16},{1,25},{9,1},{17,9},{25,17},{2,26},{10... | collective-permute-start | bytes 73736 | tf_op jit(solution)/shard_map/ppermute | solution.py:28

commit v6 on v5

--- a/solution.py
+++ b/solution.py
@@ -19,6 +19,7 @@
 EIGHT_PI_SQ = 8.0 * math.pi**2
 BLUR_VAR = 0.5
 REACH_SQ = float(RAD * RAD)
+LOG2_E = math.log2(math.e)
 VMEM_LIMIT = 18 << 20
 
 
@@ -75,24 +76,27 @@
     return high, low
 
 
-def base_profile(coordinate, sharpness, span, offset):
-    grid = (lax.broadcasted_iota(jnp.int32, (span, CAP), 0) + offset).astype(jnp.float32)
+def grid_of(span):
+    return lax.broadcasted_iota(jnp.int32, (span, CAP), 0).astype(jnp.float32)
+
+
+def base_profile(coordinate, sharpness, grid):
     distance = grid - coordinate
     square = distance * distance
     falloff = jnp.maximum(1.0 - square * (1.0 / REACH_SQ), 0.0)
-    damped = jnp.exp(-sharpness * square) * falloff
+    damped = jnp.exp2(square * (sharpness * (-LOG2_E))) * falloff
     return distance, square, falloff, damped
 
 
-def value_only(coordinate, sharpness, span, offset):
-    _, _, falloff, damped = base_profile(coordinate, sharpness, span, offset)
+def value_only(coordinate, sharpness, grid):
+    _, _, falloff, damped = base_profile(coordinate, sharpness, grid)
     return damped * falloff
 
 
-def all_kinds(coordinate, sharpness, span, offset):
-    distance, square, falloff, damped = base_profile(coordinate, sharpness, span, offset)
+def all_kinds(coordinate, sharpness, grid):
+    distance, square, falloff, damped = base_profile(coordinate, sharpness, grid)
     value = damped * falloff
-    slope = 2.0 * distance * (sharpness * value + (2.0 / REACH_SQ) * damped)
+    slope = distance * (2.0 * sharpness * value + (4.0 / REACH_SQ) * damped)
     width = -square * value
     return value, slope, width
 
@@ -128,25 +132,34 @@
     return terms(*row[:4]) + (row[4] * valid,)
 
 
-def rendered(atom, p0, p_n, j0, j_n):
+def rendered(atom, z_parts, p0, p_n, j0, j_n):
     cx, cy, cz, sharp, weight = atom
-    vx = value_only(cx, sharp, p_n, p0 - RAD) * weight
-    vy = value_only(cy, sharp, 8 * j_n, 8 * j0 - RAD)
-    z_hi, z_lo = split(value_only(cz, sharp, DEPTH, 0))
+    grid = grid_of(TILE) - float(RAD)
+    vx = value_only(cx, sharp, grid[p0 : p0 + p_n]) * weight
+    vy = value_only(cy, sharp, grid[8 * j0 : 8 * j0 + 8 * j_n])
+    z_hi, z_lo = z_parts
     weights = jnp.concatenate(
         [jnp.concatenate([z_hi, z_hi], 1), jnp.concatenate([z_lo, z_lo], 1)], 0
     )
-    rows = []
-    for p in range(p_n):
-        for j in range(j_n):
-            rows.append(vx[p : p + 1] * vy[8 * j : 8 * j + 8])
-    plane_hi, plane_lo = split(jnp.concatenate(rows, 0))
-    plane = jnp.concatenate([plane_hi, plane_lo], 1)
-    both = lax.dot_general(
-        plane, weights, (((1,), (1,)), ((), ())), preferred_element_type=jnp.float32
-    )
-    total = both[:, :DEPTH] + both[:, DEPTH:]
-    return [total[8 * j_n * p : 8 * j_n * (p + 1)] for p in range(p_n)]
+    out = []
+    step = TILE // 2 if p_n == TILE else p_n
+    for start in range(0, p_n, step):
+        rows = []
+        for p in range(start, start + step):
+            for j in range(j_n):
+                rows.append(vx[p : p + 1] * vy[8 * j : 8 * j + 8])
+        plane_hi, plane_lo = split(jnp.concatenate(rows, 0))
+        plane = jnp.concatenate([plane_hi, plane_lo], 1)
+        both = lax.dot_general(
+            plane, weights, (((1,), (1,)), ((), ())), preferred_element_type=jnp.float32
+        )
+        total = both[:, :DEPTH] + both[:, DEPTH:]
+        out += [total[8 * j_n * p : 8 * j_n * (p + 1)] for p in range(step)]
+    return out
+
+
+def z_value(atom, grid):
+    return split(value_only(atom[2], atom[3], grid))
 
 
 def packed(first, second):
@@ -154,12 +167,13 @@
     return jnp.concatenate([hi, lo], 1)
 
 
-def tile_gradient(atom, pieces, prof_x, grad_ref, a, b):
+def tile_gradient(atom, z_grid, pieces, prof_x, grad_ref, a, b):
     cx, cy, cz, sharp, weight = atom
-    for k, kind in enumerate(all_kinds(cx, sharp, TILE, -RAD)):
+    grid = grid_of(TILE) - float(RAD)
+    for k, kind in enumerate(all_kinds(cx, sharp, grid)):
         prof_x[k] = kind
-    vy, sy, wy = all_kinds(cy, sharp, TILE, -RAD)
-    vz, sz, wz = all_kinds(cz, sharp, DEPTH, 0)
+    vy, sy, wy = all_kinds(cy, sharp, grid)
+    vz, sz, wz = all_kinds(cz, sharp, z_grid)
     vz_hi, vz_lo = split(vz)
     sz_hi, sz_lo = split(sz)
     wz_hi = wz.astype(jnp.bfloat16)
@@ -214,9 +228,9 @@
     copies = []
     for k, at in enumerate((0, nx - RAD)):
         copies.append(pltpu.make_async_copy(map_hbm.at[pl.ds(at, RAD)], xrim.at[k], sems.at[k]))
-    for k, at in enumerate((0, ny - SUB)):
+    for k, at in enumerate((0, ny - 2 * RAD)):
         copies.append(
-            pltpu.make_async_copy(map_hbm.at[:, pl.ds(at, SUB)], yrim.at[k], sems.at[2 + k])
+            pltpu.make_async_copy(map_hbm.at[:, pl.ds(at, 2 * RAD)], yrim.at[k], sems.at[2 + k])
         )
     for copy in copies:
         copy.start()
@@ -263,7 +277,7 @@
         put(
             slice(RAD * i, RAD * (i + 1)),
             yrim[0, i].astype(jnp.float32)[:RAD],
-            yrim[1, i].astype(jnp.float32)[SUB - RAD :],
+            yrim[1, i].astype(jnp.float32)[RAD:],
         )
 
 
@@ -283,11 +297,14 @@
     for i in range(2 * RAD, ex):
         field[i, 0 : 2 * RAD, :] = jnp.zeros((2 * RAD, DEPTH), jnp.float32)
 
+    grid = grid_of(DEPTH)
+
     def own(i, _):
         a, b = i // cols_n, i % cols_n
         y0 = pl.multiple_of(SUB * b, SUB)
         y1 = pl.multiple_of(SUB * b + 2 * RAD, 2 * RAD)
-        for p, row in enumerate(rendered(own_atom(terms_ref, i), 0, TILE, 0, 3)):
+        atom = own_atom(terms_ref, i)
+        for p, row in enumerate(rendered(atom, z_value(atom, grid), 0, TILE, 0, 3)):
             if p < 2 * RAD:
                 field[SUB * a + p, pl.ds(y0, TILE), :] += row
             else:
@@ -295,7 +312,7 @@
                 field[SUB * a + p, pl.ds(y1, SUB), :] = row[2 * RAD :]
         return 0
 
-    lax.fori_loop(0, rows_n * cols_n, own, 0, unroll=8)
+    lax.fori_loop(0, rows_n * cols_n, own, 0, unroll=16)
     load.wait()
 
     def brick(i, _):
@@ -321,7 +338,7 @@
     lax.fori_loop(RAD, ex // 2 - RAD, pack, 0, unroll=4)
     def gradient(i, _):
         a, b = i // (cols_n - 2) + 1, i % (cols_n - 2) + 1
-        tile_gradient(own_atom(terms_ref, a * cols_n + b), pieces, prof_x, grad_ref, a, b)
+        tile_gradient(own_atom(terms_ref, a * cols_n + b), grid, pieces, prof_x, grad_ref, a, b)
         return 0
 
     lax.fori_loop(0, (rows_n - 2) * (cols_n - 2), gradient, 0, unroll=12)
@@ -353,12 +370,13 @@
     ex, ey = nx + 2 * RAD, ny + 2 * RAD
     even, valid = is_even(), valid_sides()
     ylow, yhigh = Picked(even, second_ref, first_ref), Picked(even, first_ref, second_ref)
+    grid = grid_of(DEPTH)
 
     def x_side(b, _):
         y0 = pl.multiple_of(SUB * b, SUB)
         for k, (message, p0) in enumerate(((Plain(xlow_ref), SUB), (Plain(xhigh_ref), 0))):
             atom = sent_atom(message, RAD * ny, cols_n, b, valid[k])
-            for p, row in enumerate(rendered(atom, p0, 2 * RAD, 0, 3)):
+            for p, row in enumerate(rendered(atom, z_value(atom, grid), p0, 2 * RAD, 0, 3)):
                 xband[k, p, pl.ds(y0, TILE), :] += row
         return 0
 
@@ -366,7 +384,7 @@
     for a in range(rows_n):
         for k, (message, j0, y0) in enumerate(((ylow, 2, 0), (yhigh, 0, ey - 8))):
             atom = sent_atom(message, RAD * nx, rows_n, a, valid[2 + k])
-            for p, row in enumerate(rendered(atom, 0, TILE, j0, 1)):
+            for p, row in enumerate(rendered(atom, z_value(atom, grid), 0, TILE, j0, 1)):
                 x = SUB * a + p
                 if x < 2 * RAD:
                     xband[0, x, y0 : y0 + 8, :] += row
@@ -390,11 +408,12 @@
     even, valid = is_even(), valid_sides()
     ylow, yhigh = Picked(even, second_ref, first_ref), Picked(even, first_ref, second_ref)
     sent = Plain(clow_ref), Plain(chigh_ref)
+    grid = grid_of(DEPTH)
     for ky, (j0, y0) in enumerate(((2, 0), (0, ey - 8))):
         for kx, p0 in enumerate((SUB, 0)):
             ok = valid[kx] * valid[2 + ky]
             atom = sent_atom(sent[kx], corner * ky + RAD * RAD, 1, 0, ok)
-            for p, row in enumerate(rendered(atom, p0, 2 * RAD, j0, 1)):
+            for p, row in enumerate(rendered(atom, z_value(atom, grid), p0, 2 * RAD, j0, 1)):
                 xband[kx, p, y0 : y0 + 8, :] += row
     for kx, message in enumerate((xlow_ref, xhigh_ref)):
         for i in range(RAD):
@@ -460,7 +479,7 @@
         side = i < 2 * cols_n
         a = jnp.where(side, (i // cols_n) * (rows_n - 1), k // 2 + 1)
         b = jnp.where(side, i % cols_n, (k % 2) * (cols_n - 1))
-        tile_gradient(own_atom(terms_ref, a * cols_n + b), pieces, prof_x, grad_ref, a, b)
+        tile_gradient(own_atom(terms_ref, a * cols_n + b), grid, pieces, prof_x, grad_ref, a, b)
         return 0
 
     lax.fori_loop(0, 2 * cols_n + 2 * (rows_n - 2), edges, 0, unroll=10)
@@ -515,7 +534,7 @@
         own_scratch
         + [
             pltpu.VMEM((2, RAD, ny, DEPTH), bf16),
-            pltpu.VMEM((2, nx, SUB, DEPTH), bf16),
+            pltpu.VMEM((2, nx, 2 * RAD, DEPTH), bf16),
             pltpu.SemaphoreType.DMA((4,)),
         ],
         10**6,

time: 27.2 us -> 26.3 us (0.967)
  the two profiles are of different devices: /device:TPU:21 before, /device:TPU:5 now
where the time goes in v6:
time: 26.3 us; the launch traced here: 26.2 us
  Pallas kernels  17.6 us (67%)
  starting transfers between devices  6.67 us (25%)
  waiting for transfers between devices  1.19 us (5%)
  between operations  0.7 us (3%)
    pallas_call x1, Pallas kernels, local(): call(inner_kernel, sizes, (shape((nx, ny, DEPTH), bf16), pieces, *bands,...  7.75 us
    pallas_call x1, Pallas kernels, local(): call(outer_kernel, sizes, (shape((nx, ny, DEPTH), bf16), shape((4, rows_n...  6.47 us
    ppermute x4, starting transfers between devices, shift(): return lax.ppermute(block, axis, route)  4.13 us
    ppermute x2, starting transfers between devices, swap(): return lax.ppermute(block, ('bx', 'by'), route)  2.54 us
    pallas_call x1, Pallas kernels, local(): call(sides_kernel, sizes, bands, [vmem] * 6, (vmem, vmem), [], 2 * 10 **...  2.05 us
    pallas_call x1, Pallas kernels, local(): call(message_kernel, sizes, (shape((xsize, CAP), f32),) * 2 + (shape((ysi...  1.32 us
    ppermute x4, waiting for transfers between devices, shift(): return lax.ppermute(block, axis, route)  1.18 us
  transfers between devices with their start and end apart: 6, of which 1 were waited for; matrix products, arithmetic and copies ran while one was open for 0% of the time, Pallas kernels for 37%

profile of v6, /device:TPU:5, one launch (start us, length us, event | category | flops | bytes accessed | tf_op | source)
XLA Modules:
  0.0 26.2 jit_solution(14354414499560803784)
XLA Ops:
  0.6 1.3 %shard_map.68 = (f32[552,128]{1,0:T(8,128)S(1)}, f32[552,128]{1,0:T(8,128)S(1)}, f32[280,128]{1,0:T(8,128)S(1)}, f32[280,128]{1,0:T(8,128)S(1)}, f32[32,8,128]{2,1,0:T(8,128)S(1)}) custom-call(s32[4,8]{1,0:T(4,128)} %counts_hbm.1, f32[3,4,8,128]{3,2,1,0:T(8,128)} %pos_hbm.1, f32[4,8,128]{2,1,0:T(8,128)} %bfac_hbm.1, f32[4,8,128]{2,1,0:T(8,128)} %amp_hbm.1, ...), custom_call_target="tpu_custom_call" | custom-call | flops 1000000 | bytes 1048576 | tf_op jit(solution)/shard_map/pallas_call | solution.py:526
  2.0 0.1 collective-permute-start.2
  2.0 2.5 %collective-permute-start.3 = (f32[280,128]{1,0:T(8,128)S(1)}, f32[280,128]{1,0:T(8,128)S(1)}, u32[]{:S(2)}, u32[]{:S(2)}) collective-permute-start(f32[280,128]{1,0:T(8,128)S(1)} %get-tuple-element.22), channel_id=1, source_target_pairs={{0,8},{1,2},{2,1},{3,4},{4,3},{5,6},{6,5},{7,15},{8,0},{9,10},{10,... | collective-permute-start | bytes 430088 | tf_op jit(solution)/shard_map/ppermute | solution.py:41
  4.5 2.3 %collective-permute-start = (f32[552,128]{1,0:T(8,128)S(1)}, f32[552,128]{1,0:T(8,128)S(1)}, u32[]{:S(2)}, u32[]{:S(2)}) collective-permute-start(f32[552,128]{1,0:T(8,128)S(1)} %get-tuple-element.19), channel_id=1, source_target_pairs={{0,8},{8,16},{16,24},{24,0},{1,9},{9,17},{17,25},{25,1},{2,10},{10... | collective-permute-start | bytes 847880 | tf_op jit(solution)/shard_map/ppermute | solution.py:29
  6.8 0.0 collective-permute-start.1
  6.8 7.7 %shard_map.70 = (bf16[64,128,128]{2,1,0:T(8,128)(2,1)}, bf16[36,272,256]{2,1,0:T(8,128)(2,1)S(1)}, f32[2,8,136,128]{3,2,1,0:T(8,128)S(1)}, f32[2,56,24,128]{3,2,1,0:T(8,128)S(1)}, f32[4,4,8,128]{3,2,1,0:T(8,128)S(1)}) custom-call(f32[32,8,128]{2,1,0:T(8,128)S(1)} %get-tuple-element.18.terms_ref, bf16[64,128,128]{2,1,0:T(8,128)(2,1)} %map_hbm.3), custom_call_target="tpu_custom_call" | custom-call | flops 10000000000 | bytes 1048576 | tf_op jit(solution)/shard_map/pallas_call | solution.py:550
  14.6 0.0 collective-permute-done.2.first_ref
  14.6 0.0 collective-permute-done.3.second_ref
  14.6 1.8 %collective-permute-start.4 = (f32[48,128]{1,0:T(8,128)S(1)}, f32[48,128]{1,0:T(8,128)S(1)}, u32[]{:S(2)}, u32[]{:S(2)}) collective-permute-start(f32[48,128]{1,0:T(8,128)S(1)} %get-tuple-element.23), channel_id=1, source_target_pairs={{0,8},{8,16},{16,24},{24,0},{1,9},{9,17},{17,25},{25,1},{2,10},{10... | collective-permute-start | bytes 73736 | tf_op jit(solution)/shard_map/ppermute | solution.py:29
  16.4 0.0 collective-permute-start.5
  16.4 0.0 collective-permute-done.xlow_ref
  16.4 0.0 collective-permute-done.1.xhigh_ref
  16.4 2.0 %shard_map.71 = (f32[2,8,136,128]{3,2,1,0:T(8,128)S(1)}, f32[2,56,24,128]{3,2,1,0:T(8,128)S(1)}) custom-call(f32[552,128]{1,0:T(8,128)S(1)} %collective-permute-done.xlow_ref, f32[552,128]{1,0:T(8,128)S(1)} %collective-permute-done.1.xhigh_ref, f32[280,128]{1,0:T(8,128)S(1)} %collective-permute-done.2.first_ref, ...), custom_call_target="tpu_custom_call", output_to_operand_aliasing={{0}: (4, {}), {1}: (5, {})} | custom-call | flops 2000000000 | bytes 1048576 | tf_op jit(solution)/shard_map/pallas_call | solution.py:580
  18.5 0.0 collective-permute-done.4.clow_ref
  18.5 1.2 %collective-permute-done.5.chigh_ref = f32[48,128]{1,0:T(8,128)S(1)} collective-permute-done((f32[48,128]{1,0:T(8,128)S(1)}, f32[48,128]{1,0:T(8,128)S(1)}, u32[]{:S(2)}, u32[]{:S(2)}) %collective-permute-start.5) | collective-permute-done | bytes 24608 | tf_op jit(solution)/shard_map/ppermute | solution.py:29
  19.7 6.5 %shard_map.72 = (bf16[64,128,128]{2,1,0:T(8,128)(2,1)}, f32[4,4,8,128]{3,2,1,0:T(8,128)}, f32[2,8,136,128]{3,2,1,0:T(8,128)S(1)}, f32[2,56,24,128]{3,2,1,0:T(8,128)S(1)}, bf16[36,272,256]{2,1,0:T(8,128)(2,1)S(1)}) custom-call(f32[32,8,128]{2,1,0:T(8,128)S(1)} %get-tuple-element.18.terms_ref,, ...), custom_call_target="tpu_custom_call", output_to_operand_aliasing={{0}: (11, {}), {2}: (7, {}), {3}: (8, {}), {4}: (9, {})} | custom-call | flops 10000000000 | bytes 1048576 | tf_op jit(solution)/shard_map/pallas_call | solution.py:591
  (1 shorter events, 0.0 us)
Async XLA Ops:
  2.0 12.6 %collective-permute-start.2 = (f32[280,128]{1,0:T(8,128)S(1)}, f32[280,128]{1,0:T(8,128)S(1)}, u32[]{:S(2)}, u32[]{:S(2)}) collective-permute-start(f32[280,128]{1,0:T(8,128)S(1)} %get-tuple-element.21), channel_id=1, source_target_pairs={{0,1},{1,0},{2,3},{3,2},{4,5},{5,4},{6,7},{7,6},{8,9},{9,8},{10,11... | collective-permute-start | bytes 430088 | tf_op jit(solution)/shard_map/ppermute | solution.py:41
  2.0 12.6 %collective-permute-start.3 = (f32[280,128]{1,0:T(8,128)S(1)}, f32[280,128]{1,0:T(8,128)S(1)}, u32[]{:S(2)}, u32[]{:S(2)}) collective-permute-start(f32[280,128]{1,0:T(8,128)S(1)} %get-tuple-element.22), channel_id=1, source_target_pairs={{0,8},{1,2},{2,1},{3,4},{4,3},{5,6},{6,5},{7,15},{8,0},{9,10},{10,... | collective-permute-start | bytes 430088 | tf_op jit(solution)/shard_map/ppermute | solution.py:41
  4.5 11.9 %collective-permute-start = (f32[552,128]{1,0:T(8,128)S(1)}, f32[552,128]{1,0:T(8,128)S(1)}, u32[]{:S(2)}, u32[]{:S(2)}) collective-permute-start(f32[552,128]{1,0:T(8,128)S(1)} %get-tuple-element.19), channel_id=1, source_target_pairs={{0,8},{8,16},{16,24},{24,0},{1,9},{9,17},{17,25},{25,1},{2,10},{10... | collective-permute-start | bytes 847880 | tf_op jit(solution)/shard_map/ppermute | solution.py:29
  6.8 9.6 %collective-permute-start.1 = (f32[552,128]{1,0:T(8,128)S(1)}, f32[552,128]{1,0:T(8,128)S(1)}, u32[]{:S(2)}, u32[]{:S(2)}) collective-permute-start(f32[552,128]{1,0:T(8,128)S(1)} %get-tuple-element.20), channel_id=1, source_target_pairs={{0,24},{8,0},{16,8},{24,16},{1,25},{9,1},{17,9},{25,17},{2,26},{10... | collective-permute-start | bytes 847880 | tf_op jit(solution)/shard_map/ppermute | solution.py:29
  14.6 3.9 %collective-permute-start.4 = (f32[48,128]{1,0:T(8,128)S(1)}, f32[48,128]{1,0:T(8,128)S(1)}, u32[]{:S(2)}, u32[]{:S(2)}) collective-permute-start(f32[48,128]{1,0:T(8,128)S(1)} %get-tuple-element.23), channel_id=1, source_target_pairs={{0,8},{8,16},{16,24},{24,0},{1,9},{9,17},{17,25},{25,1},{2,10},{10... | collective-permute-start | bytes 73736 | tf_op jit(solution)/shard_map/ppermute | solution.py:29
  16.4 3.3 %collective-permute-start.5 = (f32[48,128]{1,0:T(8,128)S(1)}, f32[48,128]{1,0:T(8,128)S(1)}, u32[]{:S(2)}, u32[]{:S(2)}) collective-permute-start(f32[48,128]{1,0:T(8,128)S(1)} %get-tuple-element.24), channel_id=1, source_target_pairs={{0,24},{8,0},{16,8},{24,16},{1,25},{9,1},{17,9},{25,17},{2,26},{10... | collective-permute-start | bytes 73736 | tf_op jit(solution)/shard_map/ppermute | solution.py:29

commit v7 on v6

--- a/solution.py
+++ b/solution.py
@@ -380,7 +380,7 @@
                 xband[k, p, pl.ds(y0, TILE), :] += row
         return 0
 
-    lax.fori_loop(0, cols_n, x_side, 0, unroll=4)
+    lax.fori_loop(0, cols_n, x_side, 0, unroll=8)
     for a in range(rows_n):
         for k, (message, j0, y0) in enumerate(((ylow, 2, 0), (yhigh, 0, ey - 8))):
             atom = sent_atom(message, RAD * nx, rows_n, a, valid[2 + k])

time: 26.3 us -> 26.3 us (level)
  waiting for transfers between devices: 1.19 us -> 1.51 us
  Pallas kernels: 17.6 us -> 17.3 us
    ppermute x4, waiting for transfers between devices: 1.18 us -> 1.5 us  [shift(): return lax.ppermute(block, axis, route)]
    pallas_call x1, Pallas kernels: 2.05 us -> 1.73 us  [local(): call(sides_kernel, sizes, bands, [vmem] * 6, (vmem, vmem), [], 2 * 10 **...]
  transfers between devices with their start and end apart: 6 -> 6, of which waited for: 1 -> 1; matrix products, arithmetic and copies ran while one was open for 0% -> 0% of each run, Pallas kernels for 37% -> 36%
where the time goes in v7:
time: 26.3 us; the launch traced here: 26.2 us
  Pallas kernels  17.3 us (66%)
  starting transfers between devices  6.67 us (25%)
  waiting for transfers between devices  1.51 us (6%)
  between operations  0.7 us (3%)
    pallas_call x1, Pallas kernels, local(): call(inner_kernel, sizes, (shape((nx, ny, DEPTH), bf16), pieces, *bands,...  7.75 us
    pallas_call x1, Pallas kernels, local(): call(outer_kernel, sizes, (shape((nx, ny, DEPTH), bf16), shape((4, rows_n...  6.47 us
    ppermute x4, starting transfers between devices, shift(): return lax.ppermute(block, axis, route)  4.13 us
    ppermute x2, starting transfers between devices, swap(): return lax.ppermute(block, ('bx', 'by'), route)  2.54 us
    pallas_call x1, Pallas kernels, local(): call(sides_kernel, sizes, bands, [vmem] * 6, (vmem, vmem), [], 2 * 10 **...  1.73 us
    ppermute x4, waiting for transfers between devices, shift(): return lax.ppermute(block, axis, route)  1.5 us
    pallas_call x1, Pallas kernels, local(): call(message_kernel, sizes, (shape((xsize, CAP), f32),) * 2 + (shape((ysi...  1.32 us
  transfers between devices with their start and end apart: 6, of which 1 were waited for; matrix products, arithmetic and copies ran while one was open for 0% of the time, Pallas kernels for 36%

profile of v7, /device:TPU:5, one launch (start us, length us, event | category | flops | bytes accessed | tf_op | source)
XLA Modules:
  0.0 26.2 jit_solution(14311543204187649229)
XLA Ops:
  0.6 1.3 %shard_map.68 = (f32[552,128]{1,0:T(8,128)S(1)}, f32[552,128]{1,0:T(8,128)S(1)}, f32[280,128]{1,0:T(8,128)S(1)}, f32[280,128]{1,0:T(8,128)S(1)}, f32[32,8,128]{2,1,0:T(8,128)S(1)}) custom-call(s32[4,8]{1,0:T(4,128)} %counts_hbm.1, f32[3,4,8,128]{3,2,1,0:T(8,128)} %pos_hbm.1, f32[4,8,128]{2,1,0:T(8,128)} %bfac_hbm.1, f32[4,8,128]{2,1,0:T(8,128)} %amp_hbm.1, ...), custom_call_target="tpu_custom_call" | custom-call | flops 1000000 | bytes 1048576 | tf_op jit(solution)/shard_map/pallas_call | solution.py:526
  2.0 0.1 collective-permute-start.2
  2.0 2.5 %collective-permute-start.3 = (f32[280,128]{1,0:T(8,128)S(1)}, f32[280,128]{1,0:T(8,128)S(1)}, u32[]{:S(2)}, u32[]{:S(2)}) collective-permute-start(f32[280,128]{1,0:T(8,128)S(1)} %get-tuple-element.22), channel_id=1, source_target_pairs={{0,8},{1,2},{2,1},{3,4},{4,3},{5,6},{6,5},{7,15},{8,0},{9,10},{10,... | collective-permute-start | bytes 430088 | tf_op jit(solution)/shard_map/ppermute | solution.py:41
  4.5 2.3 %collective-permute-start = (f32[552,128]{1,0:T(8,128)S(1)}, f32[552,128]{1,0:T(8,128)S(1)}, u32[]{:S(2)}, u32[]{:S(2)}) collective-permute-start(f32[552,128]{1,0:T(8,128)S(1)} %get-tuple-element.19), channel_id=1, source_target_pairs={{0,8},{8,16},{16,24},{24,0},{1,9},{9,17},{17,25},{25,1},{2,10},{10... | collective-permute-start | bytes 847880 | tf_op jit(solution)/shard_map/ppermute | solution.py:29
  6.8 0.0 collective-permute-start.1
  6.8 7.7 %shard_map.70 = (bf16[64,128,128]{2,1,0:T(8,128)(2,1)}, bf16[36,272,256]{2,1,0:T(8,128)(2,1)S(1)}, f32[2,8,136,128]{3,2,1,0:T(8,128)S(1)}, f32[2,56,24,128]{3,2,1,0:T(8,128)S(1)}, f32[4,4,8,128]{3,2,1,0:T(8,128)S(1)}) custom-call(f32[32,8,128]{2,1,0:T(8,128)S(1)} %get-tuple-element.18.terms_ref, bf16[64,128,128]{2,1,0:T(8,128)(2,1)} %map_hbm.3), custom_call_target="tpu_custom_call" | custom-call | flops 10000000000 | bytes 1048576 | tf_op jit(solution)/shard_map/pallas_call | solution.py:550
  14.6 0.0 collective-permute-done.2.first_ref
  14.6 0.0 collective-permute-done.3.second_ref
  14.6 1.8 %collective-permute-start.4 = (f32[48,128]{1,0:T(8,128)S(1)}, f32[48,128]{1,0:T(8,128)S(1)}, u32[]{:S(2)}, u32[]{:S(2)}) collective-permute-start(f32[48,128]{1,0:T(8,128)S(1)} %get-tuple-element.23), channel_id=1, source_target_pairs={{0,8},{8,16},{16,24},{24,0},{1,9},{9,17},{17,25},{25,1},{2,10},{10... | collective-permute-start | bytes 73736 | tf_op jit(solution)/shard_map/ppermute | solution.py:29
  16.4 0.0 collective-permute-start.5
  16.4 0.0 collective-permute-done.xlow_ref
  16.4 0.0 collective-permute-done.1.xhigh_ref
  16.4 1.7 %shard_map.71 = (f32[2,8,136,128]{3,2,1,0:T(8,128)S(1)}, f32[2,56,24,128]{3,2,1,0:T(8,128)S(1)}) custom-call(f32[552,128]{1,0:T(8,128)S(1)} %collective-permute-done.xlow_ref, f32[552,128]{1,0:T(8,128)S(1)} %collective-permute-done.1.xhigh_ref, f32[280,128]{1,0:T(8,128)S(1)} %collective-permute-done.2.first_ref, ...), custom_call_target="tpu_custom_call", output_to_operand_aliasing={{0}: (4, {}), {1}: (5, {})} | custom-call | flops 2000000000 | bytes 1048576 | tf_op jit(solution)/shard_map/pallas_call | solution.py:580
  18.2 0.0 collective-permute-done.4.clow_ref
  18.2 1.5 %collective-permute-done.5.chigh_ref = f32[48,128]{1,0:T(8,128)S(1)} collective-permute-done((f32[48,128]{1,0:T(8,128)S(1)}, f32[48,128]{1,0:T(8,128)S(1)}, u32[]{:S(2)}, u32[]{:S(2)}) %collective-permute-start.5) | collective-permute-done | bytes 24608 | tf_op jit(solution)/shard_map/ppermute | solution.py:29
  19.7 6.5 %shard_map.72 = (bf16[64,128,128]{2,1,0:T(8,128)(2,1)}, f32[4,4,8,128]{3,2,1,0:T(8,128)}, f32[2,8,136,128]{3,2,1,0:T(8,128)S(1)}, f32[2,56,24,128]{3,2,1,0:T(8,128)S(1)}, bf16[36,272,256]{2,1,0:T(8,128)(2,1)S(1)}) custom-call(f32[32,8,128]{2,1,0:T(8,128)S(1)} %get-tuple-element.18.terms_ref,, ...), custom_call_target="tpu_custom_call", output_to_operand_aliasing={{0}: (11, {}), {2}: (7, {}), {3}: (8, {}), {4}: (9, {})} | custom-call | flops 10000000000 | bytes 1048576 | tf_op jit(solution)/shard_map/pallas_call | solution.py:591
  (1 shorter events, 0.0 us)
Async XLA Ops:
  2.0 12.6 %collective-permute-start.2 = (f32[280,128]{1,0:T(8,128)S(1)}, f32[280,128]{1,0:T(8,128)S(1)}, u32[]{:S(2)}, u32[]{:S(2)}) collective-permute-start(f32[280,128]{1,0:T(8,128)S(1)} %get-tuple-element.21), channel_id=1, source_target_pairs={{0,1},{1,0},{2,3},{3,2},{4,5},{5,4},{6,7},{7,6},{8,9},{9,8},{10,11... | collective-permute-start | bytes 430088 | tf_op jit(solution)/shard_map/ppermute | solution.py:41
  2.0 12.6 %collective-permute-start.3 = (f32[280,128]{1,0:T(8,128)S(1)}, f32[280,128]{1,0:T(8,128)S(1)}, u32[]{:S(2)}, u32[]{:S(2)}) collective-permute-start(f32[280,128]{1,0:T(8,128)S(1)} %get-tuple-element.22), channel_id=1, source_target_pairs={{0,8},{1,2},{2,1},{3,4},{4,3},{5,6},{6,5},{7,15},{8,0},{9,10},{10,... | collective-permute-start | bytes 430088 | tf_op jit(solution)/shard_map/ppermute | solution.py:41
  4.5 11.9 %collective-permute-start = (f32[552,128]{1,0:T(8,128)S(1)}, f32[552,128]{1,0:T(8,128)S(1)}, u32[]{:S(2)}, u32[]{:S(2)}) collective-permute-start(f32[552,128]{1,0:T(8,128)S(1)} %get-tuple-element.19), channel_id=1, source_target_pairs={{0,8},{8,16},{16,24},{24,0},{1,9},{9,17},{17,25},{25,1},{2,10},{10... | collective-permute-start | bytes 847880 | tf_op jit(solution)/shard_map/ppermute | solution.py:29
  6.8 9.6 %collective-permute-start.1 = (f32[552,128]{1,0:T(8,128)S(1)}, f32[552,128]{1,0:T(8,128)S(1)}, u32[]{:S(2)}, u32[]{:S(2)}) collective-permute-start(f32[552,128]{1,0:T(8,128)S(1)} %get-tuple-element.20), channel_id=1, source_target_pairs={{0,24},{8,0},{16,8},{24,16},{1,25},{9,1},{17,9},{25,17},{2,26},{10... | collective-permute-start | bytes 847880 | tf_op jit(solution)/shard_map/ppermute | solution.py:29
  14.6 3.5 %collective-permute-start.4 = (f32[48,128]{1,0:T(8,128)S(1)}, f32[48,128]{1,0:T(8,128)S(1)}, u32[]{:S(2)}, u32[]{:S(2)}) collective-permute-start(f32[48,128]{1,0:T(8,128)S(1)} %get-tuple-element.23), channel_id=1, source_target_pairs={{0,8},{8,16},{16,24},{24,0},{1,9},{9,17},{17,25},{25,1},{2,10},{10... | collective-permute-start | bytes 73736 | tf_op jit(solution)/shard_map/ppermute | solution.py:29
  16.4 3.3 %collective-permute-start.5 = (f32[48,128]{1,0:T(8,128)S(1)}, f32[48,128]{1,0:T(8,128)S(1)}, u32[]{:S(2)}, u32[]{:S(2)}) collective-permute-start(f32[48,128]{1,0:T(8,128)S(1)} %get-tuple-element.24), channel_id=1, source_target_pairs={{0,24},{8,0},{16,8},{24,16},{1,25},{9,1},{17,9},{25,17},{2,26},{10... | collective-permute-start | bytes 73736 | tf_op jit(solution)/shard_map/ppermute | solution.py:29
